TPU v7x, 128 devices: a whole 4x4x4 slice. The times are simulated.
128 devices in a mesh: row: 8 (over y, x_lo), col: 16 (over z, x_hi, core).
Axes of the slice: x: 4 (x_hi: 2, x_lo: 2; x = x_hi * 2 + x_lo), y: 4, z: 4, core: 2. Of those that a mesh axis runs over, the one named last changes fastest.
Arguments:
- node_feats: bfloat16 [131072, 1024], P(('row', 'col')), may hold values from -6 to 6
- hub_feats: bfloat16 [4096, 1024], P('col'), may hold values from -6 to 6
- self_weight: bfloat16 [1024, 1024], replicated, may hold values from -0.1875 to 0.1875
- neigh_weight: bfloat16 [1024, 1024], replicated, may hold values from -0.1875 to 0.1875
- out_bias: float32 [1024], replicated, may hold values from -3 to 3
- tile_weights: bfloat16 [16384, 128, 128], P(('row', 'col')), may hold values from 0 to 1
- tile_blocks: int32 [128, 128], P(('row', 'col')), may hold values from 0 to 7, as said below
- send_rows: int32 [64, 2048], P('row', 'col'), may hold values from 0 to 1023
- send_count: int32 [64, 16], P('row', 'col'), may hold values from 1 to 128, as said below
- send_weight: bfloat16 [64, 2048], P('row', 'col'), may hold values from 4 to 32
- arrive_node: int32 [64, 2048], P('row', 'col'), may hold values from 0 to 1023
Outputs:
- embeddings: bfloat16 [131072, 1024], P(('row', 'col'))
Inputs may be any that keep to these rules, and one draw needn't show every extreme that they name: `tile_blocks`: within one device's row of tiles, the 4 tiles of one column shard and half name distinct tile rows. `send_count`: in every column each owner sends the full 128 slots to one destination, and one destination of each column receives 128 slots from every owner.
All inputs are finite; a program needn't handle non-finite values.
Results may differ from a plain program's by a relative error of at most 0.0065.
Values may be sent and summed in bfloat16 or wider, within the bound.
No kernel may reach another device: no remote copies, remote signals or barrier semaphores. Data moves between devices by JAX's collectives and lax.ppermute only.
A program may use at most 128 MiB of HBM per device.

v0:
```python
import jax
import jax.numpy as jnp
from jax import lax
from jax.sharding import PartitionSpec as P


def from_behind(value, axis, steps):
    count = lax.axis_size(axis)
    pairs = [(source, (source + steps) % count) for source in range(count)]
    return lax.ppermute(value, axis, pairs)


def shards(
    node_feats,
    hub_feats,
    self_weight,
    neigh_weight,
    out_bias,
    tile_weights,
    tile_blocks,
    send_rows,
    send_count,
    send_weight,
    arrive_node,
):
    columns = lax.axis_size("col")
    own_col = lax.axis_index("col")
    node_count = node_feats.shape[0]
    feat_width = node_feats.shape[1]
    tile_size = tile_weights.shape[1]
    block_count = node_count // tile_size
    per_half = tile_weights.shape[0] // (columns * 2)
    tiles_six = tile_weights.reshape(columns, 2, per_half, tile_size, tile_size)
    blocks_three = tile_blocks.reshape(columns, 2, per_half)
    block_ids = jnp.arange(block_count, dtype=jnp.int32)
    zero_sums = jnp.zeros((block_count, tile_size, feat_width), jnp.float32)

    def add_source(running, hub_half, source, which_half):
        chosen = lax.dynamic_index_in_dim(tiles_six[:, which_half], source, 0, keepdims=False)
        targets = lax.dynamic_index_in_dim(blocks_three[:, which_half], source, 0, keepdims=False)
        select = (block_ids[:, None] == targets[None, :]).astype(jnp.bfloat16)
        placed = jnp.einsum(
            "nt,tij->nij", select, chosen, preferred_element_type=jnp.float32
        ).astype(jnp.bfloat16)
        return running + jnp.einsum(
            "nij,jd->nid", placed, hub_half, preferred_element_type=jnp.float32
        )

    started = add_source(zero_sums, hub_feats[:tile_size], own_col, 0)
    started = add_source(started, hub_feats[tile_size:], own_col, 1)

    def rotate_step(step_index, carried):
        running, hub_shard = carried
        hub_shard = from_behind(hub_shard, "col", 1)
        source = (own_col - step_index) % columns
        running = add_source(running, hub_shard[:tile_size], source, 0)
        running = add_source(running, hub_shard[tile_size:], source, 1)
        return (running, hub_shard)

    hub_sum = lax.fori_loop(1, columns, rotate_step, (started, hub_feats))[0]
    row_sums = jnp.sum(tile_weights, axis=-1, dtype=jnp.float32)
    tile_select = (tile_blocks[0][:, None] == block_ids[None, :]).astype(jnp.float32)
    hub_weight = jnp.einsum("tn,ti->ni", tile_select, row_sums)
    slots = send_rows.shape[1]
    picked = node_feats[send_rows]
    usable = jnp.arange(slots, dtype=jnp.int32)[None, :] < send_count
    slot_weight = send_weight.astype(jnp.float32)
    message = jnp.where(usable[:, :, None], slot_weight[:, :, None] * picked, 0.0).astype(
        jnp.bfloat16
    )
    kept_weight = jnp.where(usable, send_weight, jnp.zeros_like(send_weight))
    arrived, arrived_weight = (
        lax.all_to_all(message, "row", split_axis=0, concat_axis=0, tiled=True),
        lax.all_to_all(kept_weight, "row", split_axis=0, concat_axis=0, tiled=True),
    )
    arrive_at = arrive_node.reshape(-1)
    node_ids = jnp.arange(node_count, dtype=jnp.int32)
    arrive_select = (node_ids[:, None] == arrive_at[None, :]).astype(jnp.bfloat16)
    tail_sum = jnp.dot(
        arrive_select, arrived.reshape(-1, feat_width), preferred_element_type=jnp.float32
    )
    tail_weight = jnp.dot(
        arrive_select, arrived_weight.reshape(-1, 1), preferred_element_type=jnp.float32
    ).reshape(node_count)
    combined = hub_sum.reshape(node_count, feat_width) + tail_sum
    weight_sum = hub_weight.reshape(node_count) + tail_weight
    neighbour = (combined * lax.rsqrt(1.0 + weight_sum)[:, None]).astype(jnp.bfloat16)
    preact = jnp.dot(node_feats, self_weight, preferred_element_type=jnp.float32)
    preact = (
        preact + jnp.dot(neighbour, neigh_weight, preferred_element_type=jnp.float32) + out_bias
    )
    hidden = jnp.maximum(preact, 0.0)
    row_scale = lax.rsqrt(jnp.mean(hidden * hidden, axis=-1, keepdims=True) + 1e-06)
    return (hidden * row_scale).astype(jnp.bfloat16)


def solution(mesh):
    placed = (
        P(("row", "col"), None),
        P("col", None),
        P(),
        P(),
        P(),
        P(("row", "col"), None, None),
        P(("row", "col"), None),
        P("row", "col"),
        P("row", "col"),
        P("row", "col"),
        P("row", "col"),
    )
    return jax.shard_map(
        shards, mesh=mesh, in_specs=placed, out_specs=P(("row", "col"), None), check_vma=False
    )
```

profile of v0, /device:TPU:2, one launch (start us, length us, event | category | flops | bytes accessed | tf_op | source)
XLA Modules:
  0.0 333.4 jit_solution(13054842579885908102)
XLA Ops:
  2.6 5.9 %all-to-all-start.1 = ((bf16[8,1,128]{2,1,0:T(2,128)(2,1)}), bf16[8,1,128]{2,1,0:T(2,128)(2,1)S(1)}, u32[]{:S(2)}, u32[]{:S(2)}) async-start(bf16[8,1,128]{2,1,0:T(2,128)(2,1)} %copy.26), calls=%async_computation.1 | async-start | bytes 8192 | tf_op jit(solution)/shard_map/all_to_all | solution.py:74
  9.3 4.9 %fusion.56 = (bf16[16,1,4,128,128]{4,3,2,1,0:T(8,128)(2,1)}, bf16[16,1,4,128,128]{4,3,2,1,0:T(8,128)(2,1)}) fusion(bf16[16,2,4,128,128]{4,3,2,1,0:T(8,128)(2,1)} %bitcast.97), kind=kLoop, calls=%fused_computation.83 | loop fusion | bytes 8388608 | tf_op jit(solution)/shard_map/slice | solution.py:39
  15.4 5.4 %gather_fusion = bf16[1024,1024]{1,0:T(8,128)(2,1)} fusion(bf16[1024,1024]{1,0:T(8,128)(2,1)S(1)} %copy-done, s32[1024]{0:T(1024)S(1)} %fusion.44), kind=kCustom, calls=%fused_computation | custom fusion | bytes 4198400 | tf_op jit(solution)/shard_map/gather | solution.py:65
  20.8 5.9 %fusion.59 = f32[1024,1024]{0,1:T(8,128)} fusion(bf16[1024,1024]{1,0:T(8,128)(2,1)S(1)} %copy-done, bf16[1024,1024]{1,0:T(8,128)(2,1)} %param.15), kind=kOutput, calls=%fused_computation.86 | convolution fusion | flops 2147483648 | bytes 8388608 | tf_op jit(solution)/shard_map/dot_general | solution.py:88
  35.9 5.9 %copy.25 = bf16[16,2,4,128,128]{4,2,3,1,0:T(4,128)(2,1)} copy(bf16[16,2,4,128,128]{4,3,2,1,0:T(8,128)(2,1)S(1)} %bitcast.98) | data formatting | bytes 8388608
  41.8 5.8 %all-to-all-start = ((bf16[8,128,1024]{2,1,0:T(8,128)(2,1)}), bf16[8,128,1024]{2,1,0:T(8,128)(2,1)}, u32[]{:S(2)}, u32[]{:S(2)}) async-start(bf16[8,128,1024]{2,1,0:T(8,128)(2,1)} %fusion.21), calls=%async_computation | async-start | bytes 4194304 | tf_op jit(solution)/shard_map/all_to_all | solution.py:73
  48.7 270.3 %while.19 = (s32[]{:T(128)}, f32[8,128,1024]{2,1,0:T(8,128)}, bf16[256,1024]{1,0:T(8,128)(2,1)S(1)}, s32[16,2,4]{2,1,0:T(2,128)S(1)}, s32[]{:T(128)}, /*index=5*...) while((s32[]{:T(128)}, f32[8,128,1024]{2,1,0:T(8,128)}, ...), condition=%wide.region_1.2_spmd.clone.clone, body=%wide.region_0.1_spmd.clone.clone.sunk | while | flops 541327488 | bytes 63702468 | solution.py:60
  55.9 26.0 %collective-permute-done = bf16[256,1024]{1,0:T(8,128)(2,1)S(1)} collective-permute-done((bf16[256,1024]{1,0:T(8,128)(2,1)S(1)}, bf16[256,1024]{1,0:T(8,128)(2,1)S(1)}, u32[]{:S(2)}, u32[]{:S(2)}) %collective-permute-start) | collective-permute-done | bytes 524320 | tf_op jit(solution)/shard_map/while/body/eval_jaxpr/ppermute | solution.py:10
  93.5 5.0 %collective-permute-done = bf16[256,1024]{1,0:T(8,128)(2,1)S(1)} collective-permute-done((bf16[256,1024]{1,0:T(8,128)(2,1)S(1)}, bf16[256,1024]{1,0:T(8,128)(2,1)S(1)}, u32[]{:S(2)}, u32[]{:S(2)}) %collective-permute-start) | collective-permute-done | bytes 524320 | tf_op jit(solution)/shard_map/while/body/eval_jaxpr/ppermute | solution.py:10
  110.1 5.0 %collective-permute-done = bf16[256,1024]{1,0:T(8,128)(2,1)S(1)} collective-permute-done((bf16[256,1024]{1,0:T(8,128)(2,1)S(1)}, bf16[256,1024]{1,0:T(8,128)(2,1)S(1)}, u32[]{:S(2)}, u32[]{:S(2)}) %collective-permute-start) | collective-permute-done | bytes 524320 | tf_op jit(solution)/shard_map/while/body/eval_jaxpr/ppermute | solution.py:10
  126.7 5.0 %collective-permute-done = bf16[256,1024]{1,0:T(8,128)(2,1)S(1)} collective-permute-done((bf16[256,1024]{1,0:T(8,128)(2,1)S(1)}, bf16[256,1024]{1,0:T(8,128)(2,1)S(1)}, u32[]{:S(2)}, u32[]{:S(2)}) %collective-permute-start) | collective-permute-done | bytes 524320 | tf_op jit(solution)/shard_map/while/body/eval_jaxpr/ppermute | solution.py:10
  136.2 4.5 %fusion.82 = (bf16[16,1,4,128,128]{4,2,3,1,0:T(4,128)(2,1)}, bf16[16,1,4,128,128]{4,2,3,1,0:T(4,128)(2,1)}) fusion(bf16[16,2,4,128,128]{4,2,3,1,0:T(4,128)(2,1)} %get-tuple-element.328), kind=kLoop, calls=%fused_computation.81.clone.1 | loop fusion | bytes 8388608 | tf_op jit(solution)/shard_map/while/body/eval_jaxpr/slice | solution.py:39
  143.3 5.0 %collective-permute-done = bf16[256,1024]{1,0:T(8,128)(2,1)S(1)} collective-permute-done((bf16[256,1024]{1,0:T(8,128)(2,1)S(1)}, bf16[256,1024]{1,0:T(8,128)(2,1)S(1)}, u32[]{:S(2)}, u32[]{:S(2)}) %collective-permute-start) | collective-permute-done | bytes 524320 | tf_op jit(solution)/shard_map/while/body/eval_jaxpr/ppermute | solution.py:10
  159.9 5.0 %collective-permute-done = bf16[256,1024]{1,0:T(8,128)(2,1)S(1)} collective-permute-done((bf16[256,1024]{1,0:T(8,128)(2,1)S(1)}, bf16[256,1024]{1,0:T(8,128)(2,1)S(1)}, u32[]{:S(2)}, u32[]{:S(2)}) %collective-permute-start) | collective-permute-done | bytes 524320 | tf_op jit(solution)/shard_map/while/body/eval_jaxpr/ppermute | solution.py:10
  176.6 5.0 %collective-permute-done = bf16[256,1024]{1,0:T(8,128)(2,1)S(1)} collective-permute-done((bf16[256,1024]{1,0:T(8,128)(2,1)S(1)}, bf16[256,1024]{1,0:T(8,128)(2,1)S(1)}, u32[]{:S(2)}, u32[]{:S(2)}) %collective-permute-start) | collective-permute-done | bytes 524320 | tf_op jit(solution)/shard_map/while/body/eval_jaxpr/ppermute | solution.py:10
  193.2 5.0 %collective-permute-done = bf16[256,1024]{1,0:T(8,128)(2,1)S(1)} collective-permute-done((bf16[256,1024]{1,0:T(8,128)(2,1)S(1)}, bf16[256,1024]{1,0:T(8,128)(2,1)S(1)}, u32[]{:S(2)}, u32[]{:S(2)}) %collective-permute-start) | collective-permute-done | bytes 524320 | tf_op jit(solution)/shard_map/while/body/eval_jaxpr/ppermute | solution.py:10
  209.8 5.0 %collective-permute-done = bf16[256,1024]{1,0:T(8,128)(2,1)S(1)} collective-permute-done((bf16[256,1024]{1,0:T(8,128)(2,1)S(1)}, bf16[256,1024]{1,0:T(8,128)(2,1)S(1)}, u32[]{:S(2)}, u32[]{:S(2)}) %collective-permute-start) | collective-permute-done | bytes 524320 | tf_op jit(solution)/shard_map/while/body/eval_jaxpr/ppermute | solution.py:10
  226.4 5.0 %collective-permute-done = bf16[256,1024]{1,0:T(8,128)(2,1)S(1)} collective-permute-done((bf16[256,1024]{1,0:T(8,128)(2,1)S(1)}, bf16[256,1024]{1,0:T(8,128)(2,1)S(1)}, u32[]{:S(2)}, u32[]{:S(2)}) %collective-permute-start) | collective-permute-done | bytes 524320 | tf_op jit(solution)/shard_map/while/body/eval_jaxpr/ppermute | solution.py:10
  243.1 5.0 %collective-permute-done = bf16[256,1024]{1,0:T(8,128)(2,1)S(1)} collective-permute-done((bf16[256,1024]{1,0:T(8,128)(2,1)S(1)}, bf16[256,1024]{1,0:T(8,128)(2,1)S(1)}, u32[]{:S(2)}, u32[]{:S(2)}) %collective-permute-start) | collective-permute-done | bytes 524320 | tf_op jit(solution)/shard_map/while/body/eval_jaxpr/ppermute | solution.py:10
  259.7 5.0 %collective-permute-done = bf16[256,1024]{1,0:T(8,128)(2,1)S(1)} collective-permute-done((bf16[256,1024]{1,0:T(8,128)(2,1)S(1)}, bf16[256,1024]{1,0:T(8,128)(2,1)S(1)}, u32[]{:S(2)}, u32[]{:S(2)}) %collective-permute-start) | collective-permute-done | bytes 524320 | tf_op jit(solution)/shard_map/while/body/eval_jaxpr/ppermute | solution.py:10
  276.3 5.0 %collective-permute-done = bf16[256,1024]{1,0:T(8,128)(2,1)S(1)} collective-permute-done((bf16[256,1024]{1,0:T(8,128)(2,1)S(1)}, bf16[256,1024]{1,0:T(8,128)(2,1)S(1)}, u32[]{:S(2)}, u32[]{:S(2)}) %collective-permute-start) | collective-permute-done | bytes 524320 | tf_op jit(solution)/shard_map/while/body/eval_jaxpr/ppermute | solution.py:10
  292.9 5.0 %collective-permute-done = bf16[256,1024]{1,0:T(8,128)(2,1)S(1)} collective-permute-done((bf16[256,1024]{1,0:T(8,128)(2,1)S(1)}, bf16[256,1024]{1,0:T(8,128)(2,1)S(1)}, u32[]{:S(2)}, u32[]{:S(2)}) %collective-permute-start) | collective-permute-done | bytes 524320 | tf_op jit(solution)/shard_map/while/body/eval_jaxpr/ppermute | solution.py:10
  309.6 5.0 %collective-permute-done = bf16[256,1024]{1,0:T(8,128)(2,1)S(1)} collective-permute-done((bf16[256,1024]{1,0:T(8,128)(2,1)S(1)}, bf16[256,1024]{1,0:T(8,128)(2,1)S(1)}, u32[]{:S(2)}, u32[]{:S(2)}) %collective-permute-start) | collective-permute-done | bytes 524320 | tf_op jit(solution)/shard_map/while/body/eval_jaxpr/ppermute | solution.py:10
  319.0 5.3 %fusion.23 = bf16[1024,1024]{1,0:T(8,128)(2,1)S(1)} fusion(f32[8,128,1024]{2,1,0:T(8,128)} %get-tuple-element.185, f32[1024]{0:T(1024)S(1)} %fusion.30, bf16[1024,1024]{1,0:T(8,128)(2,1)} %bitcast.14, s32[1024]{0:T(1024)S(1)} %bitcast.103), kind=kOutput, calls=%fused_computation.33 | convolution fusion | flops 2151677952 | bytes 8396800 | tf_op jit(solution)/shard_map/dot_general | solution.py:79
  (237 shorter events, 192.1 us)
Async XLA Ops:
  0.0 15.4 %copy-start = (bf16[1024,1024]{1,0:T(8,128)(2,1)S(1)}, bf16[1024,1024]{1,0:T(8,128)(2,1)}, u32[]{:S(2)}) copy-start(bf16[1024,1024]{1,0:T(8,128)(2,1)} %param.13) | copy-start | bytes 6291460
  2.6 39.2 %all-to-all-start.1 = ((bf16[8,1,128]{2,1,0:T(2,128)(2,1)}), bf16[8,1,128]{2,1,0:T(2,128)(2,1)S(1)}, u32[]{:S(2)}, u32[]{:S(2)}) async-start(bf16[8,1,128]{2,1,0:T(2,128)(2,1)} %copy.26), calls=%async_computation.1 | async-start | bytes 8192 | tf_op jit(solution)/shard_map/all_to_all | solution.py:74
  41.8 277.2 %all-to-all-start = ((bf16[8,128,1024]{2,1,0:T(8,128)(2,1)}), bf16[8,128,1024]{2,1,0:T(8,128)(2,1)}, u32[]{:S(2)}, u32[]{:S(2)}) async-start(bf16[8,128,1024]{2,1,0:T(8,128)(2,1)} %fusion.21), calls=%async_computation | async-start | bytes 4194304 | tf_op jit(solution)/shard_map/all_to_all | solution.py:73
  48.7 33.2 %collective-permute-start = (bf16[256,1024]{1,0:T(8,128)(2,1)S(1)}, bf16[256,1024]{1,0:T(8,128)(2,1)S(1)}, u32[]{:S(2)}, u32[]{:S(2)}) collective-permute-start(bf16[256,1024]{1,0:T(8,128)(2,1)S(1)} %get-tuple-element.315), channel_id=1, source_target_pairs={{0,1},{1,2},{2,3},{3,4},{4,5},{5,6},{6,7},{7,8},{8,9},{9,10},{10,1... | collective-permute-start | bytes 1572872 | tf_op jit(solution)/shard_map/while/body/eval_jaxpr/ppermute | solution.py:10
  53.2 29.4 %copy-start.1 = (f32[8,128,1024]{2,1,0:T(8,128)S(1)}, f32[8,128,1024]{2,1,0:T(8,128)}, u32[]{:S(2)}) copy-start(f32[8,128,1024]{2,1,0:T(8,128)} %get-tuple-element.314) | copy-start | bytes 12582916 | tf_op jit(solution)/shard_map/while
  86.3 12.2 %collective-permute-start = (bf16[256,1024]{1,0:T(8,128)(2,1)S(1)}, bf16[256,1024]{1,0:T(8,128)(2,1)S(1)}, u32[]{:S(2)}, u32[]{:S(2)}) collective-permute-start(bf16[256,1024]{1,0:T(8,128)(2,1)S(1)} %get-tuple-element.315), channel_id=1, source_target_pairs={{0,1},{1,2},{2,3},{3,4},{4,5},{5,6},{6,7},{7,8},{8,9},{9,10},{10,1... | collective-permute-start | bytes 1572872 | tf_op jit(solution)/shard_map/while/body/eval_jaxpr/ppermute | solution.py:10
  90.8 8.4 %copy-start.1 = (f32[8,128,1024]{2,1,0:T(8,128)S(1)}, f32[8,128,1024]{2,1,0:T(8,128)}, u32[]{:S(2)}) copy-start(f32[8,128,1024]{2,1,0:T(8,128)} %get-tuple-element.314) | copy-start | bytes 12582916 | tf_op jit(solution)/shard_map/while
  102.9 12.2 %collective-permute-start = (bf16[256,1024]{1,0:T(8,128)(2,1)S(1)}, bf16[256,1024]{1,0:T(8,128)(2,1)S(1)}, u32[]{:S(2)}, u32[]{:S(2)}) collective-permute-start(bf16[256,1024]{1,0:T(8,128)(2,1)S(1)} %get-tuple-element.315), channel_id=1, source_target_pairs={{0,1},{1,2},{2,3},{3,4},{4,5},{5,6},{6,7},{7,8},{8,9},{9,10},{10,1... | collective-permute-start | bytes 1572872 | tf_op jit(solution)/shard_map/while/body/eval_jaxpr/ppermute | solution.py:10
  107.4 8.4 %copy-start.1 = (f32[8,128,1024]{2,1,0:T(8,128)S(1)}, f32[8,128,1024]{2,1,0:T(8,128)}, u32[]{:S(2)}) copy-start(f32[8,128,1024]{2,1,0:T(8,128)} %get-tuple-element.314) | copy-start | bytes 12582916 | tf_op jit(solution)/shard_map/while
  119.5 12.2 %collective-permute-start = (bf16[256,1024]{1,0:T(8,128)(2,1)S(1)}, bf16[256,1024]{1,0:T(8,128)(2,1)S(1)}, u32[]{:S(2)}, u32[]{:S(2)}) collective-permute-start(bf16[256,1024]{1,0:T(8,128)(2,1)S(1)} %get-tuple-element.315), channel_id=1, source_target_pairs={{0,1},{1,2},{2,3},{3,4},{4,5},{5,6},{6,7},{7,8},{8,9},{9,10},{10,1... | collective-permute-start | bytes 1572872 | tf_op jit(solution)/shard_map/while/body/eval_jaxpr/ppermute | solution.py:10
  124.1 8.4 %copy-start.1 = (f32[8,128,1024]{2,1,0:T(8,128)S(1)}, f32[8,128,1024]{2,1,0:T(8,128)}, u32[]{:S(2)}) copy-start(f32[8,128,1024]{2,1,0:T(8,128)} %get-tuple-element.314) | copy-start | bytes 12582916 | tf_op jit(solution)/shard_map/while
  136.1 12.2 %collective-permute-start = (bf16[256,1024]{1,0:T(8,128)(2,1)S(1)}, bf16[256,1024]{1,0:T(8,128)(2,1)S(1)}, u32[]{:S(2)}, u32[]{:S(2)}) collective-permute-start(bf16[256,1024]{1,0:T(8,128)(2,1)S(1)} %get-tuple-element.315), channel_id=1, source_target_pairs={{0,1},{1,2},{2,3},{3,4},{4,5},{5,6},{6,7},{7,8},{8,9},{9,10},{10,1... | collective-permute-start | bytes 1572872 | tf_op jit(solution)/shard_map/while/body/eval_jaxpr/ppermute | solution.py:10
  140.7 8.4 %copy-start.1 = (f32[8,128,1024]{2,1,0:T(8,128)S(1)}, f32[8,128,1024]{2,1,0:T(8,128)}, u32[]{:S(2)}) copy-start(f32[8,128,1024]{2,1,0:T(8,128)} %get-tuple-element.314) | copy-start | bytes 12582916 | tf_op jit(solution)/shard_map/while
  152.8 12.2 %collective-permute-start = (bf16[256,1024]{1,0:T(8,128)(2,1)S(1)}, bf16[256,1024]{1,0:T(8,128)(2,1)S(1)}, u32[]{:S(2)}, u32[]{:S(2)}) collective-permute-start(bf16[256,1024]{1,0:T(8,128)(2,1)S(1)} %get-tuple-element.315), channel_id=1, source_target_pairs={{0,1},{1,2},{2,3},{3,4},{4,5},{5,6},{6,7},{7,8},{8,9},{9,10},{10,1... | collective-permute-start | bytes 1572872 | tf_op jit(solution)/shard_map/while/body/eval_jaxpr/ppermute | solution.py:10
  157.3 8.4 %copy-start.1 = (f32[8,128,1024]{2,1,0:T(8,128)S(1)}, f32[8,128,1024]{2,1,0:T(8,128)}, u32[]{:S(2)}) copy-start(f32[8,128,1024]{2,1,0:T(8,128)} %get-tuple-element.314) | copy-start | bytes 12582916 | tf_op jit(solution)/shard_map/while
  169.4 12.2 %collective-permute-start = (bf16[256,1024]{1,0:T(8,128)(2,1)S(1)}, bf16[256,1024]{1,0:T(8,128)(2,1)S(1)}, u32[]{:S(2)}, u32[]{:S(2)}) collective-permute-start(bf16[256,1024]{1,0:T(8,128)(2,1)S(1)} %get-tuple-element.315), channel_id=1, source_target_pairs={{0,1},{1,2},{2,3},{3,4},{4,5},{5,6},{6,7},{7,8},{8,9},{9,10},{10,1... | collective-permute-start | bytes 1572872 | tf_op jit(solution)/shard_map/while/body/eval_jaxpr/ppermute | solution.py:10
  186.0 12.2 %collective-permute-start = (bf16[256,1024]{1,0:T(8,128)(2,1)S(1)}, bf16[256,1024]{1,0:T(8,128)(2,1)S(1)}, u32[]{:S(2)}, u32[]{:S(2)}) collective-permute-start(bf16[256,1024]{1,0:T(8,128)(2,1)S(1)} %get-tuple-element.315), channel_id=1, source_target_pairs={{0,1},{1,2},{2,3},{3,4},{4,5},{5,6},{6,7},{7,8},{8,9},{9,10},{10,1... | collective-permute-start | bytes 1572872 | tf_op jit(solution)/shard_map/while/body/eval_jaxpr/ppermute | solution.py:10
  202.6 12.2 %collective-permute-start = (bf16[256,1024]{1,0:T(8,128)(2,1)S(1)}, bf16[256,1024]{1,0:T(8,128)(2,1)S(1)}, u32[]{:S(2)}, u32[]{:S(2)}) collective-permute-start(bf16[256,1024]{1,0:T(8,128)(2,1)S(1)} %get-tuple-element.315), channel_id=1, source_target_pairs={{0,1},{1,2},{2,3},{3,4},{4,5},{5,6},{6,7},{7,8},{8,9},{9,10},{10,1... | collective-permute-start | bytes 1572872 | tf_op jit(solution)/shard_map/while/body/eval_jaxpr/ppermute | solution.py:10
  219.3 12.2 %collective-permute-start = (bf16[256,1024]{1,0:T(8,128)(2,1)S(1)}, bf16[256,1024]{1,0:T(8,128)(2,1)S(1)}, u32[]{:S(2)}, u32[]{:S(2)}) collective-permute-start(bf16[256,1024]{1,0:T(8,128)(2,1)S(1)} %get-tuple-element.315), channel_id=1, source_target_pairs={{0,1},{1,2},{2,3},{3,4},{4,5},{5,6},{6,7},{7,8},{8,9},{9,10},{10,1... | collective-permute-start | bytes 1572872 | tf_op jit(solution)/shard_map/while/body/eval_jaxpr/ppermute | solution.py:10
  235.9 12.2 %collective-permute-start = (bf16[256,1024]{1,0:T(8,128)(2,1)S(1)}, bf16[256,1024]{1,0:T(8,128)(2,1)S(1)}, u32[]{:S(2)}, u32[]{:S(2)}) collective-permute-start(bf16[256,1024]{1,0:T(8,128)(2,1)S(1)} %get-tuple-element.315), channel_id=1, source_target_pairs={{0,1},{1,2},{2,3},{3,4},{4,5},{5,6},{6,7},{7,8},{8,9},{9,10},{10,1... | collective-permute-start | bytes 1572872 | tf_op jit(solution)/shard_map/while/body/eval_jaxpr/ppermute | solution.py:10
  252.5 12.2 %collective-permute-start = (bf16[256,1024]{1,0:T(8,128)(2,1)S(1)}, bf16[256,1024]{1,0:T(8,128)(2,1)S(1)}, u32[]{:S(2)}, u32[]{:S(2)}) collective-permute-start(bf16[256,1024]{1,0:T(8,128)(2,1)S(1)} %get-tuple-element.315), channel_id=1, source_target_pairs={{0,1},{1,2},{2,3},{3,4},{4,5},{5,6},{6,7},{7,8},{8,9},{9,10},{10,1... | collective-permute-start | bytes 1572872 | tf_op jit(solution)/shard_map/while/body/eval_jaxpr/ppermute | solution.py:10
  269.1 12.2 %collective-permute-start = (bf16[256,1024]{1,0:T(8,128)(2,1)S(1)}, bf16[256,1024]{1,0:T(8,128)(2,1)S(1)}, u32[]{:S(2)}, u32[]{:S(2)}) collective-permute-start(bf16[256,1024]{1,0:T(8,128)(2,1)S(1)} %get-tuple-element.315), channel_id=1, source_target_pairs={{0,1},{1,2},{2,3},{3,4},{4,5},{5,6},{6,7},{7,8},{8,9},{9,10},{10,1... | collective-permute-start | bytes 1572872 | tf_op jit(solution)/shard_map/while/body/eval_jaxpr/ppermute | solution.py:10
  285.8 12.2 %collective-permute-start = (bf16[256,1024]{1,0:T(8,128)(2,1)S(1)}, bf16[256,1024]{1,0:T(8,128)(2,1)S(1)}, u32[]{:S(2)}, u32[]{:S(2)}) collective-permute-start(bf16[256,1024]{1,0:T(8,128)(2,1)S(1)} %get-tuple-element.315), channel_id=1, source_target_pairs={{0,1},{1,2},{2,3},{3,4},{4,5},{5,6},{6,7},{7,8},{8,9},{9,10},{10,1... | collective-permute-start | bytes 1572872 | tf_op jit(solution)/shard_map/while/body/eval_jaxpr/ppermute | solution.py:10
  302.4 12.2 %collective-permute-start = (bf16[256,1024]{1,0:T(8,128)(2,1)S(1)}, bf16[256,1024]{1,0:T(8,128)(2,1)S(1)}, u32[]{:S(2)}, u32[]{:S(2)}) collective-permute-start(bf16[256,1024]{1,0:T(8,128)(2,1)S(1)} %get-tuple-element.315), channel_id=1, source_target_pairs={{0,1},{1,2},{2,3},{3,4},{4,5},{5,6},{6,7},{7,8},{8,9},{9,10},{10,1... | collective-permute-start | bytes 1572872 | tf_op jit(solution)/shard_map/while/body/eval_jaxpr/ppermute | solution.py:10
  (32 other events, 144.4 us)
where the time goes:
time: 334 us; the launch traced here: 333 us
  local copies, waits for them, and re-layouts  122 us (37%)
  waiting for transfers between devices  96.6 us (29%)
  matrix products  94.3 us (28%)
  starting transfers between devices  11.8 us (4%)
  other arithmetic  7.15 us (2%)
    ppermute x15, waiting for transfers between devices, from_behind(): return lax.ppermute(value, axis, pairs)  96.6 us
    slice x16, local copies, waits for them, and re-layouts, add_source(): tiles_six[:, which_half]  72.5 us
    dot_general x32, matrix products, add_source(): jnp.einsum('nt,tij->nij', select, chosen, preferred_element_type=jnp.floa...  40 us
    dot_general x32, matrix products, add_source(): jnp.einsum('nij,jd->nid', placed, hub_half, preferred_element_type=jnp.fl...  38.9 us
    while x75, local copies, waits for them, and re-layouts  30 us
    unnamed x21, local copies, waits for them, and re-layouts  8.67 us
  transfers between devices with their start and end apart: 17, of which 15 were waited for; matrix products, arithmetic and copies ran while one was open for 53% of the time, Pallas kernels for 0%

commit v1 on v0

v1 whole, which is shorter than its diff:
```python
import numpy as np
import jax
import jax.numpy as jnp
from jax import lax
from jax.experimental import pallas as pl
from jax.experimental.pallas import tpu as pltpu
from jax.sharding import PartitionSpec as P

MESH_AXES = ("row", "col")
D = 1024
TB = 128
NODES = 1024
SLOTS = 128
PAD = 8
MIB = 1 << 20


def flat(y, xl, z, xh, k):
    return (y * 2 + xl) * 16 + z * 4 + xh * 2 + k


def pairs_of(move):
    pairs = []
    for source in range(128):
        row, col = divmod(source, 16)
        place = (row // 2, row % 2, col // 4, (col // 2) % 2, col % 2)
        pairs.append((source, flat(*move(*place))))
    return pairs


ACROSS = pairs_of(lambda y, xl, z, xh, k: (y, 1 - xl, z, 1 - xh, k))
UP = pairs_of(lambda y, xl, z, xh, k: (y, xl, (z + 1) % 4, xh, k))
DOWN = pairs_of(lambda y, xl, z, xh, k: (y, xl, (z - 1) % 4, xh, k))
CORE = pairs_of(lambda y, xl, z, xh, k: (y, xl, z, xh, 1 - k))


def send(value, pairs):
    return lax.ppermute(value, MESH_AXES, pairs)


def both_cores(halves):
    return [(dz, dx, 0, h) for dz, dx, h in halves] + [(dz, dx, 1, h) for dz, dx, h in halves]


def whole(dz, dx):
    return [(dz, dx, 0), (dz, dx, 1)]


FIRST = [(0, 0, 0, 0), (0, 0, 0, 1), (0, 0, 1, 0), (0, 0, 1, 1)] + both_cores(
    whole(0, 1) + whole(-1, 0) + whole(1, 0)
)
SECOND = both_cores([(-1, 1, 0), (2, 0, 0), (-1, 1, 1), (1, 1, 0), (1, 1, 1), (2, 0, 1)])
THIRD = both_cores([(2, 1, 0), (2, 1, 1)])
ORDER = np.array(FIRST + SECOND + THIRD, np.int32)


def half_order():
    col = lax.axis_index("col").astype(jnp.int32)
    z, xh, k = col // 4, (col // 2) % 2, col % 2
    dz, dx, dk, h = (jnp.asarray(ORDER[:, i]) for i in range(4))
    shard = ((z + dz) % 4) * 4 + (xh ^ dx) * 2 + (k ^ dk)
    return shard * 2 + h


def message_kernel(count_ref, rows_ref, weight_ref, feats_ref, out_ref, hot_ref):
    slot = lax.broadcasted_iota(jnp.int32, (1, SLOTS), 1)
    kept = [
        jnp.where(slot < count_ref[d], weight_ref[d : d + 1, :].astype(jnp.float32), 0.0)
        for d in range(8)
    ]
    kept = jnp.concatenate(kept, axis=0)
    kept_t = jnp.transpose(kept)

    @pl.when(pl.program_id(0) == 0)
    def _():
        rows_t = jnp.transpose(rows_ref[...])
        node = lax.broadcasted_iota(jnp.int32, (SLOTS, NODES), 1)
        for d in range(8):
            hot_ref[d * SLOTS : (d + 1) * SLOTS, :] = jnp.where(
                rows_t[:, d : d + 1] == node, 1.0, 0.0
            ).astype(jnp.bfloat16)

    picked = jnp.dot(hot_ref[...], feats_ref[...], preferred_element_type=jnp.float32)
    for d in range(8):
        block = picked[d * SLOTS : (d + 1) * SLOTS, :] * kept_t[:, d : d + 1]
        out_ref[d, 0:SLOTS, :] = block.astype(jnp.bfloat16)
        line = jnp.broadcast_to(kept[d : d + 1, :], (PAD, SLOTS)).astype(jnp.bfloat16)
        out_ref[d, SLOTS : SLOTS + PAD, 0:SLOTS] = line
        out_ref[d, SLOTS : SLOTS + PAD, SLOTS:] = jnp.zeros_like(
            out_ref[d, SLOTS : SLOTS + PAD, SLOTS:]
        )


def messages(node_feats, send_rows, send_count, send_weight):
    tn = 256
    return pl.pallas_call(
        message_kernel,
        grid_spec=pltpu.PrefetchScalarGridSpec(
            num_scalar_prefetch=1,
            grid=(D // tn,),
            in_specs=[
                pl.BlockSpec((8, SLOTS), lambda j, c: (0, 0)),
                pl.BlockSpec((8, SLOTS), lambda j, c: (0, 0)),
                pl.BlockSpec((NODES, tn), lambda j, c: (0, j)),
            ],
            out_specs=pl.BlockSpec((8, SLOTS + PAD, tn), lambda j, c: (0, 0, j)),
            scratch_shapes=[pltpu.VMEM((NODES, NODES), jnp.bfloat16)],
        ),
        out_shape=jax.ShapeDtypeStruct((8, SLOTS + PAD, D), jnp.bfloat16),
        compiler_params=pltpu.CompilerParams(vmem_limit_bytes=16 * MIB),
        name="messages",
    )(send_count.reshape(8), send_rows, send_weight, node_feats)


PER_STEP = 4


def place_kernel(order_ref, blocks_ref, *refs):
    tiles = refs[:PER_STEP]
    out_ref, sums_ref = refs[PER_STEP:]
    step = pl.program_id(0)

    @pl.when(step == 0)
    def _():
        sums_ref[...] = jnp.zeros_like(sums_ref)

    out_ref[...] = jnp.zeros_like(out_ref)
    for q in range(PER_STEP):
        first = order_ref[step * PER_STEP + q] * 4
        for t in range(4):
            at = pl.multiple_of(blocks_ref[first + t] * TB, TB)
            tile = tiles[q][t]
            out_ref[pl.ds(at, TB), q * TB : (q + 1) * TB] = tile
            sums_ref[pl.ds(at, TB), :] += tile.astype(jnp.float32)


def placed_tiles(order, tile_blocks, tile_weights):
    def tile_spec(q):
        return pl.BlockSpec((4, TB, TB), lambda i, o, b: (o[i * PER_STEP + q], 0, 0))

    return pl.pallas_call(
        place_kernel,
        grid_spec=pltpu.PrefetchScalarGridSpec(
            num_scalar_prefetch=2,
            grid=(32 // PER_STEP,),
            in_specs=[tile_spec(q) for q in range(PER_STEP)],
            out_specs=[
                pl.BlockSpec((NODES, PER_STEP * TB), lambda i, o, b: (0, i)),
                pl.BlockSpec((NODES, TB), lambda i, o, b: (0, 0)),
            ],
        ),
        out_shape=[
            jax.ShapeDtypeStruct((NODES, 32 * TB), jnp.bfloat16),
            jax.ShapeDtypeStruct((NODES, TB), jnp.float32),
        ],
        compiler_params=pltpu.CompilerParams(vmem_limit_bytes=16 * MIB),
        name="placed_tiles",
    )(order, tile_blocks.reshape(128), *([tile_weights] * PER_STEP))


def self_kernel(feats_ref, weight_ref, bias_ref, out_ref):
    out_ref[...] = (
        jnp.dot(feats_ref[...], weight_ref[...], preferred_element_type=jnp.float32)
        + bias_ref[...]
    )


def self_part(node_feats, self_weight, out_bias):
    tm = 256
    return pl.pallas_call(
        self_kernel,
        grid=(NODES // tm,),
        in_specs=[
            pl.BlockSpec((tm, D), lambda i: (i, 0)),
            pl.BlockSpec((D, D), lambda i: (0, 0)),
            pl.BlockSpec((1, D), lambda i: (0, 0)),
        ],
        out_specs=pl.BlockSpec((tm, D), lambda i: (i, 0)),
        out_shape=jax.ShapeDtypeStruct((NODES, D), jnp.float32),
        compiler_params=pltpu.CompilerParams(vmem_limit_bytes=16 * MIB),
        name="self_part",
    )(node_feats, self_weight, out_bias.reshape(1, D))


def stack(parts, hub_ref):
    at = 0
    for part in parts:
        rows = part.shape[0]
        hub_ref[at : at + rows, :] = part[...]
        at += rows


def hub_kernel(placed_ref, *refs, count, carried):
    parts = refs[:count]
    refs = refs[count:]
    out_ref, hub_ref = refs[-2:]

    @pl.when(pl.program_id(0) == 0)
    def _():
        stack(parts, hub_ref)

    product = jnp.dot(placed_ref[...], hub_ref[...], preferred_element_type=jnp.float32)
    if carried:
        product = product + refs[0][...]
    out_ref[...] = product


def hub_products(placed, first, parts, carry=None):
    tm = 256
    width = sum(part.shape[0] for part in parts)
    column = first // width if first % width == 0 else None
    operands = [placed, *parts]
    if column is None:
        spec = pl.BlockSpec((pl.Element(tm), pl.Element(width)), lambda i: (i * tm, first))
    else:
        spec = pl.BlockSpec((tm, width), lambda i: (i, column))
    in_specs = [spec]
    in_specs += [pl.BlockSpec(part.shape, lambda i: (0, 0)) for part in parts]
    if carry is not None:
        in_specs.append(pl.BlockSpec((tm, D), lambda i: (i, 0)))
        operands.append(carry)

    def body(*refs):
        hub_kernel(*refs, count=len(parts), carried=carry is not None)

    return pl.pallas_call(
        body,
        grid=(NODES // tm,),
        in_specs=in_specs,
        out_specs=pl.BlockSpec((tm, D), lambda i: (i, 0)),
        out_shape=jax.ShapeDtypeStruct((NODES, D), jnp.float32),
        scratch_shapes=[pltpu.VMEM((width, D), jnp.bfloat16)],
        compiler_params=pltpu.CompilerParams(vmem_limit_bytes=32 * MIB),
        name="hub_products",
    )(*operands)


def last_kernel(
    placed_ref, f0, f1, c0, c1, sums_ref, carry_ref, base_ref, at_ref, got_ref, line_ref,
    weight_ref, out_ref, hub_ref, hot_ref,
):
    tm = out_ref.shape[0]
    step = pl.program_id(0)

    @pl.when(step == 0)
    def _():
        stack((f0, f1, c0, c1), hub_ref)

    node = lax.broadcasted_iota(jnp.int32, (tm, SLOTS), 0) + step * tm
    weights = sums_ref[...]
    for o in range(8):
        hit = at_ref[o : o + 1, :] == node
        hot_ref[:, o * SLOTS : (o + 1) * SLOTS] = jnp.where(hit, 1.0, 0.0).astype(jnp.bfloat16)
        line = line_ref[o, 0:1, 0:SLOTS].astype(jnp.float32)
        weights = weights + jnp.where(hit, line, 0.0)
    weight_sum = jnp.sum(weights, axis=-1, keepdims=True)
    combined = carry_ref[...] + jnp.dot(
        placed_ref[...], hub_ref[...], preferred_element_type=jnp.float32
    )
    combined = combined + jnp.dot(
        hot_ref[...],
        got_ref[...].reshape(8 * SLOTS, D),
        preferred_element_type=jnp.float32,
    )
    neighbour = (combined * lax.rsqrt(1.0 + weight_sum)).astype(jnp.bfloat16)
    preact = base_ref[...] + jnp.dot(
        neighbour, weight_ref[...], preferred_element_type=jnp.float32
    )
    hidden = jnp.maximum(preact, 0.0)
    scale = lax.rsqrt(jnp.mean(hidden * hidden, axis=-1, keepdims=True) + 1e-06)
    out_ref[...] = (hidden * scale).astype(jnp.bfloat16)


def last_part(placed, parts, sums, carry, base, arrive_node, arrived, neigh_weight):
    tm = 256
    width = 512
    column = placed.shape[1] // width - 1
    return pl.pallas_call(
        last_kernel,
        grid=(NODES // tm,),
        in_specs=[pl.BlockSpec((tm, width), lambda i: (i, column))]
        + [pl.BlockSpec(part.shape, lambda i: (0, 0)) for part in parts]
        + [
            pl.BlockSpec((tm, TB), lambda i: (i, 0)),
            pl.BlockSpec((tm, D), lambda i: (i, 0)),
            pl.BlockSpec((tm, D), lambda i: (i, 0)),
            pl.BlockSpec((8, SLOTS), lambda i: (0, 0)),
            pl.BlockSpec((8, SLOTS, D), lambda i: (0, 0, 0)),
            pl.BlockSpec((8, PAD, SLOTS), lambda i: (0, SLOTS // PAD, 0)),
            pl.BlockSpec((D, D), lambda i: (0, 0)),
        ],
        out_specs=pl.BlockSpec((tm, D), lambda i: (i, 0)),
        out_shape=jax.ShapeDtypeStruct((NODES, D), jnp.bfloat16),
        scratch_shapes=[
            pltpu.VMEM((width, D), jnp.bfloat16),
            pltpu.VMEM((tm, 8 * SLOTS), jnp.bfloat16),
        ],
        compiler_params=pltpu.CompilerParams(vmem_limit_bytes=32 * MIB),
        name="last_part",
    )(placed, *parts, sums, carry, base, arrive_node, arrived, arrived, neigh_weight)


def shards(
    node_feats,
    hub_feats,
    self_weight,
    neigh_weight,
    out_bias,
    tile_weights,
    tile_blocks,
    send_rows,
    send_count,
    send_weight,
    arrive_node,
):
    own = hub_feats
    across = send(own, ACROSS)
    up = send(own, UP)
    down = send(own, DOWN)
    own_c = send(own, CORE)

    message = messages(node_feats, send_rows, send_count, send_weight)
    arrived = lax.all_to_all(message, "row", split_axis=0, concat_axis=0, tiled=True)

    placed, sums = placed_tiles(half_order(), tile_blocks, tile_weights)
    base = self_part(node_feats, self_weight, out_bias)

    up2 = send(jnp.concatenate([across[:TB], up[:TB]], 0), UP)
    down2 = send(jnp.concatenate([across[TB:], down[TB:]], 0), DOWN)
    across2 = send(jnp.concatenate([up[TB:], down[:TB]], 0), ACROSS)
    across_c = send(across, CORE)
    up_c = send(up, CORE)
    down_c = send(down, CORE)

    carry = hub_products(
        placed, 0, [own, own_c, across, up, down, across_c, up_c, down_c]
    )

    up3 = send(up2[:TB], UP)
    down3 = send(down2[:TB], DOWN)
    up2_c = send(up2, CORE)
    across2_c = send(across2, CORE)
    down2_c = send(down2, CORE)
    carry = hub_products(
        placed, 2048, [up2, across2, down2, up2_c, across2_c, down2_c], carry
    )
    up3_c = send(up3, CORE)
    down3_c = send(down3, CORE)
    return last_part(
        placed,
        [up3, down3, up3_c, down3_c],
        sums,
        carry,
        base,
        arrive_node,
        arrived,
        neigh_weight,
    )


def solution(mesh):
    placed = (
        P(("row", "col"), None),
        P("col", None),
        P(),
        P(),
        P(),
        P(("row", "col"), None, None),
        P(("row", "col"), None),
        P("row", "col"),
        P("row", "col"),
        P("row", "col"),
        P("row", "col"),
    )
    return jax.shard_map(
        shards, mesh=mesh, in_specs=placed, out_specs=P(("row", "col"), None), check_vma=False
    )
```

time: 334 us -> 105 us (0.31)
  the two profiles are of different devices: /device:TPU:2 before, /device:TPU:1 now
where the time goes in v1:
time: 105 us; the launch traced here: 104 us
  Pallas kernels  33.3 us (32%)
  local copies, waits for them, and re-layouts  26.6 us (25%)
  starting transfers between devices  25.8 us (25%)
  waiting for transfers between devices  17.7 us (17%)
    unnamed x68, local copies, waits for them, and re-layouts  23.5 us
    ppermute x17, starting transfers between devices, send(): return lax.ppermute(value, MESH_AXES, pairs)  21.6 us
    ppermute x17, waiting for transfers between devices, send(): return lax.ppermute(value, MESH_AXES, pairs)  17.7 us
    pallas_call x2, Pallas kernels, hub_products(): pl.pallas_call(body, grid=(NODES // tm,), in_specs=in_specs, out_specs=pl...  13.3 us
    pallas_call x1, Pallas kernels, last_part(): pl.pallas_call(last_kernel, grid=(NODES // tm,), in_specs=[pl.BlockSpec((...  8.85 us
    pallas_call x1, Pallas kernels, messages(): pl.pallas_call(message_kernel, grid_spec=pltpu.PrefetchScalarGridSpec(num...  4.82 us
    all_to_all x1, starting transfers between devices, shards(): lax.all_to_all(message, 'row', split_axis=0, concat_axis=0, tiled=True)  4.19 us
    pallas_call x1, Pallas kernels, placed_tiles(): pl.pallas_call(place_kernel, grid_spec=pltpu.PrefetchScalarGridSpec(num_s...  3.45 us
  transfers between devices with their start and end apart: 18, of which 3 were waited for; matrix products, arithmetic and copies ran while one was open for 3% of the time, Pallas kernels for 23%

profile of v1, /device:TPU:1, one launch (start us, length us, event | category | flops | bytes accessed | tf_op | source)
XLA Modules:
  0.0 103.9 jit_solution(14586586549113888376)
XLA Ops:
  0.0 2.5 %collective-permute-start.1 = (bf16[256,1024]{1,0:T(8,128)(2,1)}, bf16[256,1024]{1,0:T(8,128)(2,1)S(1)}, u32[]{:S(2)}, u32[]{:S(2)}) collective-permute-start(bf16[256,1024]{1,0:T(8,128)(2,1)} %refs_1_.3), channel_id=1, source_target_pairs={{0,4},{1,5},{2,6},{3,7},{4,8},{5,9},{6,10},{7,11},{8,12},{9,13},{1... | collective-permute-start | bytes 1572872 | tf_op jit(solution)/shard_map/ppermute | solution.py:38
  2.5 2.5 %collective-permute-start = (bf16[256,1024]{1,0:T(8,128)(2,1)}, bf16[256,1024]{1,0:T(8,128)(2,1)S(1)}, u32[]{:S(2)}, u32[]{:S(2)}) collective-permute-start(bf16[256,1024]{1,0:T(8,128)(2,1)} %refs_1_.3), channel_id=1, source_target_pairs={{0,18},{1,19},{2,16},{3,17},{4,22},{5,23},{6,20},{7,21},{8,26},{9,... | collective-permute-start | bytes 1572872 | tf_op jit(solution)/shard_map/ppermute | solution.py:38
  4.9 2.1 %collective-permute-start.4 = (bf16[256,1024]{1,0:T(8,128)(2,1)}, bf16[256,1024]{1,0:T(8,128)(2,1)}, u32[]{:S(2)}, u32[]{:S(2)}) collective-permute-start(bf16[256,1024]{1,0:T(8,128)(2,1)} %refs_1_.3), channel_id=1, source_target_pairs={{0,12},{1,13},{2,14},{3,15},{4,0},{5,1},{6,2},{7,3},{8,4},{9,5},{1... | collective-permute-start | bytes 1572872 | tf_op jit(solution)/shard_map/ppermute | solution.py:38
  7.1 1.6 %copy-done.8 = bf16[1024,1024]{1,0:T(8,128)(2,1)S(1)} copy-done((bf16[1024,1024]{1,0:T(8,128)(2,1)S(1)}, bf16[1024,1024]{1,0:T(8,128)(2,1)}, u32[]{:S(2)}) %copy-start.8) | copy-done | bytes 2097176
  10.7 4.8 %messages.1 = bf16[8,136,1024]{2,1,0:T(8,128)(2,1)S(1)} custom-call(s32[8]{0:T(128)S(1)} %bitcast.4, s32[8,128]{1,0:T(8,128)S(1)} %copy-done.24, bf16[8,128]{1,0:T(8,128)(2,1)S(1)} %copy-done.27, bf16[1024,1024]{1,0:T(8,128)(2,1)S(1)} %copy-done.8), custom_call_target="tpu_custom_call" | custom-call | tf_op jit(solution)/shard_map/messages/pallas_call | solution.py:96
  16.9 4.2 %all-to-all-start = ((bf16[8,136,1024]{2,1,0:T(8,128)(2,1)}), bf16[8,136,1024]{2,1,0:T(8,128)(2,1)S(1)}, u32[]{:S(2)}, u32[]{:S(2)}) async-start(bf16[8,136,1024]{2,1,0:T(8,128)(2,1)} %copy-done.7), calls=%async_computation | async-start | bytes 4456448 | tf_op jit(solution)/shard_map/all_to_all | solution.py:323
  22.5 2.7 %collective-permute-start.5 = (bf16[256,1024]{1,0:T(8,128)(2,1)S(1)}, bf16[256,1024]{1,0:T(8,128)(2,1)}, u32[]{:S(2)}, u32[]{:S(2)}) collective-permute-start(bf16[256,1024]{1,0:T(8,128)(2,1)S(1)} %pad_maximum_fusion.1), channel_id=1, source_target_pairs={{0,12},{1,13},{2,14},{3,15},{4,0},{5,1},{6,2},{7,3},{8,4},{9,5},{1... | collective-permute-start | bytes 1572872 | tf_op jit(solution)/shard_map/ppermute | solution.py:38
  25.2 2.1 %collective-permute-start.13 = (bf16[256,1024]{1,0:T(8,128)(2,1)S(1)}, bf16[256,1024]{1,0:T(8,128)(2,1)S(1)}, u32[]{:S(2)}, u32[]{:S(2)}) collective-permute-start(bf16[256,1024]{1,0:T(8,128)(2,1)S(1)} %copy-done.12), channel_id=1, source_target_pairs={{0,1},{1,0},{2,3},{3,2},{4,5},{5,4},{6,7},{7,6},{8,9},{9,8},{10,11... | collective-permute-start | bytes 1572872 | tf_op jit(solution)/shard_map/ppermute | solution.py:38
  27.9 6.6 %collective-permute-done.2.refs_1_ = bf16[256,1024]{1,0:T(8,128)(2,1)} collective-permute-done((bf16[256,1024]{1,0:T(8,128)(2,1)S(1)}, bf16[256,1024]{1,0:T(8,128)(2,1)}, u32[]{:S(2)}, u32[]{:S(2)}) %collective-permute-start.2) | collective-permute-done | bytes 524320 | tf_op jit(solution)/shard_map/ppermute | solution.py:38
  35.6 3.0 %collective-permute-start.16 = (bf16[256,1024]{1,0:T(8,128)(2,1)}, bf16[256,1024]{1,0:T(8,128)(2,1)S(1)}, u32[]{:S(2)}, u32[]{:S(2)}) collective-permute-start(bf16[256,1024]{1,0:T(8,128)(2,1)} %collective-permute-done.4.refs_5_), channel_id=1, source_target_pairs={{0,1},{1,0},{2,3},{3,2},{4,5},{5,4},{6,7},{7,6},{8,9},{9,8},{10,11... | collective-permute-start | bytes 1572872 | tf_op jit(solution)/shard_map/ppermute | solution.py:38
  43.5 3.3 %collective-permute-done.9.refs_2_ = bf16[256,1024]{1,0:T(8,128)(2,1)} collective-permute-done((bf16[256,1024]{1,0:T(8,128)(2,1)S(1)}, bf16[256,1024]{1,0:T(8,128)(2,1)}, u32[]{:S(2)}, u32[]{:S(2)}) %collective-permute-start.9) | collective-permute-done | bytes 524320 | tf_op jit(solution)/shard_map/ppermute | solution.py:38
  46.8 3.4 %collective-permute-start.11 = (bf16[256,1024]{1,0:T(8,128)(2,1)}, bf16[256,1024]{1,0:T(8,128)(2,1)}, u32[]{:S(2)}, u32[]{:S(2)}) collective-permute-start(bf16[256,1024]{1,0:T(8,128)(2,1)} %collective-permute-done.9.refs_2_), channel_id=1, source_target_pairs={{0,1},{1,0},{2,3},{3,2},{4,5},{5,4},{6,7},{7,6},{8,9},{9,8},{10,11... | collective-permute-start | bytes 1572872 | tf_op jit(solution)/shard_map/ppermute | solution.py:38
  51.3 7.7 %collective-permute-done.6.f1 = bf16[128,1024]{1,0:T(8,128)(2,1)} collective-permute-done((bf16[128,1024]{1,0:T(8,128)(2,1)S(1)}, bf16[128,1024]{1,0:T(8,128)(2,1)}, u32[]{:S(2)}, u32[]{:S(2)}) %collective-permute-start.6) | collective-permute-done | bytes 262176 | tf_op jit(solution)/shard_map/ppermute | solution.py:38
  59.8 1.6 %copy-done.9 = bf16[1024,1024]{1,0:T(8,128)(2,1)S(1)} copy-done((bf16[1024,1024]{1,0:T(8,128)(2,1)S(1)}, bf16[1024,1024]{1,0:T(8,128)(2,1)}, u32[]{:S(2)}) %copy-start.9) | copy-done | bytes 2097176
  63.1 2.9 %self_part.1.base_ref = f32[1024,1024]{1,0:T(8,128)S(1)} custom-call(bf16[1024,1024]{1,0:T(8,128)(2,1)S(1)} %copy-done.9, bf16[1024,1024]{1,0:T(8,128)(2,1)S(1)} %copy-done.10, f32[1,1024]{1,0:T(1,128)S(1)} %bitcast.3), custom_call_target="tpu_custom_call" | custom-call | tf_op jit(solution)/shard_map/self_part/pallas_call | solution.py:170
  66.1 3.4 %placed_tiles.1 = (bf16[1024,4096]{1,0:T(8,128)(2,1)S(1)}, f32[1024,128]{1,0:T(8,128)S(1)}) custom-call(s32[32]{0:T(128)S(1)} %multiply_add_fusion.order_ref, s32[128]{0:T(128)S(1)} %bitcast.5, bf16[128,128,128]{2,1,0:T(8,128)(2,1)S(1)} %copy-done.2, bf16[128,128,128]{2,1,0:T(8,128)(2,1)S(1)} %copy-done.2, bf16[128,128,128]{2,1,0:T(8,128)(2,1)S(1)} %copy-done.2, ...), custom_call_target="tpu_custom_call" | custom-call | tf_op jit(solution)/shard_map/placed_tiles/pallas_call | solution.py:141
  70.4 7.0 %hub_products.2.refs_7_ = f32[1024,1024]{1,0:T(8,128)S(1)} custom-call(bf16[1024,4096]{1,0:T(8,128)(2,1)S(1)} %get-tuple-element.7.refs_0_.placed_ref, bf16[256,1024]{1,0:T(8,128)(2,1)S(1)} %copy-done.13, bf16[256,1024]{1,0:T(8,128)(2,1)S(1)} %copy-done.15, bf16[256,1024]{1,0:T(8,128)(2,1)S(1)} %collective-permute-done.refs_3_, ...), custom_call_target="tpu_custom_call" | custom-call | tf_op jit(solution)/shard_map/hub_products/pallas_call | solution.py:226
  77.4 6.3 %hub_products.3.carry_ref = f32[1024,1024]{1,0:T(8,128)S(1)} custom-call(bf16[1024,4096]{1,0:T(8,128)(2,1)S(1)} %get-tuple-element.7.refs_0_.placed_ref, bf16[256,1024]{1,0:T(8,128)(2,1)} %collective-permute-done.2.refs_1_, bf16[256,1024]{1,0:T(8,128)(2,1)} %collective-permute-done.9.refs_2_, bf16[256,1024]{1,0:T(8,128)(2,1)} %collective-permute-done.5.refs_3_, ...), custom_call_target="tpu_custom_call" | custom-call | tf_op jit(solution)/shard_map/hub_products/pallas_call | solution.py:226
  83.7 1.9 %copy-done.3 = f32[1024,1024]{1,0:T(8,128)} copy-done((f32[1024,1024]{1,0:T(8,128)}, f32[1024,1024]{1,0:T(8,128)S(1)}, u32[]{:S(2)}) %copy-start.3) | copy-done | bytes 4194328
  85.7 3.4 %copy-done.1 = bf16[1024,4096]{1,0:T(8,128)(2,1)S(1)} copy-done((bf16[1024,4096]{1,0:T(8,128)(2,1)S(1)}, bf16[1024,4096]{1,0:T(8,128)(2,1)}, u32[]{:S(2)}) %copy-start.1) | copy-done | bytes 8388632
  89.1 2.2 %copy-done.4 = f32[1024,1024]{1,0:T(8,128)S(1)} copy-done((f32[1024,1024]{1,0:T(8,128)S(1)}, f32[1024,1024]{1,0:T(8,128)}, u32[]{:S(2)}) %copy-start.4) | copy-done | bytes 4194328
  91.3 2.2 %copy-done.6 = f32[1024,1024]{1,0:T(8,128)S(1)} copy-done((f32[1024,1024]{1,0:T(8,128)S(1)}, f32[1024,1024]{1,0:T(8,128)}, u32[]{:S(2)}) %copy-start.6) | copy-done | bytes 4194328
  93.5 1.6 %copy-done.11 = bf16[1024,1024]{1,0:T(8,128)(2,1)S(1)} copy-done((bf16[1024,1024]{1,0:T(8,128)(2,1)S(1)}, bf16[1024,1024]{1,0:T(8,128)(2,1)}, u32[]{:S(2)}) %copy-start.11) | copy-done | bytes 2097176
  95.0 8.9 %last_part.1 = bf16[1024,1024]{1,0:T(8,128)(2,1)} custom-call(bf16[1024,4096]{1,0:T(8,128)(2,1)S(1)} %copy-done.1, bf16[128,1024]{1,0:T(8,128)(2,1)S(1)} %collective-permute-done.3.f0, bf16[128,1024]{1,0:T(8,128)(2,1)} %collective-permute-done.6.f1, bf16[128,1024]{1,0:T(8,128)(2,1)} %collective-permute-done.7.c0, ...), custom_call_target="tpu_custom_call" | custom-call | tf_op jit(solution)/shard_map/last_part/pallas_call | solution.py:278
  (95 shorter events, 15.7 us)
Async XLA Ops:
  0.0 21.1 %collective-permute-start.1 = (bf16[256,1024]{1,0:T(8,128)(2,1)}, bf16[256,1024]{1,0:T(8,128)(2,1)S(1)}, u32[]{:S(2)}, u32[]{:S(2)}) collective-permute-start(bf16[256,1024]{1,0:T(8,128)(2,1)} %refs_1_.3), channel_id=1, source_target_pairs={{0,4},{1,5},{2,6},{3,7},{4,8},{5,9},{6,10},{7,11},{8,12},{9,13},{1... | collective-permute-start | bytes 1572872 | tf_op jit(solution)/shard_map/ppermute | solution.py:38
  2.5 18.7 %collective-permute-start = (bf16[256,1024]{1,0:T(8,128)(2,1)}, bf16[256,1024]{1,0:T(8,128)(2,1)S(1)}, u32[]{:S(2)}, u32[]{:S(2)}) collective-permute-start(bf16[256,1024]{1,0:T(8,128)(2,1)} %refs_1_.3), channel_id=1, source_target_pairs={{0,18},{1,19},{2,16},{3,17},{4,22},{5,23},{6,20},{7,21},{8,26},{9,... | collective-permute-start | bytes 1572872 | tf_op jit(solution)/shard_map/ppermute | solution.py:38
  4.9 16.4 %collective-permute-start.4 = (bf16[256,1024]{1,0:T(8,128)(2,1)}, bf16[256,1024]{1,0:T(8,128)(2,1)}, u32[]{:S(2)}, u32[]{:S(2)}) collective-permute-start(bf16[256,1024]{1,0:T(8,128)(2,1)} %refs_1_.3), channel_id=1, source_target_pairs={{0,12},{1,13},{2,14},{3,15},{4,0},{5,1},{6,2},{7,3},{8,4},{9,5},{1... | collective-permute-start | bytes 1572872 | tf_op jit(solution)/shard_map/ppermute | solution.py:38
  16.9 68.8 %all-to-all-start = ((bf16[8,136,1024]{2,1,0:T(8,128)(2,1)}), bf16[8,136,1024]{2,1,0:T(8,128)(2,1)S(1)}, u32[]{:S(2)}, u32[]{:S(2)}) async-start(bf16[8,136,1024]{2,1,0:T(8,128)(2,1)} %copy-done.7), calls=%async_computation | async-start | bytes 4456448 | tf_op jit(solution)/shard_map/all_to_all | solution.py:323
  21.3 38.6 %copy-start.25 = (f32[1024]{0:T(1024)S(1)}, f32[1024]{0:T(1024)}, u32[]{:S(2)}) copy-start(f32[1024]{0:T(1024)} %param.19) | copy-start | bytes 12292
  21.3 13.3 %collective-permute-start.2 = (bf16[256,1024]{1,0:T(8,128)(2,1)S(1)}, bf16[256,1024]{1,0:T(8,128)(2,1)}, u32[]{:S(2)}, u32[]{:S(2)}) collective-permute-start(bf16[256,1024]{1,0:T(8,128)(2,1)S(1)} %pad_maximum_fusion), channel_id=1, source_target_pairs={{0,4},{1,5},{2,6},{3,7},{4,8},{5,9},{6,10},{7,11},{8,12},{9,13},{1... | collective-permute-start | bytes 1572872 | tf_op jit(solution)/shard_map/ppermute | solution.py:38
  22.5 13.2 %collective-permute-start.5 = (bf16[256,1024]{1,0:T(8,128)(2,1)S(1)}, bf16[256,1024]{1,0:T(8,128)(2,1)}, u32[]{:S(2)}, u32[]{:S(2)}) collective-permute-start(bf16[256,1024]{1,0:T(8,128)(2,1)S(1)} %pad_maximum_fusion.1), channel_id=1, source_target_pairs={{0,12},{1,13},{2,14},{3,15},{4,0},{5,1},{6,2},{7,3},{8,4},{9,5},{1... | collective-permute-start | bytes 1572872 | tf_op jit(solution)/shard_map/ppermute | solution.py:38
  25.2 15.4 %collective-permute-start.13 = (bf16[256,1024]{1,0:T(8,128)(2,1)S(1)}, bf16[256,1024]{1,0:T(8,128)(2,1)S(1)}, u32[]{:S(2)}, u32[]{:S(2)}) collective-permute-start(bf16[256,1024]{1,0:T(8,128)(2,1)S(1)} %copy-done.12), channel_id=1, source_target_pairs={{0,1},{1,0},{2,3},{3,2},{4,5},{5,4},{6,7},{7,6},{8,9},{9,8},{10,11... | collective-permute-start | bytes 1572872 | tf_op jit(solution)/shard_map/ppermute | solution.py:38
  27.3 14.1 %collective-permute-start.14 = (bf16[256,1024]{1,0:T(8,128)(2,1)S(1)}, bf16[256,1024]{1,0:T(8,128)(2,1)S(1)}, u32[]{:S(2)}, u32[]{:S(2)}) collective-permute-start(bf16[256,1024]{1,0:T(8,128)(2,1)S(1)} %collective-permute-done.refs_3_), channel_id=1, source_target_pairs={{0,1},{1,0},{2,3},{3,2},{4,5},{5,4},{6,7},{7,6},{8,9},{9,8},{10,11... | collective-permute-start | bytes 1572872 | tf_op jit(solution)/shard_map/ppermute | solution.py:38
  27.3 14.9 %collective-permute-start.15 = (bf16[256,1024]{1,0:T(8,128)(2,1)S(1)}, bf16[256,1024]{1,0:T(8,128)(2,1)S(1)}, u32[]{:S(2)}, u32[]{:S(2)}) collective-permute-start(bf16[256,1024]{1,0:T(8,128)(2,1)S(1)} %collective-permute-done.1.refs_4_), channel_id=1, source_target_pairs={{0,1},{1,0},{2,3},{3,2},{4,5},{5,4},{6,7},{7,6},{8,9},{9,8},{10,11... | collective-permute-start | bytes 1572872 | tf_op jit(solution)/shard_map/ppermute | solution.py:38
  34.5 12.3 %collective-permute-start.9 = (bf16[256,1024]{1,0:T(8,128)(2,1)S(1)}, bf16[256,1024]{1,0:T(8,128)(2,1)}, u32[]{:S(2)}, u32[]{:S(2)}) collective-permute-start(bf16[256,1024]{1,0:T(8,128)(2,1)S(1)} %pad_maximum_fusion.2), channel_id=1, source_target_pairs={{0,18},{1,19},{2,16},{3,17},{4,22},{5,23},{6,20},{7,21},{8,26},{9,... | collective-permute-start | bytes 1572872 | tf_op jit(solution)/shard_map/ppermute | solution.py:38
  35.6 14.6 %collective-permute-start.16 = (bf16[256,1024]{1,0:T(8,128)(2,1)}, bf16[256,1024]{1,0:T(8,128)(2,1)S(1)}, u32[]{:S(2)}, u32[]{:S(2)}) collective-permute-start(bf16[256,1024]{1,0:T(8,128)(2,1)} %collective-permute-done.4.refs_5_), channel_id=1, source_target_pairs={{0,1},{1,0},{2,3},{3,2},{4,5},{5,4},{6,7},{7,6},{8,9},{9,8},{10,11... | collective-permute-start | bytes 1572872 | tf_op jit(solution)/shard_map/ppermute | solution.py:38
  41.4 9.6 %collective-permute-start.3 = (bf16[128,1024]{1,0:T(8,128)(2,1)S(1)}, bf16[128,1024]{1,0:T(8,128)(2,1)S(1)}, u32[]{:S(2)}, u32[]{:S(2)}) collective-permute-start(bf16[128,1024]{1,0:T(8,128)(2,1)S(1)} %slice.34), channel_id=1, source_target_pairs={{0,4},{1,5},{2,6},{3,7},{4,8},{5,9},{6,10},{7,11},{8,12},{9,13},{1... | collective-permute-start | bytes 786440 | tf_op jit(solution)/shard_map/ppermute | solution.py:38
  42.2 35.2 %collective-permute-start.10 = (bf16[256,1024]{1,0:T(8,128)(2,1)}, bf16[256,1024]{1,0:T(8,128)(2,1)}, u32[]{:S(2)}, u32[]{:S(2)}) collective-permute-start(bf16[256,1024]{1,0:T(8,128)(2,1)} %collective-permute-done.2.refs_1_), channel_id=1, source_target_pairs={{0,1},{1,0},{2,3},{3,2},{4,5},{5,4},{6,7},{7,6},{8,9},{9,8},{10,11... | collective-permute-start | bytes 1572872 | tf_op jit(solution)/shard_map/ppermute | solution.py:38
  43.0 34.4 %collective-permute-start.12 = (bf16[256,1024]{1,0:T(8,128)(2,1)}, bf16[256,1024]{1,0:T(8,128)(2,1)}, u32[]{:S(2)}, u32[]{:S(2)}) collective-permute-start(bf16[256,1024]{1,0:T(8,128)(2,1)} %collective-permute-done.5.refs_3_), channel_id=1, source_target_pairs={{0,1},{1,0},{2,3},{3,2},{4,5},{5,4},{6,7},{7,6},{8,9},{9,8},{10,11... | collective-permute-start | bytes 1572872 | tf_op jit(solution)/shard_map/ppermute | solution.py:38
  46.8 30.6 %collective-permute-start.11 = (bf16[256,1024]{1,0:T(8,128)(2,1)}, bf16[256,1024]{1,0:T(8,128)(2,1)}, u32[]{:S(2)}, u32[]{:S(2)}) collective-permute-start(bf16[256,1024]{1,0:T(8,128)(2,1)} %collective-permute-done.9.refs_2_), channel_id=1, source_target_pairs={{0,1},{1,0},{2,3},{3,2},{4,5},{5,4},{6,7},{7,6},{8,9},{9,8},{10,11... | collective-permute-start | bytes 1572872 | tf_op jit(solution)/shard_map/ppermute | solution.py:38
  51.0 8.0 %collective-permute-start.6 = (bf16[128,1024]{1,0:T(8,128)(2,1)S(1)}, bf16[128,1024]{1,0:T(8,128)(2,1)}, u32[]{:S(2)}, u32[]{:S(2)}) collective-permute-start(bf16[128,1024]{1,0:T(8,128)(2,1)S(1)} %slice.37), channel_id=1, source_target_pairs={{0,12},{1,13},{2,14},{3,15},{4,0},{5,1},{6,2},{7,3},{8,4},{9,5},{1... | collective-permute-start | bytes 786440 | tf_op jit(solution)/shard_map/ppermute | solution.py:38
  51.0 34.7 %collective-permute-start.7 = (bf16[128,1024]{1,0:T(8,128)(2,1)S(1)}, bf16[128,1024]{1,0:T(8,128)(2,1)}, u32[]{:S(2)}, u32[]{:S(2)}) collective-permute-start(bf16[128,1024]{1,0:T(8,128)(2,1)S(1)} %collective-permute-done.3.f0), channel_id=1, source_target_pairs={{0,1},{1,0},{2,3},{3,2},{4,5},{5,4},{6,7},{7,6},{8,9},{9,8},{10,11... | collective-permute-start | bytes 786440 | tf_op jit(solution)/shard_map/ppermute | solution.py:38
  59.0 26.6 %collective-permute-start.8 = (bf16[128,1024]{1,0:T(8,128)(2,1)}, bf16[128,1024]{1,0:T(8,128)(2,1)}, u32[]{:S(2)}, u32[]{:S(2)}) collective-permute-start(bf16[128,1024]{1,0:T(8,128)(2,1)} %collective-permute-done.6.f1), channel_id=1, source_target_pairs={{0,1},{1,0},{2,3},{3,2},{4,5},{5,4},{6,7},{7,6},{8,9},{9,8},{10,11... | collective-permute-start | bytes 786440 | tf_op jit(solution)/shard_map/ppermute | solution.py:38
  66.0 4.3 %copy-start.13 = (bf16[256,1024]{1,0:T(8,128)(2,1)S(1)}, bf16[256,1024]{1,0:T(8,128)(2,1)}, u32[]{:S(2)}) copy-start(bf16[256,1024]{1,0:T(8,128)(2,1)} %refs_1_.3) | copy-start | bytes 1572868
  66.0 4.3 %copy-start.15 = (bf16[256,1024]{1,0:T(8,128)(2,1)S(1)}, bf16[256,1024]{1,0:T(8,128)(2,1)}, u32[]{:S(2)}) copy-start(bf16[256,1024]{1,0:T(8,128)(2,1)} %copy-done.14) | copy-start | bytes 1572868
  70.3 7.1 %copy-start = (bf16[1024,4096]{1,0:T(8,128)(2,1)}, bf16[1024,4096]{1,0:T(8,128)(2,1)S(1)}, u32[]{:S(2)}) copy-start(bf16[1024,4096]{1,0:T(8,128)(2,1)S(1)} %get-tuple-element.7.refs_0_.placed_ref) | copy-start | bytes 25165828
  77.4 8.3 %copy-start.23 = (f32[1024,128]{1,0:T(8,128)S(1)}, f32[1024,128]{1,0:T(8,128)}, u32[]{:S(2)}) copy-start(f32[1024,128]{1,0:T(8,128)} %copy-done.22) | copy-start | bytes 1572868
  77.4 8.3 %copy-start.26 = (s32[8,128]{1,0:T(8,128)S(1)}, s32[8,128]{1,0:T(8,128)}, u32[]{:S(2)}) copy-start(s32[8,128]{1,0:T(8,128)} %at_ref.1) | copy-start | bytes 12292
  (28 other events, 61.7 us)

commit v2 on v0

v2 whole, which is shorter than its diff:
```python
import numpy as np
import jax
import jax.numpy as jnp
from jax import lax
from jax.experimental import pallas as pl
from jax.experimental.pallas import tpu as pltpu
from jax.sharding import PartitionSpec as P

MESH_AXES = ("row", "col")
D = 1024
TB = 128
NODES = 1024
SLOTS = 128
PAD = 8
MIB = 1 << 20


def flat(y, xl, z, xh, k):
    return (y * 2 + xl) * 16 + z * 4 + xh * 2 + k


def pairs_of(move):
    pairs = []
    for source in range(128):
        row, col = divmod(source, 16)
        place = (row // 2, row % 2, col // 4, (col // 2) % 2, col % 2)
        pairs.append((source, flat(*move(*place))))
    return pairs


ACROSS = pairs_of(lambda y, xl, z, xh, k: (y, 1 - xl, z, 1 - xh, k))
UP = pairs_of(lambda y, xl, z, xh, k: (y, xl, (z + 1) % 4, xh, k))
DOWN = pairs_of(lambda y, xl, z, xh, k: (y, xl, (z - 1) % 4, xh, k))
CORE = pairs_of(lambda y, xl, z, xh, k: (y, xl, z, xh, 1 - k))


def send(value, pairs):
    return lax.ppermute(value, MESH_AXES, pairs)


def both_cores(*steps):
    return [(dz, dx, k, h) for k in (0, 1) for dz, dx in steps for h in (0, 1)]


FIRST = both_cores((0, 0), (0, 1), (-1, 0), (1, 0))
LATER = ((-1, 1), (1, 1), (2, 1))
SECOND = both_cores((2, 0)) + both_cores(*LATER)[: 2 * len(LATER)]
THIRD = both_cores(*LATER)[2 * len(LATER) :]
ORDER = np.array(FIRST + SECOND + THIRD, np.int32)


def half_order():
    col = lax.axis_index("col").astype(jnp.int32)
    z, xh, k = col // 4, (col // 2) % 2, col % 2
    dz, dx, dk, h = (jnp.asarray(ORDER[:, i]) for i in range(4))
    shard = ((z + dz) % 4) * 4 + (xh ^ dx) * 2 + (k ^ dk)
    return shard * 2 + h


ROWS = pl.BlockSpec(memory_space=pltpu.VMEM)
FAR = pl.BlockSpec(memory_space=pltpu.HBM)
WORDS = pl.BlockSpec(memory_space=pltpu.SMEM)


def near(value):
    return pltpu.with_memory_space_constraint(value, pltpu.VMEM)


def far(value):
    return pltpu.with_memory_space_constraint(value, pltpu.HBM)


def params(mib):
    return pltpu.CompilerParams(vmem_limit_bytes=mib * MIB)


SHARE = 4


def cost(flops, nbytes):
    return pl.CostEstimate(flops=flops // SHARE, transcendentals=0, bytes_accessed=nbytes // SHARE)


def product(left, right):
    return jnp.dot(left, right, preferred_element_type=jnp.float32)


def message_kernel(count_ref, rows_ref, weight_ref, feats_ref, out_ref, stage_ref, sems):
    slot = lax.broadcasted_iota(jnp.int32, (1, SLOTS), 1)
    kept = [
        jnp.where(slot < count_ref[d], weight_ref[d : d + 1, :].astype(jnp.float32), 0.0)
        for d in range(8)
    ]
    kept = jnp.concatenate(kept, axis=0)
    kept_t = jnp.transpose(kept)
    rows_t = jnp.transpose(rows_ref[...])
    node = lax.broadcasted_iota(jnp.int32, (SLOTS, NODES), 1)
    copies = []
    for pair in range(4):
        hot = [
            jnp.where(rows_t[:, d : d + 1] == node, 1.0, 0.0).astype(jnp.bfloat16)
            for d in (2 * pair, 2 * pair + 1)
        ]
        picked = product(jnp.concatenate(hot, axis=0), feats_ref[...])
        for q in range(2):
            d = 2 * pair + q
            block = picked[q * SLOTS : (q + 1) * SLOTS, :] * kept_t[:, d : d + 1]
            stage_ref[d, 0:SLOTS, :] = block.astype(jnp.bfloat16)
            line = jnp.broadcast_to(kept[d : d + 1, :], (PAD, SLOTS)).astype(jnp.bfloat16)
            stage_ref[d, SLOTS : SLOTS + PAD, 0:SLOTS] = line
            stage_ref[d, SLOTS : SLOTS + PAD, SLOTS:] = jnp.zeros(
                (PAD, D - SLOTS), jnp.bfloat16
            )
            copy = pltpu.make_async_copy(stage_ref.at[d], out_ref.at[d], sems.at[d])
            copy.start()
            copies.append(copy)
    for copy in copies:
        copy.wait()


def messages(node_feats, send_rows, send_count, send_weight):
    return pl.pallas_call(
        message_kernel,
        in_specs=[WORDS, ROWS, ROWS, ROWS],
        out_specs=FAR,
        out_shape=pltpu.HBM((8, SLOTS + PAD, D), jnp.bfloat16),
        scratch_shapes=[
            pltpu.VMEM((8, SLOTS + PAD, D), jnp.bfloat16),
            pltpu.SemaphoreType.DMA((8,)),
        ],
        compiler_params=params(8),
        cost_estimate=cost(2 * NODES * NODES * D, 5 * MIB),
        name="messages",
    )(send_count.reshape(8), near(send_rows), near(send_weight), near(node_feats))


LATE = len(THIRD)
EARLY = len(FIRST) + len(SECOND)


def place_kernel(
    order_ref, blocks_ref, tiles_ref, early_ref, late_ref, sums_ref, stage_ref, tally_ref, sems
):
    tally_ref[...] = jnp.zeros_like(tally_ref)
    stage_ref[...] = jnp.zeros_like(stage_ref)
    early_ref[...] = jnp.zeros_like(early_ref)

    def place(p, ref, column):
        first = order_ref[p] * 4
        for t in range(4):
            at = pl.multiple_of(blocks_ref[first + t] * TB, TB)
            tile = tiles_ref[first + t]
            ref[pl.ds(at, TB), column * TB : (column + 1) * TB] = tile
            tally_ref[pl.ds(at, TB), :] += tile.astype(jnp.float32)

    for p in range(LATE):
        place(EARLY + p, stage_ref, p)
    late_copy = pltpu.make_async_copy(stage_ref, late_ref, sems.at[0])
    late_copy.start()
    for p in range(EARLY):
        place(p, early_ref, p)
    sums_copy = pltpu.make_async_copy(tally_ref, sums_ref, sems.at[1])
    sums_copy.start()
    late_copy.wait()
    sums_copy.wait()


def placed_tiles(order, tile_blocks, tile_weights):
    return pl.pallas_call(
        place_kernel,
        in_specs=[WORDS, WORDS, ROWS],
        out_specs=[ROWS, FAR, FAR],
        out_shape=[
            pltpu.VMEM((NODES, EARLY * TB), jnp.bfloat16),
            pltpu.HBM((NODES, LATE * TB), jnp.bfloat16),
            pltpu.HBM((NODES, TB), jnp.float32),
        ],
        scratch_shapes=[
            pltpu.VMEM((NODES, LATE * TB), jnp.bfloat16),
            pltpu.VMEM((NODES, TB), jnp.float32),
            pltpu.SemaphoreType.DMA((2,)),
        ],
        compiler_params=params(6),
        cost_estimate=cost(0, 12 * MIB),
        name="placed_tiles",
    )(order, tile_blocks.reshape(128), near(tile_weights))


def self_kernel(feats_ref, weight_ref, bias_ref, out_ref, stage_ref, sems):
    copies = []
    for step in range(4):
        lanes = slice(step * 256, (step + 1) * 256)
        stage_ref[:, lanes] = product(feats_ref[...], weight_ref[:, lanes]) + bias_ref[:, lanes]
        copy = pltpu.make_async_copy(
            stage_ref.at[:, lanes], out_ref.at[:, lanes], sems.at[step]
        )
        copy.start()
        copies.append(copy)
    for copy in copies:
        copy.wait()


def self_part(node_feats, self_weight, out_bias):
    return pl.pallas_call(
        self_kernel,
        in_specs=[ROWS, ROWS, ROWS],
        out_specs=FAR,
        out_shape=pltpu.HBM((NODES, D), jnp.float32),
        scratch_shapes=[
            pltpu.VMEM((NODES, D), jnp.float32),
            pltpu.SemaphoreType.DMA((4,)),
        ],
        compiler_params=params(8),
        cost_estimate=cost(2 * NODES * D * D, 8 * MIB),
        name="self_part",
    )(near(node_feats), near(self_weight), near(out_bias.reshape(1, D)))


def hub_products(placed, first, parts, carry=None):
    width = sum(part.shape[0] for part in parts)
    operands = [near(placed), *[near(part) for part in parts]]
    if carry is not None:
        operands.append(near(carry))

    def body(placed_ref, *refs):
        if carry is None:
            stage_ref = refs[-1]
        else:
            out_ref, stage_ref, sems = refs[-3:]
        copies = []
        for step in range(4):
            lanes = slice(step * 256, (step + 1) * 256)
            hubs = jnp.concatenate([ref[:, lanes] for ref in refs[: len(parts)]], axis=0)
            total = product(placed_ref[:, first : first + width], hubs)
            if carry is not None:
                total = total + refs[len(parts)][:, lanes]
            stage_ref[:, lanes] = total
            if carry is not None:
                copy = pltpu.make_async_copy(
                    stage_ref.at[:, lanes], out_ref.at[:, lanes], sems.at[step]
                )
                copy.start()
                copies.append(copy)
        for copy in copies:
            copy.wait()

    stage = pltpu.VMEM((NODES, D), jnp.float32)
    return pl.pallas_call(
        body,
        in_specs=[ROWS] * len(operands),
        out_specs=ROWS if carry is None else FAR,
        out_shape=stage if carry is None else pltpu.HBM((NODES, D), jnp.float32),
        scratch_shapes=[] if carry is None else [stage, pltpu.SemaphoreType.DMA((4,))],
        compiler_params=params(8 if carry is None else 10),
        cost_estimate=cost(2 * NODES * width * D, 10 * MIB),
        name="hub_products",
    )(*operands)


def last_part(placed, parts, sums, carry, base, arrive_node, arrived, neigh_weight):
    width = sum(part.shape[0] for part in parts)
    tm = 256
    steps = NODES // tm

    def body(
        got_ref, at_ref, placed_hbm, part_a, part_b, part_c, sums_hbm, carry_hbm, base_hbm,
        weight_hbm, out_ref, placed_ref, hub_ref, sums_ref, carry_ref, base_ref, weight_ref, stage_ref,
        in_sems, out_sems,
    ):
        third = width // 3

        def rows(step):
            return slice(step * tm, (step + 1) * tm)

        loads = [
            (part_a, hub_ref.at[0:third]),
            (part_b, hub_ref.at[third : 2 * third]),
            (part_c, hub_ref.at[2 * third :]),
            (placed_hbm, placed_ref),
            (sums_hbm, sums_ref),
            (carry_hbm.at[rows(0)], carry_ref.at[rows(0)]),
            (weight_hbm, weight_ref),
            (base_hbm.at[rows(0)], base_ref.at[rows(0)]),
        ]
        for step in range(1, steps):
            loads.append((carry_hbm.at[rows(step)], carry_ref.at[rows(step)]))
            loads.append((base_hbm.at[rows(step)], base_ref.at[rows(step)]))
        loads = [
            pltpu.make_async_copy(source, target, in_sems.at[i])
            for i, (source, target) in enumerate(loads)
        ]
        for load in loads:
            load.start()
        copies = []
        for step in range(steps):
            here = rows(step)
            node = lax.broadcasted_iota(jnp.int32, (tm, SLOTS), 0) + step * tm
            weights = jnp.zeros((tm, SLOTS), jnp.float32)
            hot = []
            for o in range(8):
                hit = at_ref[o : o + 1, :] == node
                hot.append(jnp.where(hit, 1.0, 0.0).astype(jnp.bfloat16))
                line = got_ref[o, SLOTS : SLOTS + 1, 0:SLOTS].astype(jnp.float32)
                weights = weights + jnp.where(hit, line, 0.0)
            got = jnp.concatenate([got_ref[o, 0:SLOTS, :] for o in range(8)], axis=0)
            combined = product(jnp.concatenate(hot, axis=1), got)
            if step == 0:
                for load in loads[:6]:
                    load.wait()
            else:
                loads[6 + 2 * step].wait()
            weight_sum = jnp.sum(weights + sums_ref[here, :], axis=-1, keepdims=True)
            combined = combined + product(placed_ref[here, :], hub_ref[...])
            combined = combined + carry_ref[here, :]
            neighbour = (combined * lax.rsqrt(1.0 + weight_sum)).astype(jnp.bfloat16)
            if step == 0:
                loads[6].wait()
            loads[7 + 2 * step].wait()
            preact = base_ref[here, :] + product(neighbour, weight_ref[...])
            hidden = jnp.maximum(preact, 0.0)
            scale = lax.rsqrt(jnp.mean(hidden * hidden, axis=-1, keepdims=True) + 1e-06)
            stage_ref[here, :] = (hidden * scale).astype(jnp.bfloat16)
            copy = pltpu.make_async_copy(
                stage_ref.at[here], out_ref.at[here], out_sems.at[step]
            )
            copy.start()
            copies.append(copy)
        for copy in copies:
            copy.wait()

    return pl.pallas_call(
        body,
        in_specs=[ROWS, ROWS] + [FAR] * 8,
        out_specs=FAR,
        out_shape=pltpu.HBM((NODES, D), jnp.bfloat16),
        scratch_shapes=[
            pltpu.VMEM((NODES, width), jnp.bfloat16),
            pltpu.VMEM((width, D), jnp.bfloat16),
            pltpu.VMEM((NODES, TB), jnp.float32),
            pltpu.VMEM((NODES, D), jnp.float32),
            pltpu.VMEM((NODES, D), jnp.float32),
            pltpu.VMEM((D, D), jnp.bfloat16),
            pltpu.VMEM((NODES, D), jnp.bfloat16),
            pltpu.SemaphoreType.DMA((7 + 2 * steps,)),
            pltpu.SemaphoreType.DMA((steps,)),
        ],
        compiler_params=params(26),
        cost_estimate=cost(2 * NODES * D * (width + 2 * D), 16 * MIB),
        name="last_part",
    )(
        near(arrived), near(arrive_node),
        *[far(value) for value in (placed, *parts, sums, carry, base, neigh_weight)],
    )


def after(value, *others):
    return lax.optimization_barrier((value, *others))[0]


def shards(
    node_feats,
    hub_feats,
    self_weight,
    neigh_weight,
    out_bias,
    tile_weights,
    tile_blocks,
    send_rows,
    send_count,
    send_weight,
    arrive_node,
):
    own = hub_feats
    across = send(own, ACROSS)
    up = send(own, UP)
    down = send(own, DOWN)

    order, node_feats = lax.optimization_barrier((half_order(), node_feats))
    message = messages(node_feats, send_rows, send_count, send_weight)
    own_k, order, message = lax.optimization_barrier((own, order, message))
    arrived = lax.all_to_all(message, "row", split_axis=0, concat_axis=0, tiled=True)
    own_c = send(own_k, CORE)
    placed, placed_late, sums = placed_tiles(order, tile_blocks, tile_weights)

    up, down, across, own_c, placed = lax.optimization_barrier(
        (up, down, across, own_c, placed)
    )
    two_low = send(up[:TB], UP)
    two_high = send(down[TB:], DOWN)
    across_c = send(across, CORE)
    up_c = send(up, CORE)
    down_c = send(down, CORE)
    base = self_part(node_feats, self_weight, out_bias)

    two_low, two_high, across, across_c, up_c, down_c, base = lax.optimization_barrier(
        (two_low, two_high, across, across_c, up_c, down_c, base)
    )
    two = jnp.concatenate([two_low, two_high], 0)
    up_x = send(across, UP)
    down_x = send(across, DOWN)
    two_x = send(two, ACROSS)
    two_c = send(two, CORE)
    carry = hub_products(
        placed, 0, [own, across, up, down, own_c, across_c, up_c, down_c]
    )

    up_x, down_x, two_x, two_c, carry = lax.optimization_barrier(
        (up_x, down_x, two_x, two_c, carry)
    )
    late = [send(part, CORE) for part in (up_x, down_x, two_x)]
    carry = hub_products(placed, 2048, [two, two_c, up_x, down_x, two_x], carry)
    return last_part(
        placed_late, late, sums, carry, base, arrive_node, arrived, neigh_weight
    )


def solution(mesh):
    placed = (
        P(("row", "col"), None),
        P("col", None),
        P(),
        P(),
        P(),
        P(("row", "col"), None, None),
        P(("row", "col"), None),
        P("row", "col"),
        P("row", "col"),
        P("row", "col"),
        P("row", "col"),
    )
    return jax.shard_map(
        shards, mesh=mesh, in_specs=placed, out_specs=P(("row", "col"), None), check_vma=False
    )
```

time: 334 us -> 77.2 us (0.23)
  the two profiles are of different devices: /device:TPU:2 before, /device:TPU:1 now
where the time goes in v2:
time: 77.2 us; the launch traced here: 76.8 us
  Pallas kernels  35 us (45%)
  starting transfers between devices  23.1 us (30%)
  waiting for transfers between devices  11.8 us (15%)
  local copies, waits for them, and re-layouts  5.89 us (8%)
    ppermute x16, starting transfers between devices, send(): return lax.ppermute(value, MESH_AXES, pairs)  18.9 us
    pallas_call x1, Pallas kernels, last_part(): pl.pallas_call(body, in_specs=[ROWS, ROWS] + [FAR] * 8, out_specs=FAR, ou...  11.8 us
    pallas_call x2, Pallas kernels, hub_products(): pl.pallas_call(body, in_specs=[ROWS] * len(operands), out_specs=ROWS if c...  11.8 us
    ppermute x16, waiting for transfers between devices, send(): return lax.ppermute(value, MESH_AXES, pairs)  11.8 us
    unnamed x21, local copies, waits for them, and re-layouts  5.83 us
    all_to_all x1, starting transfers between devices, shards(): lax.all_to_all(message, 'row', split_axis=0, concat_axis=0, tiled=True)  4.19 us
    pallas_call x1, Pallas kernels, messages(): pl.pallas_call(message_kernel, in_specs=[WORDS, ROWS, ROWS, ROWS], out_sp...  3.99 us
    pallas_call x1, Pallas kernels, self_part(): pl.pallas_call(self_kernel, in_specs=[ROWS, ROWS, ROWS], out_specs=FAR, o...  3.87 us
  transfers between devices with their start and end apart: 17, of which 5 were waited for; matrix products, arithmetic and copies ran while one was open for 1% of the time, Pallas kernels for 30%

profile of v2, /device:TPU:1, one launch (start us, length us, event | category | flops | bytes accessed | tf_op | source)
XLA Modules:
  0.0 76.8 jit_solution(2055887670890040777)
XLA Ops:
  0.0 4.6 %collective-permute-start.1 = (bf16[256,1024]{1,0:T(8,128)(2,1)}, bf16[256,1024]{1,0:T(8,128)(2,1)S(1)}, u32[]{:S(2)}, u32[]{:S(2)}) collective-permute-start(bf16[256,1024]{1,0:T(8,128)(2,1)} %refs_0_.1), channel_id=1, source_target_pairs={{0,12},{1,13},{2,14},{3,15},{4,0},{5,1},{6,2},{7,3},{8,4},{9,5},{1... | collective-permute-start | bytes 1572872 | tf_op jit(solution)/shard_map/ppermute | solution.py:38
  4.6 2.5 %collective-permute-start.2 = (bf16[256,1024]{1,0:T(8,128)(2,1)}, bf16[256,1024]{1,0:T(8,128)(2,1)}, u32[]{:S(2)}, u32[]{:S(2)}) collective-permute-start(bf16[256,1024]{1,0:T(8,128)(2,1)} %refs_0_.1), channel_id=1, source_target_pairs={{0,18},{1,19},{2,16},{3,17},{4,22},{5,23},{6,20},{7,21},{8,26},{9,... | collective-permute-start | bytes 1572872 | tf_op jit(solution)/shard_map/ppermute | solution.py:38
  7.1 0.7 multiply_add_fusion.order_ref
  7.8 1.6 %copy-done = bf16[1024,1024]{1,0:T(8,128)(2,1)S(1)} copy-done((bf16[1024,1024]{1,0:T(8,128)(2,1)S(1)}, bf16[1024,1024]{1,0:T(8,128)(2,1)}, u32[]{:S(2)}) %copy-start) | copy-done | bytes 2097176
  9.4 0.7 copy-done.4
  10.1 0.7 copy-done.7
  11.4 4.0 %messages.1 = bf16[8,136,1024]{2,1,0:T(8,128)(2,1)} custom-call(s32[8]{0:T(128)S(1)} %bitcast.4, s32[8,128]{1,0:T(8,128)S(1)} %copy-done.4, bf16[8,128]{1,0:T(8,128)(2,1)S(1)} %copy-done.7, bf16[1024,1024]{1,0:T(8,128)(2,1)S(1)} %copy-done), custom_call_target="tpu_custom_call" | custom-call | flops 536870912 | bytes 1310720 | tf_op jit(solution)/shard_map/messages/pallas_call | solution.py:122
  15.4 1.3 %collective-permute-start.3 = (bf16[256,1024]{1,0:T(8,128)(2,1)}, bf16[256,1024]{1,0:T(8,128)(2,1)}, u32[]{:S(2)}, u32[]{:S(2)}) collective-permute-start(bf16[256,1024]{1,0:T(8,128)(2,1)} %refs_0_.1), channel_id=1, source_target_pairs={{0,1},{1,0},{2,3},{3,2},{4,5},{5,4},{6,7},{7,6},{8,9},{9,8},{10,11... | collective-permute-start | bytes 1572872 | tf_op jit(solution)/shard_map/ppermute | solution.py:38
  16.7 4.2 %all-to-all-start = ((bf16[8,136,1024]{2,1,0:T(8,128)(2,1)}), bf16[8,136,1024]{2,1,0:T(8,128)(2,1)S(1)}, u32[]{:S(2)}, u32[]{:S(2)}) async-start(bf16[8,136,1024]{2,1,0:T(8,128)(2,1)} %messages.1), calls=%async_computation | async-start | bytes 4456448 | tf_op jit(solution)/shard_map/all_to_all | solution.py:381
  20.9 2.2 %copy-done.2 = bf16[128,128,128]{2,1,0:T(8,128)(2,1)S(1)} copy-done((bf16[128,128,128]{2,1,0:T(8,128)(2,1)S(1)}, bf16[128,128,128]{2,1,0:T(8,128)(2,1)}, u32[]{:S(2)}) %copy-start.2) | copy-done | bytes 4194328
  23.1 3.5 %placed_tiles.1 = (bf16[1024,3328]{1,0:T(8,128)(2,1)S(1)}, bf16[1024,768]{1,0:T(8,128)(2,1)}, f32[1024,128]{1,0:T(8,128)}) custom-call(s32[32]{0:T(128)S(1)} %multiply_add_fusion.order_ref, s32[128]{0:T(128)S(1)} %bitcast.5, bf16[128,128,128]{2,1,0:T(8,128)(2,1)S(1)} %copy-done.2), custom_call_target="tpu_custom_call" | custom-call | bytes 3145728 | tf_op jit(solution)/shard_map/placed_tiles/pallas_call | solution.py:169
  27.6 3.0 %collective-permute-start.5 = (bf16[128,1024]{1,0:T(8,128)(2,1)S(1)}, bf16[128,1024]{1,0:T(8,128)(2,1)S(1)}, u32[]{:S(2)}, u32[]{:S(2)}) collective-permute-start(bf16[128,1024]{1,0:T(8,128)(2,1)S(1)} %slice.7), channel_id=1, source_target_pairs={{0,12},{1,13},{2,14},{3,15},{4,0},{5,1},{6,2},{7,3},{8,4},{9,5},{1... | collective-permute-start | bytes 786440 | tf_op jit(solution)/shard_map/ppermute | solution.py:38
  30.6 3.9 %self_part.1.base_hbm = f32[1024,1024]{1,0:T(8,128)} custom-call(bf16[1024,1024]{1,0:T(8,128)(2,1)S(1)} %copy-done.1, bf16[1024,1024]{1,0:T(8,128)(2,1)S(1)} %copy-done.3, f32[1,1024]{1,0:T(1,128)S(1)} %bitcast.3), custom_call_target="tpu_custom_call" | custom-call | flops 536870912 | bytes 2097152 | tf_op jit(solution)/shard_map/self_part/pallas_call | solution.py:204
  34.5 1.6 %collective-permute-done.5 = bf16[128,1024]{1,0:T(8,128)(2,1)S(1)} collective-permute-done((bf16[128,1024]{1,0:T(8,128)(2,1)S(1)}, bf16[128,1024]{1,0:T(8,128)(2,1)S(1)}, u32[]{:S(2)}, u32[]{:S(2)}) %collective-permute-start.5) | collective-permute-done | bytes 262176 | tf_op jit(solution)/shard_map/ppermute | solution.py:38
  36.1 3.1 %collective-permute-done.4 = bf16[128,1024]{1,0:T(8,128)(2,1)S(1)} collective-permute-done((bf16[128,1024]{1,0:T(8,128)(2,1)S(1)}, bf16[128,1024]{1,0:T(8,128)(2,1)S(1)}, u32[]{:S(2)}, u32[]{:S(2)}) %collective-permute-start.4) | collective-permute-done | bytes 262176 | tf_op jit(solution)/shard_map/ppermute | solution.py:38
  39.3 1.4 %collective-permute-start.12 = (bf16[256,1024]{1,0:T(8,128)(2,1)S(1)}, bf16[256,1024]{1,0:T(8,128)(2,1)S(1)}, u32[]{:S(2)}, u32[]{:S(2)}) collective-permute-start(bf16[256,1024]{1,0:T(8,128)(2,1)S(1)} %constant_dynamic-update-slice_fusion.refs_0_), channel_id=1, source_target_pairs={{0,1},{1,0},{2,3},{3,2},{4,5},{5,4},{6,7},{7,6},{8,9},{9,8},{10,11... | collective-permute-start | bytes 1572872 | tf_op jit(solution)/shard_map/ppermute | solution.py:38
  40.7 1.7 %collective-permute-start.11 = (bf16[256,1024]{1,0:T(8,128)(2,1)S(1)}, bf16[256,1024]{1,0:T(8,128)(2,1)}, u32[]{:S(2)}, u32[]{:S(2)}) collective-permute-start(bf16[256,1024]{1,0:T(8,128)(2,1)S(1)} %constant_dynamic-update-slice_fusion.refs_0_), channel_id=1, source_target_pairs={{0,18},{1,19},{2,16},{3,17},{4,22},{5,23},{6,20},{7,21},{8,26},{9,... | collective-permute-start | bytes 1572872 | tf_op jit(solution)/shard_map/ppermute | solution.py:38
  42.4 1.5 %collective-permute-start.9 = (bf16[256,1024]{1,0:T(8,128)(2,1)}, bf16[256,1024]{1,0:T(8,128)(2,1)}, u32[]{:S(2)}, u32[]{:S(2)}) collective-permute-start(bf16[256,1024]{1,0:T(8,128)(2,1)} %collective-permute-done.2.refs_1_), channel_id=1, source_target_pairs={{0,4},{1,5},{2,6},{3,7},{4,8},{5,9},{6,10},{7,11},{8,12},{9,13},{1... | collective-permute-start | bytes 1572872 | tf_op jit(solution)/shard_map/ppermute | solution.py:38
  43.8 5.9 %hub_products.2.refs_5_ = f32[1024,1024]{1,0:T(8,128)S(1)} custom-call(bf16[1024,3328]{1,0:T(8,128)(2,1)S(1)} %get-tuple-element.43.placed_ref, bf16[256,1024]{1,0:T(8,128)(2,1)} %refs_0_.1, bf16[256,1024]{1,0:T(8,128)(2,1)} %collective-permute-done.2.refs_1_, bf16[256,1024]{1,0:T(8,128)(2,1)S(1)} %collective-permute-done.refs_2_, ...), custom_call_target="tpu_custom_call" | custom-call | flops 1073741824 | bytes 2621440 | tf_op jit(solution)/shard_map/hub_products/pallas_call | solution.py:248
  49.7 5.8 %collective-permute-done.11.refs_4_ = bf16[256,1024]{1,0:T(8,128)(2,1)} collective-permute-done((bf16[256,1024]{1,0:T(8,128)(2,1)S(1)}, bf16[256,1024]{1,0:T(8,128)(2,1)}, u32[]{:S(2)}, u32[]{:S(2)}) %collective-permute-start.11) | collective-permute-done | bytes 524320 | tf_op jit(solution)/shard_map/ppermute | solution.py:38
  55.8 0.9 %collective-permute-done.9.refs_2_ = bf16[256,1024]{1,0:T(8,128)(2,1)} collective-permute-done((bf16[256,1024]{1,0:T(8,128)(2,1)}, bf16[256,1024]{1,0:T(8,128)(2,1)}, u32[]{:S(2)}, u32[]{:S(2)}) %collective-permute-start.9) | collective-permute-done | bytes 524320 | tf_op jit(solution)/shard_map/ppermute | solution.py:38
  56.7 1.5 %collective-permute-start.13 = (bf16[256,1024]{1,0:T(8,128)(2,1)}, bf16[256,1024]{1,0:T(8,128)(2,1)}, u32[]{:S(2)}, u32[]{:S(2)}) collective-permute-start(bf16[256,1024]{1,0:T(8,128)(2,1)} %collective-permute-done.9.refs_2_), channel_id=1, source_target_pairs={{0,1},{1,0},{2,3},{3,2},{4,5},{5,4},{6,7},{7,6},{8,9},{9,8},{10,11... | collective-permute-start | bytes 1572872 | tf_op jit(solution)/shard_map/ppermute | solution.py:38
  58.8 6.0 %hub_products.3.carry_hbm = f32[1024,1024]{1,0:T(8,128)} custom-call(bf16[1024,3328]{1,0:T(8,128)(2,1)S(1)} %get-tuple-element.43.placed_ref, bf16[256,1024]{1,0:T(8,128)(2,1)S(1)} %constant_dynamic-update-slice_fusion.refs_0_, bf16[256,1024]{1,0:T(8,128)(2,1)S(1)} %collective-permute-done.12.refs_1_, bf16[256,1024]{1,0:T(8,128)(2,1)} %collective-permute-done.9.refs_2_, ...), custom_call_target="tpu_custom_call" | custom-call | flops 671088640 | bytes 2621440 | tf_op jit(solution)/shard_map/hub_products/pallas_call | solution.py:248
  64.8 11.8 %last_part.1 = bf16[1024,1024]{1,0:T(8,128)(2,1)} custom-call(bf16[8,136,1024]{2,1,0:T(8,128)(2,1)S(1)} %all-to-all-done.got_ref, s32[8,128]{1,0:T(8,128)S(1)} %copy-done.6, bf16[1024,768]{1,0:T(8,128)(2,1)} %get-tuple-element.34.placed_hbm, bf16[256,1024]{1,0:T(8,128)(2,1)} %collective-permute-done.13.part_a, ...), custom_call_target="tpu_custom_call" | custom-call | flops 1476395008 | bytes 4194304 | tf_op jit(solution)/shard_map/last_part/pallas_call | solution.py:331
  (41 shorter events, 2.6 us)
Async XLA Ops:
  0.0 26.6 %collective-permute-start.1 = (bf16[256,1024]{1,0:T(8,128)(2,1)}, bf16[256,1024]{1,0:T(8,128)(2,1)S(1)}, u32[]{:S(2)}, u32[]{:S(2)}) collective-permute-start(bf16[256,1024]{1,0:T(8,128)(2,1)} %refs_0_.1), channel_id=1, source_target_pairs={{0,12},{1,13},{2,14},{3,15},{4,0},{5,1},{6,2},{7,3},{8,4},{9,5},{1... | collective-permute-start | bytes 1572872 | tf_op jit(solution)/shard_map/ppermute | solution.py:38
  4.6 22.0 %collective-permute-start = (bf16[256,1024]{1,0:T(8,128)(2,1)}, bf16[256,1024]{1,0:T(8,128)(2,1)S(1)}, u32[]{:S(2)}, u32[]{:S(2)}) collective-permute-start(bf16[256,1024]{1,0:T(8,128)(2,1)} %refs_0_.1), channel_id=1, source_target_pairs={{0,4},{1,5},{2,6},{3,7},{4,8},{5,9},{6,10},{7,11},{8,12},{9,13},{1... | collective-permute-start | bytes 1572872 | tf_op jit(solution)/shard_map/ppermute | solution.py:38
  4.6 22.0 %collective-permute-start.2 = (bf16[256,1024]{1,0:T(8,128)(2,1)}, bf16[256,1024]{1,0:T(8,128)(2,1)}, u32[]{:S(2)}, u32[]{:S(2)}) collective-permute-start(bf16[256,1024]{1,0:T(8,128)(2,1)} %refs_0_.1), channel_id=1, source_target_pairs={{0,18},{1,19},{2,16},{3,17},{4,22},{5,23},{6,20},{7,21},{8,26},{9,... | collective-permute-start | bytes 1572872 | tf_op jit(solution)/shard_map/ppermute | solution.py:38
  7.8 1.6 %copy-start = (bf16[1024,1024]{1,0:T(8,128)(2,1)S(1)}, bf16[1024,1024]{1,0:T(8,128)(2,1)}, u32[]{:S(2)}) copy-start(bf16[1024,1024]{1,0:T(8,128)(2,1)} %feats_ref.1) | copy-start | bytes 6291460
  15.4 5.5 %copy-start.9 = (s32[1,128]{1,0:T(1,128)S(1)}, s32[1,128]{1,0:T(1,128)}, u32[]{:S(2)}) copy-start(s32[1,128]{1,0:T(1,128)} %param.21) | copy-start | bytes 1540
  15.4 11.2 %collective-permute-start.3 = (bf16[256,1024]{1,0:T(8,128)(2,1)}, bf16[256,1024]{1,0:T(8,128)(2,1)}, u32[]{:S(2)}, u32[]{:S(2)}) collective-permute-start(bf16[256,1024]{1,0:T(8,128)(2,1)} %refs_0_.1), channel_id=1, source_target_pairs={{0,1},{1,0},{2,3},{3,2},{4,5},{5,4},{6,7},{7,6},{8,9},{9,8},{10,11... | collective-permute-start | bytes 1572872 | tf_op jit(solution)/shard_map/ppermute | solution.py:38
  16.7 48.0 %all-to-all-start = ((bf16[8,136,1024]{2,1,0:T(8,128)(2,1)}), bf16[8,136,1024]{2,1,0:T(8,128)(2,1)S(1)}, u32[]{:S(2)}, u32[]{:S(2)}) async-start(bf16[8,136,1024]{2,1,0:T(8,128)(2,1)} %messages.1), calls=%async_computation | async-start | bytes 4456448 | tf_op jit(solution)/shard_map/all_to_all | solution.py:381
  20.9 2.2 %copy-start.2 = (bf16[128,128,128]{2,1,0:T(8,128)(2,1)S(1)}, bf16[128,128,128]{2,1,0:T(8,128)(2,1)}, u32[]{:S(2)}) copy-start(bf16[128,128,128]{2,1,0:T(8,128)(2,1)} %tiles_ref.1) | copy-start | bytes 12582916
  23.1 7.5 %copy-start.1 = (bf16[1024,1024]{1,0:T(8,128)(2,1)S(1)}, bf16[1024,1024]{1,0:T(8,128)(2,1)}, u32[]{:S(2)}) copy-start(bf16[1024,1024]{1,0:T(8,128)(2,1)} %feats_ref.1) | copy-start | bytes 6291460
  23.1 7.5 %copy-start.3 = (bf16[1024,1024]{1,0:T(8,128)(2,1)S(1)}, bf16[1024,1024]{1,0:T(8,128)(2,1)}, u32[]{:S(2)}) copy-start(bf16[1024,1024]{1,0:T(8,128)(2,1)} %weight_ref.3) | copy-start | bytes 6291460
  23.1 7.5 %copy-start.5 = (f32[1024]{0:T(1024)S(1)}, f32[1024]{0:T(1024)}, u32[]{:S(2)}) copy-start(f32[1024]{0:T(1024)} %param.19) | copy-start | bytes 12292
  26.7 12.6 %collective-permute-start.6 = (bf16[256,1024]{1,0:T(8,128)(2,1)}, bf16[256,1024]{1,0:T(8,128)(2,1)S(1)}, u32[]{:S(2)}, u32[]{:S(2)}) collective-permute-start(bf16[256,1024]{1,0:T(8,128)(2,1)} %collective-permute-done.2.refs_1_), channel_id=1, source_target_pairs={{0,1},{1,0},{2,3},{3,2},{4,5},{5,4},{6,7},{7,6},{8,9},{9,8},{10,11... | collective-permute-start | bytes 1572872 | tf_op jit(solution)/shard_map/ppermute | solution.py:38
  27.0 12.2 %collective-permute-start.7 = (bf16[256,1024]{1,0:T(8,128)(2,1)S(1)}, bf16[256,1024]{1,0:T(8,128)(2,1)S(1)}, u32[]{:S(2)}, u32[]{:S(2)}) collective-permute-start(bf16[256,1024]{1,0:T(8,128)(2,1)S(1)} %collective-permute-done.refs_2_), channel_id=1, source_target_pairs={{0,1},{1,0},{2,3},{3,2},{4,5},{5,4},{6,7},{7,6},{8,9},{9,8},{10,11... | collective-permute-start | bytes 1572872 | tf_op jit(solution)/shard_map/ppermute | solution.py:38
  27.2 12.0 %collective-permute-start.8 = (bf16[256,1024]{1,0:T(8,128)(2,1)S(1)}, bf16[256,1024]{1,0:T(8,128)(2,1)S(1)}, u32[]{:S(2)}, u32[]{:S(2)}) collective-permute-start(bf16[256,1024]{1,0:T(8,128)(2,1)S(1)} %collective-permute-done.1.refs_3_), channel_id=1, source_target_pairs={{0,1},{1,0},{2,3},{3,2},{4,5},{5,4},{6,7},{7,6},{8,9},{9,8},{10,11... | collective-permute-start | bytes 1572872 | tf_op jit(solution)/shard_map/ppermute | solution.py:38
  27.6 8.5 %collective-permute-start.5 = (bf16[128,1024]{1,0:T(8,128)(2,1)S(1)}, bf16[128,1024]{1,0:T(8,128)(2,1)S(1)}, u32[]{:S(2)}, u32[]{:S(2)}) collective-permute-start(bf16[128,1024]{1,0:T(8,128)(2,1)S(1)} %slice.7), channel_id=1, source_target_pairs={{0,12},{1,13},{2,14},{3,15},{4,0},{5,1},{6,2},{7,3},{8,4},{9,5},{1... | collective-permute-start | bytes 786440 | tf_op jit(solution)/shard_map/ppermute | solution.py:38
  30.6 8.6 %collective-permute-start.4 = (bf16[128,1024]{1,0:T(8,128)(2,1)S(1)}, bf16[128,1024]{1,0:T(8,128)(2,1)S(1)}, u32[]{:S(2)}, u32[]{:S(2)}) collective-permute-start(bf16[128,1024]{1,0:T(8,128)(2,1)S(1)} %slice.6), channel_id=1, source_target_pairs={{0,4},{1,5},{2,6},{3,7},{4,8},{5,9},{6,10},{7,11},{8,12},{9,13},{1... | collective-permute-start | bytes 786440 | tf_op jit(solution)/shard_map/ppermute | solution.py:38
  39.3 10.4 %collective-permute-start.12 = (bf16[256,1024]{1,0:T(8,128)(2,1)S(1)}, bf16[256,1024]{1,0:T(8,128)(2,1)S(1)}, u32[]{:S(2)}, u32[]{:S(2)}) collective-permute-start(bf16[256,1024]{1,0:T(8,128)(2,1)S(1)} %constant_dynamic-update-slice_fusion.refs_0_), channel_id=1, source_target_pairs={{0,1},{1,0},{2,3},{3,2},{4,5},{5,4},{6,7},{7,6},{8,9},{9,8},{10,11... | collective-permute-start | bytes 1572872 | tf_op jit(solution)/shard_map/ppermute | solution.py:38
  40.7 14.8 %collective-permute-start.11 = (bf16[256,1024]{1,0:T(8,128)(2,1)S(1)}, bf16[256,1024]{1,0:T(8,128)(2,1)}, u32[]{:S(2)}, u32[]{:S(2)}) collective-permute-start(bf16[256,1024]{1,0:T(8,128)(2,1)S(1)} %constant_dynamic-update-slice_fusion.refs_0_), channel_id=1, source_target_pairs={{0,18},{1,19},{2,16},{3,17},{4,22},{5,23},{6,20},{7,21},{8,26},{9,... | collective-permute-start | bytes 1572872 | tf_op jit(solution)/shard_map/ppermute | solution.py:38
  42.4 13.5 %collective-permute-start.10 = (bf16[256,1024]{1,0:T(8,128)(2,1)}, bf16[256,1024]{1,0:T(8,128)(2,1)}, u32[]{:S(2)}, u32[]{:S(2)}) collective-permute-start(bf16[256,1024]{1,0:T(8,128)(2,1)} %collective-permute-done.2.refs_1_), channel_id=1, source_target_pairs={{0,12},{1,13},{2,14},{3,15},{4,0},{5,1},{6,2},{7,3},{8,4},{9,5},{1... | collective-permute-start | bytes 1572872 | tf_op jit(solution)/shard_map/ppermute | solution.py:38
  42.4 14.4 %collective-permute-start.9 = (bf16[256,1024]{1,0:T(8,128)(2,1)}, bf16[256,1024]{1,0:T(8,128)(2,1)}, u32[]{:S(2)}, u32[]{:S(2)}) collective-permute-start(bf16[256,1024]{1,0:T(8,128)(2,1)} %collective-permute-done.2.refs_1_), channel_id=1, source_target_pairs={{0,4},{1,5},{2,6},{3,7},{4,8},{5,9},{6,10},{7,11},{8,12},{9,13},{1... | collective-permute-start | bytes 1572872 | tf_op jit(solution)/shard_map/ppermute | solution.py:38
  49.7 15.1 %copy-start.6 = (s32[8,128]{1,0:T(8,128)S(1)}, s32[8,128]{1,0:T(8,128)}, u32[]{:S(2)}) copy-start(s32[8,128]{1,0:T(8,128)} %at_ref.1) | copy-start | bytes 12292
  56.7 8.0 %collective-permute-start.13 = (bf16[256,1024]{1,0:T(8,128)(2,1)}, bf16[256,1024]{1,0:T(8,128)(2,1)}, u32[]{:S(2)}, u32[]{:S(2)}) collective-permute-start(bf16[256,1024]{1,0:T(8,128)(2,1)} %collective-permute-done.9.refs_2_), channel_id=1, source_target_pairs={{0,1},{1,0},{2,3},{3,2},{4,5},{5,4},{6,7},{7,6},{8,9},{9,8},{10,11... | collective-permute-start | bytes 1572872 | tf_op jit(solution)/shard_map/ppermute | solution.py:38
  58.3 6.5 %collective-permute-start.14 = (bf16[256,1024]{1,0:T(8,128)(2,1)}, bf16[256,1024]{1,0:T(8,128)(2,1)}, u32[]{:S(2)}, u32[]{:S(2)}) collective-permute-start(bf16[256,1024]{1,0:T(8,128)(2,1)} %collective-permute-done.10.refs_3_), channel_id=1, source_target_pairs={{0,1},{1,0},{2,3},{3,2},{4,5},{5,4},{6,7},{7,6},{8,9},{9,8},{10,11... | collective-permute-start | bytes 1572872 | tf_op jit(solution)/shard_map/ppermute | solution.py:38
  58.3 6.5 %collective-permute-start.15 = (bf16[256,1024]{1,0:T(8,128)(2,1)}, bf16[256,1024]{1,0:T(8,128)(2,1)}, u32[]{:S(2)}, u32[]{:S(2)}) collective-permute-start(bf16[256,1024]{1,0:T(8,128)(2,1)} %collective-permute-done.11.refs_4_), channel_id=1, source_target_pairs={{0,1},{1,0},{2,3},{3,2},{4,5},{5,4},{6,7},{7,6},{8,9},{9,8},{10,11... | collective-permute-start | bytes 1572872 | tf_op jit(solution)/shard_map/ppermute | solution.py:38
  (3 other events, 2.0 us)

commit v3 on v2

v3 whole, which is shorter than its diff:
```python
import numpy as np
import jax
import jax.numpy as jnp
from jax import lax
from jax.experimental import pallas as pl
from jax.experimental.pallas import tpu as pltpu
from jax.sharding import PartitionSpec as P

MESH_AXES = ("row", "col")
D = 1024
TB = 128
NODES = 1024
SLOTS = 128
PAD = 8
MIB = 1 << 20


def flat(y, xl, z, xh, k):
    return (y * 2 + xl) * 16 + z * 4 + xh * 2 + k


def pairs_of(move):
    pairs = []
    for source in range(128):
        row, col = divmod(source, 16)
        place = (row // 2, row % 2, col // 4, (col // 2) % 2, col % 2)
        pairs.append((source, flat(*move(*place))))
    return pairs


ACROSS = pairs_of(lambda y, xl, z, xh, k: (y, 1 - xl, z, 1 - xh, k))
UP = pairs_of(lambda y, xl, z, xh, k: (y, xl, (z + 1) % 4, xh, k))
DOWN = pairs_of(lambda y, xl, z, xh, k: (y, xl, (z - 1) % 4, xh, k))
CORE = pairs_of(lambda y, xl, z, xh, k: (y, xl, z, xh, 1 - k))


def send(value, pairs):
    return lax.ppermute(value, MESH_AXES, pairs)


def both_cores(*steps):
    return [(dz, dx, k, h) for k in (0, 1) for dz, dx in steps for h in (0, 1)]


FIRST = both_cores((0, 0), (0, 1), (-1, 0), (1, 0))
LATER = ((-1, 1), (1, 1), (2, 1))
SECOND = both_cores((2, 0)) + both_cores(*LATER)[: 2 * len(LATER)]
THIRD = both_cores(*LATER)[2 * len(LATER) :]
ORDER = np.array(FIRST + SECOND + THIRD, np.int32)


def half_index(col, entry):
    dz, dx, dk, half = ORDER[entry].tolist()
    z = (col // 4 + dz) % 4
    xh = (col // 2 + dx) % 2
    k = (col + dk) % 2
    return (z * 4 + xh * 2 + k) * 2 + half


ROWS = pl.BlockSpec(memory_space=pltpu.VMEM)
FAR = pl.BlockSpec(memory_space=pltpu.HBM)
WORDS = pl.BlockSpec(memory_space=pltpu.SMEM)


def near(value):
    return pltpu.with_memory_space_constraint(value, pltpu.VMEM)


def far(value):
    return pltpu.with_memory_space_constraint(value, pltpu.HBM)


def params(mib):
    return pltpu.CompilerParams(vmem_limit_bytes=mib * MIB)


def cost(flops, nbytes):
    return pl.CostEstimate(flops=2 * flops, transcendentals=0, bytes_accessed=2 * nbytes)


def product(left, right):
    return jnp.dot(left, right, preferred_element_type=jnp.float32)


def message_kernel(
    count_ref, rows_hbm, weight_hbm, feats_hbm, out_ref, rows_ref, weight_ref, feats_ref,
    stage_ref, load_sems, sems,
):
    sources = (rows_hbm, weight_hbm, feats_hbm)
    targets = (rows_ref, weight_ref, feats_ref)
    loads = [
        pltpu.make_async_copy(source, target, load_sems.at[i])
        for i, (source, target) in enumerate(zip(sources, targets))
    ]
    for load in loads:
        load.start()
    loads[0].wait()
    loads[1].wait()
    slot = lax.broadcasted_iota(jnp.int32, (1, SLOTS), 1)
    kept = [
        jnp.where(slot < count_ref[d], weight_ref[d : d + 1, :].astype(jnp.float32), 0.0)
        for d in range(8)
    ]
    kept = jnp.concatenate(kept, axis=0)
    kept_t = jnp.transpose(kept)
    rows_t = jnp.transpose(rows_ref[...])
    node = lax.broadcasted_iota(jnp.int32, (SLOTS, NODES), 1)
    copies = []
    for pair in range(4):
        hot = [
            jnp.where(rows_t[:, d : d + 1] == node, 1.0, 0.0).astype(jnp.bfloat16)
            for d in (2 * pair, 2 * pair + 1)
        ]
        if pair == 0:
            loads[2].wait()
        picked = product(jnp.concatenate(hot, axis=0), feats_ref[...])
        for q in range(2):
            d = 2 * pair + q
            block = picked[q * SLOTS : (q + 1) * SLOTS, :] * kept_t[:, d : d + 1]
            stage_ref[d, 0:SLOTS, :] = block.astype(jnp.bfloat16)
            line = jnp.broadcast_to(kept[d : d + 1, :], (PAD, SLOTS)).astype(jnp.bfloat16)
            stage_ref[d, SLOTS : SLOTS + PAD, 0:SLOTS] = line
            stage_ref[d, SLOTS : SLOTS + PAD, SLOTS:] = jnp.zeros(
                (PAD, D - SLOTS), jnp.bfloat16
            )
            copy = pltpu.make_async_copy(stage_ref.at[d], out_ref.at[d], sems.at[d])
            copy.start()
            copies.append(copy)
    for copy in copies:
        copy.wait()


def messages(node_feats, send_rows, send_count, send_weight):
    return pl.pallas_call(
        message_kernel,
        in_specs=[WORDS, FAR, FAR, FAR],
        out_specs=FAR,
        out_shape=pltpu.HBM((8, SLOTS + PAD, D), jnp.bfloat16),
        scratch_shapes=[
            pltpu.VMEM((8, SLOTS), jnp.int32),
            pltpu.VMEM((8, SLOTS), jnp.bfloat16),
            pltpu.VMEM((NODES, D), jnp.bfloat16),
            pltpu.VMEM((8, SLOTS + PAD, D), jnp.bfloat16),
            pltpu.SemaphoreType.DMA((3,)),
            pltpu.SemaphoreType.DMA((8,)),
        ],
        compiler_params=params(12),
        cost_estimate=cost(2 * NODES * NODES * D, 5 * MIB),
        name="messages",
    )(send_count.reshape(8), far(send_rows), far(send_weight), far(node_feats))


FIRST_HALVES = len(FIRST)
LATER_HALVES = len(SECOND) + len(THIRD)


def place_kernel(
    blocks_ref, tiles_ref, early_ref, later_ref, sums_ref, stage_ref, tally_ref, sems
):
    col = lax.axis_index("col")
    tally_ref[...] = jnp.zeros_like(tally_ref)
    stage_ref[...] = jnp.zeros_like(stage_ref)
    early_ref[...] = jnp.zeros_like(early_ref)

    def place(p, ref, column):
        first = half_index(col, p) * 4
        for t in range(4):
            at = pl.multiple_of(blocks_ref[first + t] * TB, TB)
            tile = tiles_ref[first + t]
            ref[pl.ds(at, TB), column * TB : (column + 1) * TB] = tile
            tally_ref[pl.ds(at, TB), :] += tile.astype(jnp.float32)

    for p in range(LATER_HALVES):
        place(FIRST_HALVES + p, stage_ref, p)
    copies = [pltpu.make_async_copy(stage_ref, later_ref, sems.at[0])]
    copies[0].start()
    for p in range(FIRST_HALVES):
        place(p, early_ref, p)
    copies.append(pltpu.make_async_copy(tally_ref, sums_ref, sems.at[1]))
    copies[1].start()
    for copy in copies:
        copy.wait()


def placed_tiles(tile_blocks, tile_weights):
    return pl.pallas_call(
        place_kernel,
        in_specs=[WORDS, ROWS],
        out_specs=[ROWS, FAR, FAR],
        out_shape=[
            pltpu.VMEM((NODES, FIRST_HALVES * TB), jnp.bfloat16),
            pltpu.HBM((NODES, LATER_HALVES * TB), jnp.bfloat16),
            pltpu.HBM((NODES, TB), jnp.float32),
        ],
        scratch_shapes=[
            pltpu.VMEM((NODES, LATER_HALVES * TB), jnp.bfloat16),
            pltpu.VMEM((NODES, TB), jnp.float32),
            pltpu.SemaphoreType.DMA((2,)),
        ],
        compiler_params=params(8),
        cost_estimate=cost(0, 12 * MIB),
        name="placed_tiles",
    )(tile_blocks.reshape(128), near(tile_weights))


def bias_kernel(bias_ref, out_ref):
    out_ref[...] = jnp.broadcast_to(bias_ref[...], (8, D))


def bias_rows(out_bias):
    return pl.pallas_call(
        bias_kernel,
        in_specs=[ROWS],
        out_specs=ROWS,
        out_shape=pltpu.VMEM((8, D), jnp.float32),
        compiler_params=params(2),
        cost_estimate=cost(1000, 1000),
        name="bias_rows",
    )(near(out_bias.reshape(1, D)))


def self_kernel(feats_ref, weight_ref, bias_ref, out_ref, stage_ref, sems):
    copies = []
    for step in range(4):
        lanes = slice(step * 256, (step + 1) * 256)
        stage_ref[:, lanes] = (
            product(feats_ref[...], weight_ref[:, lanes]) + bias_ref[0:1, lanes]
        )
        copy = pltpu.make_async_copy(
            stage_ref.at[:, lanes], out_ref.at[:, lanes], sems.at[step]
        )
        copy.start()
        copies.append(copy)
    for copy in copies:
        copy.wait()


def self_part(node_feats, self_weight, bias):
    return pl.pallas_call(
        self_kernel,
        in_specs=[ROWS, ROWS, ROWS],
        out_specs=FAR,
        out_shape=pltpu.HBM((NODES, D), jnp.float32),
        scratch_shapes=[
            pltpu.VMEM((NODES, D), jnp.float32),
            pltpu.SemaphoreType.DMA((4,)),
        ],
        compiler_params=params(8),
        cost_estimate=cost(1000, 1000),
        name="self_part",
    )(near(node_feats), near(self_weight), near(bias))


def hub_products(placed, parts):
    width = sum(part.shape[0] for part in parts)

    def body(placed_ref, *refs):
        out_ref, stage_ref, sems = refs[-3:]
        copies = []
        for step in range(4):
            lanes = slice(step * 256, (step + 1) * 256)
            hubs = jnp.concatenate([ref[:, lanes] for ref in refs[: len(parts)]], axis=0)
            stage_ref[:, lanes] = product(placed_ref[:, :width], hubs)
            copy = pltpu.make_async_copy(
                stage_ref.at[:, lanes], out_ref.at[:, lanes], sems.at[step]
            )
            copy.start()
            copies.append(copy)
        for copy in copies:
            copy.wait()

    return pl.pallas_call(
        body,
        in_specs=[ROWS] * (1 + len(parts)),
        out_specs=FAR,
        out_shape=pltpu.HBM((NODES, D), jnp.float32),
        scratch_shapes=[pltpu.VMEM((NODES, D), jnp.float32), pltpu.SemaphoreType.DMA((4,))],
        compiler_params=params(10),
        cost_estimate=cost(2 * NODES * width * D, 10 * MIB),
        name="hub_products",
    )(near(placed), *[near(part) for part in parts])


def tail_part(sums, carry, arrive_node, arrived):
    def body(
        at_ref, got_ref, sums_hbm, carry_hbm, out_ref, scale_ref, hot_ref, sums_ref,
        carry_ref, sems,
    ):
        pairs = [(sums_hbm, sums_ref)]
        for step in range(4):
            lanes = slice(step * 256, (step + 1) * 256)
            pairs.append((carry_hbm.at[:, lanes], carry_ref.at[:, lanes]))
        loads = [
            pltpu.make_async_copy(source, target, sems.at[i])
            for i, (source, target) in enumerate(pairs)
        ]
        for load in loads:
            load.start()
        loads[0].wait()
        for step in range(4):
            rows = slice(step * 256, (step + 1) * 256)
            node = lax.broadcasted_iota(jnp.int32, (256, SLOTS), 0) + step * 256
            weights = sums_ref[rows, :]
            for o in range(8):
                hit = at_ref[o : o + 1, :] == node
                hot_ref[rows, o * SLOTS : (o + 1) * SLOTS] = jnp.where(hit, 1.0, 0.0).astype(
                    jnp.bfloat16
                )
                line = got_ref[o, SLOTS : SLOTS + 1, 0:SLOTS].astype(jnp.float32)
                weights = weights + jnp.where(hit, line, 0.0)
            weight_sum = jnp.sum(weights, axis=-1, keepdims=True)
            scale_ref[rows, :] = jnp.broadcast_to(lax.rsqrt(1.0 + weight_sum), (256, TB))
        for load in loads[1:]:
            load.wait()
        for step in range(4):
            lanes = slice(step * 256, (step + 1) * 256)
            got = jnp.concatenate([got_ref[o, 0:SLOTS, lanes] for o in range(8)], axis=0)
            out_ref[:, lanes] = product(hot_ref[...], got) + carry_ref[:, lanes]

    return pl.pallas_call(
        body,
        in_specs=[ROWS] * 2 + [FAR] * 2,
        out_specs=[ROWS, ROWS],
        out_shape=[pltpu.VMEM((NODES, D), jnp.float32), pltpu.VMEM((NODES, TB), jnp.float32)],
        scratch_shapes=[
            pltpu.VMEM((NODES, 8 * SLOTS), jnp.bfloat16),
            pltpu.VMEM((NODES, TB), jnp.float32),
            pltpu.VMEM((NODES, D), jnp.float32),
            pltpu.SemaphoreType.DMA((5,)),
        ],
        compiler_params=params(14),
        cost_estimate=cost(2 * NODES * NODES * D, 10 * MIB),
        name="tail_part",
    )(near(arrive_node), near(arrived), far(sums), far(carry))


def middle_part(placed, parts, carry):
    width = sum(part.shape[0] for part in parts)

    def body(placed_ref, carry_ref, *refs):
        for step in range(4):
            lanes = slice(step * 256, (step + 1) * 256)
            hubs = jnp.concatenate([ref[:, lanes] for ref in refs[: len(parts)]], axis=0)
            refs[-1][:, lanes] = product(placed_ref[:, 0:width], hubs) + carry_ref[:, lanes]

    return pl.pallas_call(
        body,
        in_specs=[ROWS] * (2 + len(parts)),
        out_specs=ROWS,
        out_shape=pltpu.VMEM((NODES, D), jnp.float32),
        compiler_params=params(8),
        cost_estimate=cost(2 * NODES * width * D, 10 * MIB),
        name="middle_part",
    )(near(placed), near(carry), *[near(part) for part in parts])


def last_part(placed, parts, scale, carry, base, neigh_weight):
    tm = 256

    width = sum(part.shape[0] for part in parts)
    first = placed.shape[1] - width

    def body(scale_ref, carry_ref, base_ref, weight_ref, placed_ref, *refs):
        out_ref, stage_ref, sems = refs[len(parts) :]
        copies = []
        for step in range(NODES // tm):
            rows = slice(step * tm, (step + 1) * tm)
            hubs = jnp.concatenate([ref[...] for ref in refs[: len(parts)]], axis=0)
            combined = carry_ref[rows, :] + product(placed_ref[rows, first:], hubs)
            neighbour = (combined * scale_ref[rows, 0:1]).astype(jnp.bfloat16)
            preact = base_ref[rows, :] + product(neighbour, weight_ref[...])
            hidden = jnp.maximum(preact, 0.0)
            norm = lax.rsqrt(jnp.mean(hidden * hidden, axis=-1, keepdims=True) + 1e-06)
            stage_ref[rows, :] = (hidden * norm).astype(jnp.bfloat16)
            copy = pltpu.make_async_copy(
                stage_ref.at[rows], out_ref.at[rows], sems.at[step]
            )
            copy.start()
            copies.append(copy)
        for copy in copies:
            copy.wait()

    return pl.pallas_call(
        body,
        in_specs=[ROWS] * (5 + len(parts)),
        out_specs=FAR,
        out_shape=pltpu.HBM((NODES, D), jnp.bfloat16),
        scratch_shapes=[
            pltpu.VMEM((NODES, D), jnp.bfloat16),
            pltpu.SemaphoreType.DMA((NODES // tm,)),
        ],
        compiler_params=params(12),
        cost_estimate=cost(2 * NODES * D * (width + D), 16 * MIB),
        name="last_part",
    )(
        *[near(value) for value in (scale, carry, base, neigh_weight, placed, *parts)],
    )


def shards(
    node_feats,
    hub_feats,
    self_weight,
    neigh_weight,
    out_bias,
    tile_weights,
    tile_blocks,
    send_rows,
    send_count,
    send_weight,
    arrive_node,
):
    own = hub_feats
    across = send(own, ACROSS)
    up = send(own, UP)
    down = send(own, DOWN)

    message = messages(node_feats, send_rows, send_count, send_weight)

    out_bias, own_k, message = lax.optimization_barrier((out_bias, own, message))
    arrived = lax.all_to_all(message, "row", split_axis=0, concat_axis=0, tiled=True)
    own_c = send(own_k, CORE)
    bias = bias_rows(out_bias)
    up, down, across, own_c, bias = lax.optimization_barrier((up, down, across, own_c, bias))
    two_low = send(up[:TB], UP)
    two_high = send(down[TB:], DOWN)
    across_c = send(across, CORE)
    up_c = send(up, CORE)
    down_c = send(down, CORE)
    placed, placed_later, sums = placed_tiles(tile_blocks, tile_weights)

    base = self_part(node_feats, self_weight, bias)

    two_low, two_high, across, across_c, up_c, down_c, placed, base = (
        lax.optimization_barrier(
            (two_low, two_high, across, across_c, up_c, down_c, placed, base)
        )
    )
    two = jnp.concatenate([two_low, two_high], 0)
    up_x = send(across, UP)
    down_x = send(across, DOWN)
    two_x = send(two, ACROSS)
    two_c = send(two, CORE)
    carry = hub_products(
        placed, [own, across, up, down, own_c, across_c, up_c, down_c]
    )

    carry, scale = tail_part(sums, carry, arrive_node, arrived)

    up_x, down_x, two_x, two_c, carry = lax.optimization_barrier(
        (up_x, down_x, two_x, two_c, carry)
    )
    late = [send(part, CORE) for part in (up_x, down_x, two_x)]
    carry = middle_part(placed_later, [two, two_c, up_x, down_x, two_x], carry)
    return last_part(placed_later, late, scale, carry, base, neigh_weight)


def solution(mesh):
    placed = (
        P(("row", "col"), None),
        P("col", None),
        P(),
        P(),
        P(),
        P(("row", "col"), None, None),
        P(("row", "col"), None),
        P("row", "col"),
        P("row", "col"),
        P("row", "col"),
        P("row", "col"),
    )
    return jax.shard_map(
        shards, mesh=mesh, in_specs=placed, out_specs=P(("row", "col"), None), check_vma=False
    )
```

time: 77.2 us -> 67.9 us (0.88)
  waiting for transfers between devices: 11.8 us -> 2.14 us
  starting transfers between devices: 23.1 us -> 25.1 us
  local copies, waits for them, and re-layouts: 5.89 us -> 4.33 us
    ppermute x16, waiting for transfers between devices: 11.8 us -> 2.13 us  [send(): return lax.ppermute(value, MESH_AXES, pairs)]
    unnamed x21, local copies, waits for them, and re-layouts: 5.83 us -> 3.58 us
    ppermute x16, starting transfers between devices: 18.9 us -> 21 us  [send(): return lax.ppermute(value, MESH_AXES, pairs)]
    pallas_call x5 -> x7, Pallas kernels: 31.1 us -> 31.7 us  [the longest x1 7.38 us: hub_products(): pl.pallas_call(body, in_specs=[ROWS] * (1 + len(parts)), out_specs=FAR, o...]
  transfers between devices with their start and end apart: 17 -> 17, of which waited for: 5 -> 1; matrix products, arithmetic and copies ran while one was open for 1% -> 2% of each run, Pallas kernels for 30% -> 45%
where the time goes in v3:
time: 67.9 us; the launch traced here: 67.6 us
  Pallas kernels  35.6 us (52%)
  starting transfers between devices  25.1 us (37%)
  local copies, waits for them, and re-layouts  4.33 us (6%)
  waiting for transfers between devices  2.14 us (3%)
    ppermute x16, starting transfers between devices, send(): return lax.ppermute(value, MESH_AXES, pairs)  21 us
    pallas_call x1, Pallas kernels, hub_products(): pl.pallas_call(body, in_specs=[ROWS] * (1 + len(parts)), out_specs=FAR, o...  7.38 us
    pallas_call x1, Pallas kernels, messages(): pl.pallas_call(message_kernel, in_specs=[WORDS, FAR, FAR, FAR], out_specs...  5.47 us
    pallas_call x1, Pallas kernels, last_part(): pl.pallas_call(body, in_specs=[ROWS] * (5 + len(parts)), out_specs=FAR, o...  5.03 us
    pallas_call x1, Pallas kernels, tail_part(): pl.pallas_call(body, in_specs=[ROWS] * 2 + [FAR] * 2, out_specs=[ROWS, RO...  4.88 us
    pallas_call x1, Pallas kernels, middle_part(): pl.pallas_call(body, in_specs=[ROWS] * (2 + len(parts)), out_specs=ROWS,...  4.69 us
    pallas_call x1, Pallas kernels, placed_tiles(): pl.pallas_call(place_kernel, in_specs=[WORDS, ROWS], out_specs=[ROWS, FAR...  4.25 us
    all_to_all x1, starting transfers between devices, shards(): lax.all_to_all(message, 'row', split_axis=0, concat_axis=0, tiled=True)  4.18 us
  transfers between devices with their start and end apart: 17, of which 1 were waited for; matrix products, arithmetic and copies ran while one was open for 2% of the time, Pallas kernels for 45%

profile of v3, /device:TPU:1, one launch (start us, length us, event | category | flops | bytes accessed | tf_op | source)
XLA Modules:
  0.0 67.6 jit_solution(5359346882850732608)
XLA Ops:
  0.0 4.6 %collective-permute-start.1 = (bf16[256,1024]{1,0:T(8,128)(2,1)}, bf16[256,1024]{1,0:T(8,128)(2,1)S(1)}, u32[]{:S(2)}, u32[]{:S(2)}) collective-permute-start(bf16[256,1024]{1,0:T(8,128)(2,1)} %refs_0_.1), channel_id=1, source_target_pairs={{0,12},{1,13},{2,14},{3,15},{4,0},{5,1},{6,2},{7,3},{8,4},{9,5},{1... | collective-permute-start | bytes 1572872 | tf_op jit(solution)/shard_map/ppermute | solution.py:38
  4.6 2.5 %collective-permute-start.2 = (bf16[256,1024]{1,0:T(8,128)(2,1)}, bf16[256,1024]{1,0:T(8,128)(2,1)}, u32[]{:S(2)}, u32[]{:S(2)}) collective-permute-start(bf16[256,1024]{1,0:T(8,128)(2,1)} %refs_0_.1), channel_id=1, source_target_pairs={{0,18},{1,19},{2,16},{3,17},{4,22},{5,23},{6,20},{7,21},{8,26},{9,... | collective-permute-start | bytes 1572872 | tf_op jit(solution)/shard_map/ppermute | solution.py:38
  7.1 0.7 copy-done.9
  7.7 5.5 %messages.1 = bf16[8,136,1024]{2,1,0:T(8,128)(2,1)} custom-call(s32[8]{0:T(128)S(1)} %bitcast.5, s32[8,128]{1,0:T(8,128)} %rows_hbm.1, bf16[8,128]{1,0:T(8,128)(2,1)} %weight_hbm.1, bf16[1024,1024]{1,0:T(8,128)(2,1)} %feats_ref.1), custom_call_target="tpu_custom_call" | custom-call | flops 4294967296 | bytes 10485760 | tf_op jit(solution)/shard_map/messages/pallas_call | solution.py:134
  13.2 1.3 %collective-permute-start.3 = (bf16[256,1024]{1,0:T(8,128)(2,1)}, bf16[256,1024]{1,0:T(8,128)(2,1)}, u32[]{:S(2)}, u32[]{:S(2)}) collective-permute-start(bf16[256,1024]{1,0:T(8,128)(2,1)} %refs_0_.1), channel_id=1, source_target_pairs={{0,1},{1,0},{2,3},{3,2},{4,5},{5,4},{6,7},{7,6},{8,9},{9,8},{10,11... | collective-permute-start | bytes 1572872 | tf_op jit(solution)/shard_map/ppermute | solution.py:38
  14.5 4.2 %all-to-all-start = ((bf16[8,136,1024]{2,1,0:T(8,128)(2,1)}), bf16[8,136,1024]{2,1,0:T(8,128)(2,1)S(1)}, u32[]{:S(2)}, u32[]{:S(2)}) async-start(bf16[8,136,1024]{2,1,0:T(8,128)(2,1)} %messages.1), calls=%async_computation | async-start | bytes 4456448 | tf_op jit(solution)/shard_map/all_to_all | solution.py:421
  18.8 1.7 %collective-permute-start.6 = (bf16[256,1024]{1,0:T(8,128)(2,1)}, bf16[256,1024]{1,0:T(8,128)(2,1)S(1)}, u32[]{:S(2)}, u32[]{:S(2)}) collective-permute-start(bf16[256,1024]{1,0:T(8,128)(2,1)} %collective-permute-done.2.refs_1_), channel_id=1, source_target_pairs={{0,1},{1,0},{2,3},{3,2},{4,5},{5,4},{6,7},{7,6},{8,9},{9,8},{10,11... | collective-permute-start | bytes 1572872 | tf_op jit(solution)/shard_map/ppermute | solution.py:38
  20.5 0.5 collective-permute-start.8
  21.0 2.7 %collective-permute-start.5 = (bf16[128,1024]{1,0:T(8,128)(2,1)S(1)}, bf16[128,1024]{1,0:T(8,128)(2,1)S(1)}, u32[]{:S(2)}, u32[]{:S(2)}) collective-permute-start(bf16[128,1024]{1,0:T(8,128)(2,1)S(1)} %slice.7), channel_id=1, source_target_pairs={{0,12},{1,13},{2,14},{3,15},{4,0},{5,1},{6,2},{7,3},{8,4},{9,5},{1... | collective-permute-start | bytes 786440 | tf_op jit(solution)/shard_map/ppermute | solution.py:38
  23.8 2.2 %copy-done = bf16[128,128,128]{2,1,0:T(8,128)(2,1)S(1)} copy-done((bf16[128,128,128]{2,1,0:T(8,128)(2,1)S(1)}, bf16[128,128,128]{2,1,0:T(8,128)(2,1)}, u32[]{:S(2)}) %copy-start) | copy-done | bytes 4194328
  26.0 4.2 %placed_tiles.1 = (bf16[1024,2048]{1,0:T(8,128)(2,1)S(1)}, bf16[1024,2048]{1,0:T(8,128)(2,1)}, f32[1024,128]{1,0:T(8,128)}) custom-call(s32[128]{0:T(128)S(1)} %bitcast.4, bf16[128,128,128]{2,1,0:T(8,128)(2,1)S(1)} %copy-done), custom_call_target="tpu_custom_call" | custom-call | bytes 25165824 | tf_op jit(solution)/shard_map/placed_tiles/pallas_call | solution.py:186
  30.2 3.9 %self_part.1.base_ref = f32[1024,1024]{1,0:T(8,128)} custom-call(bf16[1024,1024]{1,0:T(8,128)(2,1)S(1)} %copy-done.2, bf16[1024,1024]{1,0:T(8,128)(2,1)S(1)} %copy-done.3, f32[8,1024]{1,0:T(8,128)S(1)} %bias_rows.1.bias_ref), custom_call_target="tpu_custom_call" | custom-call | flops 2000 | bytes 2000 | tf_op jit(solution)/shard_map/self_part/pallas_call | solution.py:239
  34.2 0.7 %constant_dynamic-update-slice_fusion.1 = bf16[256,1024]{1,0:T(8,128)(2,1)} fusion(bf16[128,1024]{1,0:T(8,128)(2,1)S(1)} %collective-permute-done.4), kind=kLoop, calls=%fused_computation.1 | loop fusion | bytes 524288
  34.9 0.7 %constant_dynamic-update-slice_fusion.refs_0_ = bf16[256,1024]{1,0:T(8,128)(2,1)} fusion(bf16[256,1024]{1,0:T(8,128)(2,1)} %constant_dynamic-update-slice_fusion.1, bf16[128,1024]{1,0:T(8,128)(2,1)S(1)} %collective-permute-done.5), kind=kLoop, calls=%fused_computation | loop fusion | bytes 524288 | tf_op jit(solution)/shard_map/concatenate | solution.py:439
  35.6 0.3 collective-permute-start.12
  35.9 2.5 %collective-permute-start.11 = (bf16[256,1024]{1,0:T(8,128)(2,1)}, bf16[256,1024]{1,0:T(8,128)(2,1)}, u32[]{:S(2)}, u32[]{:S(2)}) collective-permute-start(bf16[256,1024]{1,0:T(8,128)(2,1)} %constant_dynamic-update-slice_fusion.refs_0_), channel_id=1, source_target_pairs={{0,18},{1,19},{2,16},{3,17},{4,22},{5,23},{6,20},{7,21},{8,26},{9,... | collective-permute-start | bytes 1572872 | tf_op jit(solution)/shard_map/ppermute | solution.py:38
  38.3 3.0 %collective-permute-start.10 = (bf16[256,1024]{1,0:T(8,128)(2,1)}, bf16[256,1024]{1,0:T(8,128)(2,1)}, u32[]{:S(2)}, u32[]{:S(2)}) collective-permute-start(bf16[256,1024]{1,0:T(8,128)(2,1)} %collective-permute-done.2.refs_1_), channel_id=1, source_target_pairs={{0,12},{1,13},{2,14},{3,15},{4,0},{5,1},{6,2},{7,3},{8,4},{9,5},{1... | collective-permute-start | bytes 1572872 | tf_op jit(solution)/shard_map/ppermute | solution.py:38
  41.3 7.4 %hub_products.1.carry_hbm = f32[1024,1024]{1,0:T(8,128)} custom-call(bf16[1024,2048]{1,0:T(8,128)(2,1)S(1)} %get-tuple-element.40.placed_ref, bf16[256,1024]{1,0:T(8,128)(2,1)} %refs_0_.1, bf16[256,1024]{1,0:T(8,128)(2,1)} %collective-permute-done.2.refs_1_, bf16[256,1024]{1,0:T(8,128)(2,1)S(1)} %collective-permute-done.refs_2_, ...), custom_call_target="tpu_custom_call" | custom-call | flops 8589934592 | bytes 20971520 | tf_op jit(solution)/shard_map/hub_products/pallas_call | solution.py:272
  48.7 4.9 %tail_part.1 = (f32[1024,1024]{1,0:T(8,128)S(1)}, f32[1024,128]{1,0:T(8,128)S(1)}) custom-call(s32[8,128]{1,0:T(8,128)S(1)} %copy-done.8, bf16[8,136,1024]{2,1,0:T(8,128)(2,1)S(1)} %all-to-all-done.got_ref, f32[1024,128]{1,0:T(8,128)} %get-tuple-element.32.sums_hbm, f32[1024,1024]{1,0:T(8,128)} %hub_products.1.carry_hbm), custom_call_target="tpu_custom_call" | custom-call | flops 4294967296 | bytes 20971520 | tf_op jit(solution)/shard_map/tail_part/pallas_call | solution.py:320
  53.7 2.1 %collective-permute-done.9.refs_2_ = bf16[256,1024]{1,0:T(8,128)(2,1)} collective-permute-done((bf16[256,1024]{1,0:T(8,128)(2,1)}, bf16[256,1024]{1,0:T(8,128)(2,1)}, u32[]{:S(2)}, u32[]{:S(2)}) %collective-permute-start.9) | collective-permute-done | bytes 524320 | tf_op jit(solution)/shard_map/ppermute | solution.py:38
  55.7 1.4 %collective-permute-start.13 = (bf16[256,1024]{1,0:T(8,128)(2,1)}, bf16[256,1024]{1,0:T(8,128)(2,1)S(1)}, u32[]{:S(2)}, u32[]{:S(2)}) collective-permute-start(bf16[256,1024]{1,0:T(8,128)(2,1)} %collective-permute-done.9.refs_2_), channel_id=1, source_target_pairs={{0,1},{1,0},{2,3},{3,2},{4,5},{5,4},{6,7},{7,6},{8,9},{9,8},{10,11... | collective-permute-start | bytes 1572872 | tf_op jit(solution)/shard_map/ppermute | solution.py:38
  57.2 0.5 collective-permute-start.15
  57.7 4.7 %middle_part.1.carry_ref = f32[1024,1024]{1,0:T(8,128)S(1)} custom-call(bf16[1024,2048]{1,0:T(8,128)(2,1)S(1)} %copy-done.6, f32[1024,1024]{1,0:T(8,128)S(1)} %get-tuple-element.51.carry_ref, bf16[256,1024]{1,0:T(8,128)(2,1)} %constant_dynamic-update-slice_fusion.refs_0_, bf16[256,1024]{1,0:T(8,128)(2,1)} %collective-permute-done.12.refs_1_, ...), custom_call_target="tpu_custom_call" | custom-call | flops 5368709120 | bytes 20971520 | tf_op jit(solution)/shard_map/middle_part/pallas_call | solution.py:346
  62.4 5.0 %last_part.1 = bf16[1024,1024]{1,0:T(8,128)(2,1)} custom-call(f32[1024,128]{1,0:T(8,128)S(1)} %get-tuple-element.46.scale_ref, f32[1024,1024]{1,0:T(8,128)S(1)} %middle_part.1.carry_ref, f32[1024,1024]{1,0:T(8,128)S(1)} %copy-done.1, bf16[1024,1024]{1,0:T(8,128)(2,1)S(1)} %copy-done.7, bf16[1024,2048]{1,0:T(8,128)(2,1)S(1)} %copy-done.6, ...), custom_call_target="tpu_custom_call" | custom-call | flops 7516192768 | bytes 33554432 | tf_op jit(solution)/shard_map/last_part/pallas_call | solution.py:383
  (42 shorter events, 0.2 us)
Async XLA Ops:
  0.0 18.7 %collective-permute-start.1 = (bf16[256,1024]{1,0:T(8,128)(2,1)}, bf16[256,1024]{1,0:T(8,128)(2,1)S(1)}, u32[]{:S(2)}, u32[]{:S(2)}) collective-permute-start(bf16[256,1024]{1,0:T(8,128)(2,1)} %refs_0_.1), channel_id=1, source_target_pairs={{0,12},{1,13},{2,14},{3,15},{4,0},{5,1},{6,2},{7,3},{8,4},{9,5},{1... | collective-permute-start | bytes 1572872 | tf_op jit(solution)/shard_map/ppermute | solution.py:38
  4.6 14.2 %collective-permute-start = (bf16[256,1024]{1,0:T(8,128)(2,1)}, bf16[256,1024]{1,0:T(8,128)(2,1)S(1)}, u32[]{:S(2)}, u32[]{:S(2)}) collective-permute-start(bf16[256,1024]{1,0:T(8,128)(2,1)} %refs_0_.1), channel_id=1, source_target_pairs={{0,4},{1,5},{2,6},{3,7},{4,8},{5,9},{6,10},{7,11},{8,12},{9,13},{1... | collective-permute-start | bytes 1572872 | tf_op jit(solution)/shard_map/ppermute | solution.py:38
  4.6 14.2 %collective-permute-start.2 = (bf16[256,1024]{1,0:T(8,128)(2,1)}, bf16[256,1024]{1,0:T(8,128)(2,1)}, u32[]{:S(2)}, u32[]{:S(2)}) collective-permute-start(bf16[256,1024]{1,0:T(8,128)(2,1)} %refs_0_.1), channel_id=1, source_target_pairs={{0,18},{1,19},{2,16},{3,17},{4,22},{5,23},{6,20},{7,21},{8,26},{9,... | collective-permute-start | bytes 1572872 | tf_op jit(solution)/shard_map/ppermute | solution.py:38
  13.2 5.5 %copy-start.4 = (f32[1024]{0:T(1024)S(1)}, f32[1024]{0:T(1024)}, u32[]{:S(2)}) copy-start(f32[1024]{0:T(1024)} %param.15) | copy-start | bytes 12292
  13.2 10.5 %copy-start.5 = (s32[1,128]{1,0:T(1,128)S(1)}, s32[1,128]{1,0:T(1,128)}, u32[]{:S(2)}) copy-start(s32[1,128]{1,0:T(1,128)} %param.17) | copy-start | bytes 1540
  13.2 5.5 %collective-permute-start.3 = (bf16[256,1024]{1,0:T(8,128)(2,1)}, bf16[256,1024]{1,0:T(8,128)(2,1)}, u32[]{:S(2)}, u32[]{:S(2)}) collective-permute-start(bf16[256,1024]{1,0:T(8,128)(2,1)} %refs_0_.1), channel_id=1, source_target_pairs={{0,1},{1,0},{2,3},{3,2},{4,5},{5,4},{6,7},{7,6},{8,9},{9,8},{10,11... | collective-permute-start | bytes 1572872 | tf_op jit(solution)/shard_map/ppermute | solution.py:38
  14.5 34.2 %all-to-all-start = ((bf16[8,136,1024]{2,1,0:T(8,128)(2,1)}), bf16[8,136,1024]{2,1,0:T(8,128)(2,1)S(1)}, u32[]{:S(2)}, u32[]{:S(2)}) async-start(bf16[8,136,1024]{2,1,0:T(8,128)(2,1)} %messages.1), calls=%async_computation | async-start | bytes 4456448 | tf_op jit(solution)/shard_map/all_to_all | solution.py:421
  18.8 15.3 %collective-permute-start.6 = (bf16[256,1024]{1,0:T(8,128)(2,1)}, bf16[256,1024]{1,0:T(8,128)(2,1)S(1)}, u32[]{:S(2)}, u32[]{:S(2)}) collective-permute-start(bf16[256,1024]{1,0:T(8,128)(2,1)} %collective-permute-done.2.refs_1_), channel_id=1, source_target_pairs={{0,1},{1,0},{2,3},{3,2},{4,5},{5,4},{6,7},{7,6},{8,9},{9,8},{10,11... | collective-permute-start | bytes 1572872 | tf_op jit(solution)/shard_map/ppermute | solution.py:38
  20.5 13.7 %collective-permute-start.7 = (bf16[256,1024]{1,0:T(8,128)(2,1)S(1)}, bf16[256,1024]{1,0:T(8,128)(2,1)S(1)}, u32[]{:S(2)}, u32[]{:S(2)}) collective-permute-start(bf16[256,1024]{1,0:T(8,128)(2,1)S(1)} %collective-permute-done.refs_2_), channel_id=1, source_target_pairs={{0,1},{1,0},{2,3},{3,2},{4,5},{5,4},{6,7},{7,6},{8,9},{9,8},{10,11... | collective-permute-start | bytes 1572872 | tf_op jit(solution)/shard_map/ppermute | solution.py:38
  20.5 13.7 %collective-permute-start.8 = (bf16[256,1024]{1,0:T(8,128)(2,1)S(1)}, bf16[256,1024]{1,0:T(8,128)(2,1)S(1)}, u32[]{:S(2)}, u32[]{:S(2)}) collective-permute-start(bf16[256,1024]{1,0:T(8,128)(2,1)S(1)} %collective-permute-done.1.refs_3_), channel_id=1, source_target_pairs={{0,1},{1,0},{2,3},{3,2},{4,5},{5,4},{6,7},{7,6},{8,9},{9,8},{10,11... | collective-permute-start | bytes 1572872 | tf_op jit(solution)/shard_map/ppermute | solution.py:38
  21.0 13.1 %collective-permute-start.5 = (bf16[128,1024]{1,0:T(8,128)(2,1)S(1)}, bf16[128,1024]{1,0:T(8,128)(2,1)S(1)}, u32[]{:S(2)}, u32[]{:S(2)}) collective-permute-start(bf16[128,1024]{1,0:T(8,128)(2,1)S(1)} %slice.7), channel_id=1, source_target_pairs={{0,12},{1,13},{2,14},{3,15},{4,0},{5,1},{6,2},{7,3},{8,4},{9,5},{1... | collective-permute-start | bytes 786440 | tf_op jit(solution)/shard_map/ppermute | solution.py:38
  23.8 10.4 %collective-permute-start.4 = (bf16[128,1024]{1,0:T(8,128)(2,1)S(1)}, bf16[128,1024]{1,0:T(8,128)(2,1)S(1)}, u32[]{:S(2)}, u32[]{:S(2)}) collective-permute-start(bf16[128,1024]{1,0:T(8,128)(2,1)S(1)} %slice.6), channel_id=1, source_target_pairs={{0,4},{1,5},{2,6},{3,7},{4,8},{5,9},{6,10},{7,11},{8,12},{9,13},{1... | collective-permute-start | bytes 786440 | tf_op jit(solution)/shard_map/ppermute | solution.py:38
  26.0 4.3 %copy-start.3 = (bf16[1024,1024]{1,0:T(8,128)(2,1)S(1)}, bf16[1024,1024]{1,0:T(8,128)(2,1)}, u32[]{:S(2)}) copy-start(bf16[1024,1024]{1,0:T(8,128)(2,1)} %weight_ref.2) | copy-start | bytes 6291460
  35.6 13.1 %copy-start.8 = (s32[8,128]{1,0:T(8,128)S(1)}, s32[8,128]{1,0:T(8,128)}, u32[]{:S(2)}) copy-start(s32[8,128]{1,0:T(8,128)} %at_ref.1) | copy-start | bytes 12292
  35.6 18.0 %collective-permute-start.12 = (bf16[256,1024]{1,0:T(8,128)(2,1)}, bf16[256,1024]{1,0:T(8,128)(2,1)}, u32[]{:S(2)}, u32[]{:S(2)}) collective-permute-start(bf16[256,1024]{1,0:T(8,128)(2,1)} %constant_dynamic-update-slice_fusion.refs_0_), channel_id=1, source_target_pairs={{0,1},{1,0},{2,3},{3,2},{4,5},{5,4},{6,7},{7,6},{8,9},{9,8},{10,11... | collective-permute-start | bytes 1572872 | tf_op jit(solution)/shard_map/ppermute | solution.py:38
  35.9 17.8 %collective-permute-start.11 = (bf16[256,1024]{1,0:T(8,128)(2,1)}, bf16[256,1024]{1,0:T(8,128)(2,1)}, u32[]{:S(2)}, u32[]{:S(2)}) collective-permute-start(bf16[256,1024]{1,0:T(8,128)(2,1)} %constant_dynamic-update-slice_fusion.refs_0_), channel_id=1, source_target_pairs={{0,18},{1,19},{2,16},{3,17},{4,22},{5,23},{6,20},{7,21},{8,26},{9,... | collective-permute-start | bytes 1572872 | tf_op jit(solution)/shard_map/ppermute | solution.py:38
  38.3 15.3 %collective-permute-start.10 = (bf16[256,1024]{1,0:T(8,128)(2,1)}, bf16[256,1024]{1,0:T(8,128)(2,1)}, u32[]{:S(2)}, u32[]{:S(2)}) collective-permute-start(bf16[256,1024]{1,0:T(8,128)(2,1)} %collective-permute-done.2.refs_1_), channel_id=1, source_target_pairs={{0,12},{1,13},{2,14},{3,15},{4,0},{5,1},{6,2},{7,3},{8,4},{9,5},{1... | collective-permute-start | bytes 1572872 | tf_op jit(solution)/shard_map/ppermute | solution.py:38
  41.3 14.4 %collective-permute-start.9 = (bf16[256,1024]{1,0:T(8,128)(2,1)}, bf16[256,1024]{1,0:T(8,128)(2,1)}, u32[]{:S(2)}, u32[]{:S(2)}) collective-permute-start(bf16[256,1024]{1,0:T(8,128)(2,1)} %collective-permute-done.2.refs_1_), channel_id=1, source_target_pairs={{0,4},{1,5},{2,6},{3,7},{4,8},{5,9},{6,10},{7,11},{8,12},{9,13},{1... | collective-permute-start | bytes 1572872 | tf_op jit(solution)/shard_map/ppermute | solution.py:38
  48.7 9.0 %copy-start.6 = (bf16[1024,2048]{1,0:T(8,128)(2,1)S(1)}, bf16[1024,2048]{1,0:T(8,128)(2,1)}, u32[]{:S(2)}) copy-start(bf16[1024,2048]{1,0:T(8,128)(2,1)} %get-tuple-element.47.placed_ref) | copy-start | bytes 12582916
  55.7 6.6 %collective-permute-start.13 = (bf16[256,1024]{1,0:T(8,128)(2,1)}, bf16[256,1024]{1,0:T(8,128)(2,1)S(1)}, u32[]{:S(2)}, u32[]{:S(2)}) collective-permute-start(bf16[256,1024]{1,0:T(8,128)(2,1)} %collective-permute-done.9.refs_2_), channel_id=1, source_target_pairs={{0,1},{1,0},{2,3},{3,2},{4,5},{5,4},{6,7},{7,6},{8,9},{9,8},{10,11... | collective-permute-start | bytes 1572872 | tf_op jit(solution)/shard_map/ppermute | solution.py:38
  57.2 5.2 %collective-permute-start.14 = (bf16[256,1024]{1,0:T(8,128)(2,1)}, bf16[256,1024]{1,0:T(8,128)(2,1)S(1)}, u32[]{:S(2)}, u32[]{:S(2)}) collective-permute-start(bf16[256,1024]{1,0:T(8,128)(2,1)} %collective-permute-done.10.refs_3_), channel_id=1, source_target_pairs={{0,1},{1,0},{2,3},{3,2},{4,5},{5,4},{6,7},{7,6},{8,9},{9,8},{10,11... | collective-permute-start | bytes 1572872 | tf_op jit(solution)/shard_map/ppermute | solution.py:38
  57.2 5.2 %collective-permute-start.15 = (bf16[256,1024]{1,0:T(8,128)(2,1)}, bf16[256,1024]{1,0:T(8,128)(2,1)S(1)}, u32[]{:S(2)}, u32[]{:S(2)}) collective-permute-start(bf16[256,1024]{1,0:T(8,128)(2,1)} %collective-permute-done.11.refs_4_), channel_id=1, source_target_pairs={{0,1},{1,0},{2,3},{3,2},{4,5},{5,4},{6,7},{7,6},{8,9},{9,8},{10,11... | collective-permute-start | bytes 1572872 | tf_op jit(solution)/shard_map/ppermute | solution.py:38
  57.7 4.7 %copy-start.1 = (f32[1024,1024]{1,0:T(8,128)S(1)}, f32[1024,1024]{1,0:T(8,128)}, u32[]{:S(2)}) copy-start(f32[1024,1024]{1,0:T(8,128)} %self_part.1.base_ref) | copy-start | bytes 12582916
  57.7 4.7 %copy-start.7 = (bf16[1024,1024]{1,0:T(8,128)(2,1)S(1)}, bf16[1024,1024]{1,0:T(8,128)(2,1)}, u32[]{:S(2)}) copy-start(bf16[1024,1024]{1,0:T(8,128)(2,1)} %weight_ref.3) | copy-start | bytes 6291460
  (3 other events, 7.1 us)

commit v4 on v3

--- a/solution.py
+++ b/solution.py
@@ -31,6 +31,7 @@
 ACROSS = pairs_of(lambda y, xl, z, xh, k: (y, 1 - xl, z, 1 - xh, k))
 UP = pairs_of(lambda y, xl, z, xh, k: (y, xl, (z + 1) % 4, xh, k))
 DOWN = pairs_of(lambda y, xl, z, xh, k: (y, xl, (z - 1) % 4, xh, k))
+ONWARD = pairs_of(lambda y, xl, z, xh, k: (y, xl, (z + 1 - 2 * k) % 4, xh, k))
 CORE = pairs_of(lambda y, xl, z, xh, k: (y, xl, z, xh, 1 - k))
 
 
@@ -219,6 +220,30 @@
     )(near(out_bias.reshape(1, D)))
 
 
+def choose_kernel(up_ref, down_ref, out_ref):
+    core = lax.axis_index("col") % 2
+
+    @pl.when(core == 0)
+    def _():
+        out_ref[...] = up_ref[...]
+
+    @pl.when(core == 1)
+    def _():
+        out_ref[...] = down_ref[...]
+
+
+def choose(up, down):
+    return pl.pallas_call(
+        choose_kernel,
+        in_specs=[ROWS, ROWS],
+        out_specs=ROWS,
+        out_shape=pltpu.VMEM(up.shape, up.dtype),
+        compiler_params=params(2),
+        cost_estimate=cost(1000, 1000),
+        name="choose",
+    )(near(up), near(down))
+
+
 def self_kernel(feats_ref, weight_ref, bias_ref, out_ref, stage_ref, sems):
     copies = []
     for step in range(4):
@@ -276,7 +301,7 @@
         out_shape=pltpu.HBM((NODES, D), jnp.float32),
         scratch_shapes=[pltpu.VMEM((NODES, D), jnp.float32), pltpu.SemaphoreType.DMA((4,))],
         compiler_params=params(10),
-        cost_estimate=cost(2 * NODES * width * D, 10 * MIB),
+        cost_estimate=cost(int(3 * NODES * width * D), 15 * MIB),
         name="hub_products",
     )(near(placed), *[near(part) for part in parts])
 
@@ -422,21 +447,15 @@
     own_c = send(own_k, CORE)
     bias = bias_rows(out_bias)
     up, down, across, own_c, bias = lax.optimization_barrier((up, down, across, own_c, bias))
-    two_low = send(up[:TB], UP)
-    two_high = send(down[TB:], DOWN)
+    two = send(choose(up, down), ONWARD)
     across_c = send(across, CORE)
     up_c = send(up, CORE)
     down_c = send(down, CORE)
     placed, placed_later, sums = placed_tiles(tile_blocks, tile_weights)
 
-    base = self_part(node_feats, self_weight, bias)
-
-    two_low, two_high, across, across_c, up_c, down_c, placed, base = (
-        lax.optimization_barrier(
-            (two_low, two_high, across, across_c, up_c, down_c, placed, base)
-        )
-    )
-    two = jnp.concatenate([two_low, two_high], 0)
+    two, across, across_c, up_c, down_c, placed, bias = lax.optimization_barrier(
+        (two, across, across_c, up_c, down_c, placed, bias)
+    )
     up_x = send(across, UP)
     down_x = send(across, DOWN)
     two_x = send(two, ACROSS)
@@ -445,10 +464,11 @@
         placed, [own, across, up, down, own_c, across_c, up_c, down_c]
     )
 
+    base = self_part(node_feats, self_weight, bias)
     carry, scale = tail_part(sums, carry, arrive_node, arrived)
 
-    up_x, down_x, two_x, two_c, carry = lax.optimization_barrier(
-        (up_x, down_x, two_x, two_c, carry)
+    up_x, down_x, two_x, two_c, carry, base = lax.optimization_barrier(
+        (up_x, down_x, two_x, two_c, carry, base)
     )
     late = [send(part, CORE) for part in (up_x, down_x, two_x)]
     carry = middle_part(placed_later, [two, two_c, up_x, down_x, two_x], carry)

time: 67.9 us -> 63.8 us (0.940)
  waiting for transfers between devices: 2.14 us -> 0.04 us
  local copies, waits for them, and re-layouts: 4.33 us -> 2.89 us
    ppermute x16 -> x15, waiting for transfers between devices: 2.13 us -> 0.04 us  [send(): return lax.ppermute(value, MESH_AXES, pairs)]
    concatenate x1 -> x0, local copies, waits for them, and re-layouts: 0.71 us -> none  [shards(): two = jnp.concatenate([two_low, two_high], 0)]
    unnamed x21 -> x20, local copies, waits for them, and re-layouts: 3.58 us -> 2.89 us
    ppermute x16 -> x15, starting transfers between devices: 21 us -> 20.3 us  [send(): return lax.ppermute(value, MESH_AXES, pairs)]
  transfers between devices with their start and end apart: 17 -> 16, of which waited for: 1 -> 0; matrix products, arithmetic and copies ran while one was open for 2% -> 0% of each run, Pallas kernels for 45% -> 48%
where the time goes in v4:
time: 63.8 us; the launch traced here: 63.5 us
  Pallas kernels  35.6 us (56%)
  starting transfers between devices  24.5 us (38%)
  local copies, waits for them, and re-layouts  2.89 us (5%)
    ppermute x15, starting transfers between devices, send(): return lax.ppermute(value, MESH_AXES, pairs)  20.3 us
    pallas_call x1, Pallas kernels, hub_products(): pl.pallas_call(body, in_specs=[ROWS] * (1 + len(parts)), out_specs=FAR, o...  7.36 us
    pallas_call x1, Pallas kernels, messages(): pl.pallas_call(message_kernel, in_specs=[WORDS, FAR, FAR, FAR], out_specs...  5.46 us
    pallas_call x1, Pallas kernels, last_part(): pl.pallas_call(body, in_specs=[ROWS] * (5 + len(parts)), out_specs=FAR, o...  5.03 us
    pallas_call x1, Pallas kernels, tail_part(): pl.pallas_call(body, in_specs=[ROWS] * 2 + [FAR] * 2, out_specs=[ROWS, RO...  4.88 us
    pallas_call x1, Pallas kernels, middle_part(): pl.pallas_call(body, in_specs=[ROWS] * (2 + len(parts)), out_specs=ROWS,...  4.69 us
    pallas_call x1, Pallas kernels, placed_tiles(): pl.pallas_call(place_kernel, in_specs=[WORDS, ROWS], out_specs=[ROWS, FAR...  4.23 us
    all_to_all x1, starting transfers between devices, shards(): lax.all_to_all(message, 'row', split_axis=0, concat_axis=0, tiled=True)  4.18 us
  transfers between devices with their start and end apart: 16, of which 0 were waited for; matrix products, arithmetic and copies ran while one was open for 0% of the time, Pallas kernels for 48%

profile of v4, /device:TPU:1, one launch (start us, length us, event | category | flops | bytes accessed | tf_op | source)
XLA Modules:
  0.0 63.5 jit_solution(12026767036778723462)
XLA Ops:
  0.0 4.6 %collective-permute-start.1 = (bf16[256,1024]{1,0:T(8,128)(2,1)}, bf16[256,1024]{1,0:T(8,128)(2,1)S(1)}, u32[]{:S(2)}, u32[]{:S(2)}) collective-permute-start(bf16[256,1024]{1,0:T(8,128)(2,1)} %refs_0_.1), channel_id=1, source_target_pairs={{0,12},{1,13},{2,14},{3,15},{4,0},{5,1},{6,2},{7,3},{8,4},{9,5},{1... | collective-permute-start | bytes 1572872 | tf_op jit(solution)/shard_map/ppermute | solution.py:39
  4.6 2.5 %collective-permute-start.2 = (bf16[256,1024]{1,0:T(8,128)(2,1)}, bf16[256,1024]{1,0:T(8,128)(2,1)}, u32[]{:S(2)}, u32[]{:S(2)}) collective-permute-start(bf16[256,1024]{1,0:T(8,128)(2,1)} %refs_0_.1), channel_id=1, source_target_pairs={{0,18},{1,19},{2,16},{3,17},{4,22},{5,23},{6,20},{7,21},{8,26},{9,... | collective-permute-start | bytes 1572872 | tf_op jit(solution)/shard_map/ppermute | solution.py:39
  7.1 0.7 %copy-done.9 = s32[8,1]{0,1:T(1,128)S(1)} copy-done((s32[8,1]{0,1:T(1,128)S(1)}, s32[8,1]{0,1:T(1,128)}, u32[]{:S(2)}) %copy-start.9) | copy-done | bytes 56
  7.7 5.5 %messages.1 = bf16[8,136,1024]{2,1,0:T(8,128)(2,1)} custom-call(s32[8]{0:T(128)S(1)} %bitcast.5, s32[8,128]{1,0:T(8,128)} %rows_hbm.1, bf16[8,128]{1,0:T(8,128)(2,1)} %weight_hbm.1, bf16[1024,1024]{1,0:T(8,128)(2,1)} %feats_ref.1), custom_call_target="tpu_custom_call" | custom-call | flops 4294967296 | bytes 10485760 | tf_op jit(solution)/shard_map/messages/pallas_call | solution.py:135
  13.2 0.0 copy-start.4
  13.2 0.0 copy-start.5
  13.2 1.3 %collective-permute-start.3 = (bf16[256,1024]{1,0:T(8,128)(2,1)}, bf16[256,1024]{1,0:T(8,128)(2,1)}, u32[]{:S(2)}, u32[]{:S(2)}) collective-permute-start(bf16[256,1024]{1,0:T(8,128)(2,1)} %refs_0_.1), channel_id=1, source_target_pairs={{0,1},{1,0},{2,3},{3,2},{4,5},{5,4},{6,7},{7,6},{8,9},{9,8},{10,11... | collective-permute-start | bytes 1572872 | tf_op jit(solution)/shard_map/ppermute | solution.py:39
  14.5 4.2 %all-to-all-start = ((bf16[8,136,1024]{2,1,0:T(8,128)(2,1)}), bf16[8,136,1024]{2,1,0:T(8,128)(2,1)S(1)}, u32[]{:S(2)}, u32[]{:S(2)}) async-start(bf16[8,136,1024]{2,1,0:T(8,128)(2,1)} %messages.1), calls=%async_computation | async-start | bytes 4456448 | tf_op jit(solution)/shard_map/all_to_all | solution.py:446
  18.8 0.1 choose.1
  18.8 3.0 %collective-permute-start.4 = (bf16[256,1024]{1,0:T(8,128)(2,1)S(1)}, bf16[256,1024]{1,0:T(8,128)(2,1)}, u32[]{:S(2)}, u32[]{:S(2)}) collective-permute-start(bf16[256,1024]{1,0:T(8,128)(2,1)S(1)} %choose.1), channel_id=1, source_target_pairs={{0,4},{1,13},{2,6},{3,15},{4,8},{5,1},{6,10},{7,3},{8,12},{9,5},{1... | collective-permute-start | bytes 1572872 | tf_op jit(solution)/shard_map/ppermute | solution.py:39
  21.9 0.5 collective-permute-start.6
  22.4 2.2 %copy-done = bf16[128,128,128]{2,1,0:T(8,128)(2,1)S(1)} copy-done((bf16[128,128,128]{2,1,0:T(8,128)(2,1)S(1)}, bf16[128,128,128]{2,1,0:T(8,128)(2,1)}, u32[]{:S(2)}) %copy-start) | copy-done | bytes 4194328
  24.6 4.2 %placed_tiles.1 = (bf16[1024,2048]{1,0:T(8,128)(2,1)S(1)}, bf16[1024,2048]{1,0:T(8,128)(2,1)}, f32[1024,128]{1,0:T(8,128)}) custom-call(s32[128]{0:T(128)S(1)} %bitcast.4, bf16[128,128,128]{2,1,0:T(8,128)(2,1)S(1)} %copy-done), custom_call_target="tpu_custom_call" | custom-call | bytes 25165824 | tf_op jit(solution)/shard_map/placed_tiles/pallas_call | solution.py:187
  28.9 2.6 %collective-permute-start.9 = (bf16[256,1024]{1,0:T(8,128)(2,1)}, bf16[256,1024]{1,0:T(8,128)(2,1)}, u32[]{:S(2)}, u32[]{:S(2)}) collective-permute-start(bf16[256,1024]{1,0:T(8,128)(2,1)} %collective-permute-done.2.refs_1_), channel_id=1, source_target_pairs={{0,12},{1,13},{2,14},{3,15},{4,0},{5,1},{6,2},{7,3},{8,4},{9,5},{1... | collective-permute-start | bytes 1572872 | tf_op jit(solution)/shard_map/ppermute | solution.py:39
  31.5 1.7 %collective-permute-start.11 = (bf16[256,1024]{1,0:T(8,128)(2,1)}, bf16[256,1024]{1,0:T(8,128)(2,1)}, u32[]{:S(2)}, u32[]{:S(2)}) collective-permute-start(bf16[256,1024]{1,0:T(8,128)(2,1)} %collective-permute-done.4.refs_0_), channel_id=1, source_target_pairs={{0,1},{1,0},{2,3},{3,2},{4,5},{5,4},{6,7},{7,6},{8,9},{9,8},{10,11... | collective-permute-start | bytes 1572872 | tf_op jit(solution)/shard_map/ppermute | solution.py:39
  33.2 2.5 %collective-permute-start.10 = (bf16[256,1024]{1,0:T(8,128)(2,1)}, bf16[256,1024]{1,0:T(8,128)(2,1)}, u32[]{:S(2)}, u32[]{:S(2)}) collective-permute-start(bf16[256,1024]{1,0:T(8,128)(2,1)} %collective-permute-done.4.refs_0_), channel_id=1, source_target_pairs={{0,18},{1,19},{2,16},{3,17},{4,22},{5,23},{6,20},{7,21},{8,26},{9,... | collective-permute-start | bytes 1572872 | tf_op jit(solution)/shard_map/ppermute | solution.py:39
  35.7 7.4 %hub_products.1.carry_hbm = f32[1024,1024]{1,0:T(8,128)} custom-call(bf16[1024,2048]{1,0:T(8,128)(2,1)S(1)} %get-tuple-element.40.placed_ref, bf16[256,1024]{1,0:T(8,128)(2,1)} %refs_0_.1, bf16[256,1024]{1,0:T(8,128)(2,1)} %collective-permute-done.2.refs_1_, bf16[256,1024]{1,0:T(8,128)(2,1)S(1)} %collective-permute-done.up_ref.refs_2_, ...), custom_call_target="tpu_custom_call" | custom-call | flops 12884901888 | bytes 31457280 | tf_op jit(solution)/shard_map/hub_products/pallas_call | solution.py:297
  43.1 3.9 %self_part.1.base_ref = f32[1024,1024]{1,0:T(8,128)} custom-call(bf16[1024,1024]{1,0:T(8,128)(2,1)S(1)} %copy-done.2, bf16[1024,1024]{1,0:T(8,128)(2,1)S(1)} %copy-done.3, f32[8,1024]{1,0:T(8,128)S(1)} %bias_rows.1.bias_ref), custom_call_target="tpu_custom_call" | custom-call | flops 2000 | bytes 2000 | tf_op jit(solution)/shard_map/self_part/pallas_call | solution.py:264
  47.0 4.9 %tail_part.1 = (f32[1024,1024]{1,0:T(8,128)S(1)}, f32[1024,128]{1,0:T(8,128)S(1)}) custom-call(s32[8,128]{1,0:T(8,128)S(1)} %copy-done.8, bf16[8,136,1024]{2,1,0:T(8,128)(2,1)S(1)} %all-to-all-done.got_ref, f32[1024,128]{1,0:T(8,128)} %get-tuple-element.32.sums_hbm, f32[1024,1024]{1,0:T(8,128)} %hub_products.1.carry_hbm), custom_call_target="tpu_custom_call" | custom-call | flops 4294967296 | bytes 20971520 | tf_op jit(solution)/shard_map/tail_part/pallas_call | solution.py:345
  52.0 1.1 %collective-permute-start.12 = (bf16[256,1024]{1,0:T(8,128)(2,1)}, bf16[256,1024]{1,0:T(8,128)(2,1)S(1)}, u32[]{:S(2)}, u32[]{:S(2)}) collective-permute-start(bf16[256,1024]{1,0:T(8,128)(2,1)} %collective-permute-done.8.refs_2_), channel_id=1, source_target_pairs={{0,1},{1,0},{2,3},{3,2},{4,5},{5,4},{6,7},{7,6},{8,9},{9,8},{10,11... | collective-permute-start | bytes 1572872 | tf_op jit(solution)/shard_map/ppermute | solution.py:39
  53.1 0.1 collective-permute-start.13
  53.2 0.4 collective-permute-start.14
  53.6 4.7 %middle_part.1.carry_ref = f32[1024,1024]{1,0:T(8,128)S(1)} custom-call(bf16[1024,2048]{1,0:T(8,128)(2,1)S(1)} %copy-done.6, f32[1024,1024]{1,0:T(8,128)S(1)} %get-tuple-element.51.carry_ref, bf16[256,1024]{1,0:T(8,128)(2,1)} %collective-permute-done.4.refs_0_, bf16[256,1024]{1,0:T(8,128)(2,1)} %collective-permute-done.11.refs_1_, ...), custom_call_target="tpu_custom_call" | custom-call | flops 5368709120 | bytes 20971520 | tf_op jit(solution)/shard_map/middle_part/pallas_call | solution.py:371
  58.3 5.0 %last_part.1 = bf16[1024,1024]{1,0:T(8,128)(2,1)} custom-call(f32[1024,128]{1,0:T(8,128)S(1)} %get-tuple-element.46.scale_ref, f32[1024,1024]{1,0:T(8,128)S(1)} %middle_part.1.carry_ref, f32[1024,1024]{1,0:T(8,128)S(1)} %copy-done.1, bf16[1024,1024]{1,0:T(8,128)(2,1)S(1)} %copy-done.7, bf16[1024,2048]{1,0:T(8,128)(2,1)S(1)} %copy-done.6, ...), custom_call_target="tpu_custom_call" | custom-call | flops 7516192768 | bytes 33554432 | tf_op jit(solution)/shard_map/last_part/pallas_call | solution.py:408
  (37 shorter events, 0.1 us)
Async XLA Ops:
  0.0 18.7 %collective-permute-start.1 = (bf16[256,1024]{1,0:T(8,128)(2,1)}, bf16[256,1024]{1,0:T(8,128)(2,1)S(1)}, u32[]{:S(2)}, u32[]{:S(2)}) collective-permute-start(bf16[256,1024]{1,0:T(8,128)(2,1)} %refs_0_.1), channel_id=1, source_target_pairs={{0,12},{1,13},{2,14},{3,15},{4,0},{5,1},{6,2},{7,3},{8,4},{9,5},{1... | collective-permute-start | bytes 1572872 | tf_op jit(solution)/shard_map/ppermute | solution.py:39
  4.6 14.2 %collective-permute-start = (bf16[256,1024]{1,0:T(8,128)(2,1)}, bf16[256,1024]{1,0:T(8,128)(2,1)S(1)}, u32[]{:S(2)}, u32[]{:S(2)}) collective-permute-start(bf16[256,1024]{1,0:T(8,128)(2,1)} %refs_0_.1), channel_id=1, source_target_pairs={{0,4},{1,5},{2,6},{3,7},{4,8},{5,9},{6,10},{7,11},{8,12},{9,13},{1... | collective-permute-start | bytes 1572872 | tf_op jit(solution)/shard_map/ppermute | solution.py:39
  4.6 14.2 %collective-permute-start.2 = (bf16[256,1024]{1,0:T(8,128)(2,1)}, bf16[256,1024]{1,0:T(8,128)(2,1)}, u32[]{:S(2)}, u32[]{:S(2)}) collective-permute-start(bf16[256,1024]{1,0:T(8,128)(2,1)} %refs_0_.1), channel_id=1, source_target_pairs={{0,18},{1,19},{2,16},{3,17},{4,22},{5,23},{6,20},{7,21},{8,26},{9,... | collective-permute-start | bytes 1572872 | tf_op jit(solution)/shard_map/ppermute | solution.py:39
  13.2 5.5 %copy-start.4 = (f32[1024]{0:T(1024)S(1)}, f32[1024]{0:T(1024)}, u32[]{:S(2)}) copy-start(f32[1024]{0:T(1024)} %param.15) | copy-start | bytes 12292
  13.2 9.2 %copy-start.5 = (s32[1,128]{1,0:T(1,128)S(1)}, s32[1,128]{1,0:T(1,128)}, u32[]{:S(2)}) copy-start(s32[1,128]{1,0:T(1,128)} %param.17) | copy-start | bytes 1540
  13.2 5.5 %collective-permute-start.3 = (bf16[256,1024]{1,0:T(8,128)(2,1)}, bf16[256,1024]{1,0:T(8,128)(2,1)}, u32[]{:S(2)}, u32[]{:S(2)}) collective-permute-start(bf16[256,1024]{1,0:T(8,128)(2,1)} %refs_0_.1), channel_id=1, source_target_pairs={{0,1},{1,0},{2,3},{3,2},{4,5},{5,4},{6,7},{7,6},{8,9},{9,8},{10,11... | collective-permute-start | bytes 1572872 | tf_op jit(solution)/shard_map/ppermute | solution.py:39
  14.5 32.5 %all-to-all-start = ((bf16[8,136,1024]{2,1,0:T(8,128)(2,1)}), bf16[8,136,1024]{2,1,0:T(8,128)(2,1)S(1)}, u32[]{:S(2)}, u32[]{:S(2)}) async-start(bf16[8,136,1024]{2,1,0:T(8,128)(2,1)} %messages.1), calls=%async_computation | async-start | bytes 4456448 | tf_op jit(solution)/shard_map/all_to_all | solution.py:446
  18.8 10.0 %collective-permute-start.4 = (bf16[256,1024]{1,0:T(8,128)(2,1)S(1)}, bf16[256,1024]{1,0:T(8,128)(2,1)}, u32[]{:S(2)}, u32[]{:S(2)}) collective-permute-start(bf16[256,1024]{1,0:T(8,128)(2,1)S(1)} %choose.1), channel_id=1, source_target_pairs={{0,4},{1,13},{2,6},{3,15},{4,8},{5,1},{6,10},{7,3},{8,12},{9,5},{1... | collective-permute-start | bytes 1572872 | tf_op jit(solution)/shard_map/ppermute | solution.py:39
  21.9 7.0 %collective-permute-start.5 = (bf16[256,1024]{1,0:T(8,128)(2,1)}, bf16[256,1024]{1,0:T(8,128)(2,1)S(1)}, u32[]{:S(2)}, u32[]{:S(2)}) collective-permute-start(bf16[256,1024]{1,0:T(8,128)(2,1)} %collective-permute-done.2.refs_1_), channel_id=1, source_target_pairs={{0,1},{1,0},{2,3},{3,2},{4,5},{5,4},{6,7},{7,6},{8,9},{9,8},{10,11... | collective-permute-start | bytes 1572872 | tf_op jit(solution)/shard_map/ppermute | solution.py:39
  21.9 7.0 %collective-permute-start.6 = (bf16[256,1024]{1,0:T(8,128)(2,1)S(1)}, bf16[256,1024]{1,0:T(8,128)(2,1)S(1)}, u32[]{:S(2)}, u32[]{:S(2)}) collective-permute-start(bf16[256,1024]{1,0:T(8,128)(2,1)S(1)} %collective-permute-done.up_ref.refs_2_), channel_id=1, source_target_pairs={{0,1},{1,0},{2,3},{3,2},{4,5},{5,4},{6,7},{7,6},{8,9},{9,8},{10,11... | collective-permute-start | bytes 1572872 | tf_op jit(solution)/shard_map/ppermute | solution.py:39
  22.4 6.5 %collective-permute-start.7 = (bf16[256,1024]{1,0:T(8,128)(2,1)S(1)}, bf16[256,1024]{1,0:T(8,128)(2,1)S(1)}, u32[]{:S(2)}, u32[]{:S(2)}) collective-permute-start(bf16[256,1024]{1,0:T(8,128)(2,1)S(1)} %collective-permute-done.1.down_ref.refs_3_), channel_id=1, source_target_pairs={{0,1},{1,0},{2,3},{3,2},{4,5},{5,4},{6,7},{7,6},{8,9},{9,8},{10,11... | collective-permute-start | bytes 1572872 | tf_op jit(solution)/shard_map/ppermute | solution.py:39
  28.9 14.2 %copy-start.2 = (bf16[1024,1024]{1,0:T(8,128)(2,1)S(1)}, bf16[1024,1024]{1,0:T(8,128)(2,1)}, u32[]{:S(2)}) copy-start(bf16[1024,1024]{1,0:T(8,128)(2,1)} %feats_ref.1) | copy-start | bytes 6291460
  28.9 14.2 %copy-start.3 = (bf16[1024,1024]{1,0:T(8,128)(2,1)S(1)}, bf16[1024,1024]{1,0:T(8,128)(2,1)}, u32[]{:S(2)}) copy-start(bf16[1024,1024]{1,0:T(8,128)(2,1)} %weight_ref.2) | copy-start | bytes 6291460
  28.9 23.1 %collective-permute-start.9 = (bf16[256,1024]{1,0:T(8,128)(2,1)}, bf16[256,1024]{1,0:T(8,128)(2,1)}, u32[]{:S(2)}, u32[]{:S(2)}) collective-permute-start(bf16[256,1024]{1,0:T(8,128)(2,1)} %collective-permute-done.2.refs_1_), channel_id=1, source_target_pairs={{0,12},{1,13},{2,14},{3,15},{4,0},{5,1},{6,2},{7,3},{8,4},{9,5},{1... | collective-permute-start | bytes 1572872 | tf_op jit(solution)/shard_map/ppermute | solution.py:39
  31.5 20.4 %collective-permute-start.8 = (bf16[256,1024]{1,0:T(8,128)(2,1)}, bf16[256,1024]{1,0:T(8,128)(2,1)}, u32[]{:S(2)}, u32[]{:S(2)}) collective-permute-start(bf16[256,1024]{1,0:T(8,128)(2,1)} %collective-permute-done.2.refs_1_), channel_id=1, source_target_pairs={{0,4},{1,5},{2,6},{3,7},{4,8},{5,9},{6,10},{7,11},{8,12},{9,13},{1... | collective-permute-start | bytes 1572872 | tf_op jit(solution)/shard_map/ppermute | solution.py:39
  31.5 20.4 %collective-permute-start.11 = (bf16[256,1024]{1,0:T(8,128)(2,1)}, bf16[256,1024]{1,0:T(8,128)(2,1)}, u32[]{:S(2)}, u32[]{:S(2)}) collective-permute-start(bf16[256,1024]{1,0:T(8,128)(2,1)} %collective-permute-done.4.refs_0_), channel_id=1, source_target_pairs={{0,1},{1,0},{2,3},{3,2},{4,5},{5,4},{6,7},{7,6},{8,9},{9,8},{10,11... | collective-permute-start | bytes 1572872 | tf_op jit(solution)/shard_map/ppermute | solution.py:39
  33.2 18.8 %collective-permute-start.10 = (bf16[256,1024]{1,0:T(8,128)(2,1)}, bf16[256,1024]{1,0:T(8,128)(2,1)}, u32[]{:S(2)}, u32[]{:S(2)}) collective-permute-start(bf16[256,1024]{1,0:T(8,128)(2,1)} %collective-permute-done.4.refs_0_), channel_id=1, source_target_pairs={{0,18},{1,19},{2,16},{3,17},{4,22},{5,23},{6,20},{7,21},{8,26},{9,... | collective-permute-start | bytes 1572872 | tf_op jit(solution)/shard_map/ppermute | solution.py:39
  43.1 4.0 %copy-start.8 = (s32[8,128]{1,0:T(8,128)S(1)}, s32[8,128]{1,0:T(8,128)}, u32[]{:S(2)}) copy-start(s32[8,128]{1,0:T(8,128)} %at_ref.1) | copy-start | bytes 12292
  47.0 6.5 %copy-start.6 = (bf16[1024,2048]{1,0:T(8,128)(2,1)S(1)}, bf16[1024,2048]{1,0:T(8,128)(2,1)}, u32[]{:S(2)}) copy-start(bf16[1024,2048]{1,0:T(8,128)(2,1)} %get-tuple-element.47.placed_ref) | copy-start | bytes 12582916
  52.0 6.3 %collective-permute-start.12 = (bf16[256,1024]{1,0:T(8,128)(2,1)}, bf16[256,1024]{1,0:T(8,128)(2,1)S(1)}, u32[]{:S(2)}, u32[]{:S(2)}) collective-permute-start(bf16[256,1024]{1,0:T(8,128)(2,1)} %collective-permute-done.8.refs_2_), channel_id=1, source_target_pairs={{0,1},{1,0},{2,3},{3,2},{4,5},{5,4},{6,7},{7,6},{8,9},{9,8},{10,11... | collective-permute-start | bytes 1572872 | tf_op jit(solution)/shard_map/ppermute | solution.py:39
  53.1 5.2 %collective-permute-start.13 = (bf16[256,1024]{1,0:T(8,128)(2,1)}, bf16[256,1024]{1,0:T(8,128)(2,1)S(1)}, u32[]{:S(2)}, u32[]{:S(2)}) collective-permute-start(bf16[256,1024]{1,0:T(8,128)(2,1)} %collective-permute-done.9.refs_3_), channel_id=1, source_target_pairs={{0,1},{1,0},{2,3},{3,2},{4,5},{5,4},{6,7},{7,6},{8,9},{9,8},{10,11... | collective-permute-start | bytes 1572872 | tf_op jit(solution)/shard_map/ppermute | solution.py:39
  53.2 5.1 %collective-permute-start.14 = (bf16[256,1024]{1,0:T(8,128)(2,1)}, bf16[256,1024]{1,0:T(8,128)(2,1)S(1)}, u32[]{:S(2)}, u32[]{:S(2)}) collective-permute-start(bf16[256,1024]{1,0:T(8,128)(2,1)} %collective-permute-done.10.refs_4_), channel_id=1, source_target_pairs={{0,1},{1,0},{2,3},{3,2},{4,5},{5,4},{6,7},{7,6},{8,9},{9,8},{10,11... | collective-permute-start | bytes 1572872 | tf_op jit(solution)/shard_map/ppermute | solution.py:39
  53.6 4.7 %copy-start.1 = (f32[1024,1024]{1,0:T(8,128)S(1)}, f32[1024,1024]{1,0:T(8,128)}, u32[]{:S(2)}) copy-start(f32[1024,1024]{1,0:T(8,128)} %self_part.1.base_ref) | copy-start | bytes 12582916
  53.6 4.7 %copy-start.7 = (bf16[1024,1024]{1,0:T(8,128)(2,1)S(1)}, bf16[1024,1024]{1,0:T(8,128)(2,1)}, u32[]{:S(2)}) copy-start(bf16[1024,1024]{1,0:T(8,128)(2,1)} %weight_ref.3) | copy-start | bytes 6291460
  (2 other events, 2.8 us)

commit v5 on v4

--- a/solution.py
+++ b/solution.py
@@ -306,26 +306,14 @@
     )(near(placed), *[near(part) for part in parts])
 
 
-def tail_part(sums, carry, arrive_node, arrived):
-    def body(
-        at_ref, got_ref, sums_hbm, carry_hbm, out_ref, scale_ref, hot_ref, sums_ref,
-        carry_ref, sems,
-    ):
-        pairs = [(sums_hbm, sums_ref)]
-        for step in range(4):
-            lanes = slice(step * 256, (step + 1) * 256)
-            pairs.append((carry_hbm.at[:, lanes], carry_ref.at[:, lanes]))
-        loads = [
-            pltpu.make_async_copy(source, target, sems.at[i])
-            for i, (source, target) in enumerate(pairs)
-        ]
-        for load in loads:
-            load.start()
-        loads[0].wait()
+def tail_part(sums, arrive_node, arrived):
+    def body(at_ref, got_ref, sums_hbm, out_ref, scale_ref, hot_ref, sums_ref, sem):
+        load = pltpu.make_async_copy(sums_hbm, sums_ref, sem)
+        load.start()
         for step in range(4):
             rows = slice(step * 256, (step + 1) * 256)
             node = lax.broadcasted_iota(jnp.int32, (256, SLOTS), 0) + step * 256
-            weights = sums_ref[rows, :]
+            weights = jnp.zeros((256, SLOTS), jnp.float32)
             for o in range(8):
                 hit = at_ref[o : o + 1, :] == node
                 hot_ref[rows, o * SLOTS : (o + 1) * SLOTS] = jnp.where(hit, 1.0, 0.0).astype(
@@ -333,50 +321,50 @@
                 )
                 line = got_ref[o, SLOTS : SLOTS + 1, 0:SLOTS].astype(jnp.float32)
                 weights = weights + jnp.where(hit, line, 0.0)
-            weight_sum = jnp.sum(weights, axis=-1, keepdims=True)
-            scale_ref[rows, :] = jnp.broadcast_to(lax.rsqrt(1.0 + weight_sum), (256, TB))
-        for load in loads[1:]:
-            load.wait()
+            scale_ref[rows, :] = weights
+        load.wait()
+        weight_sum = jnp.sum(scale_ref[...] + sums_ref[...], axis=-1, keepdims=True)
+        scale_ref[...] = jnp.broadcast_to(lax.rsqrt(1.0 + weight_sum), (NODES, TB))
         for step in range(4):
             lanes = slice(step * 256, (step + 1) * 256)
             got = jnp.concatenate([got_ref[o, 0:SLOTS, lanes] for o in range(8)], axis=0)
-            out_ref[:, lanes] = product(hot_ref[...], got) + carry_ref[:, lanes]
+            out_ref[:, lanes] = product(hot_ref[...], got)
 
     return pl.pallas_call(
         body,
-        in_specs=[ROWS] * 2 + [FAR] * 2,
+        in_specs=[ROWS] * 2 + [FAR],
         out_specs=[ROWS, ROWS],
         out_shape=[pltpu.VMEM((NODES, D), jnp.float32), pltpu.VMEM((NODES, TB), jnp.float32)],
         scratch_shapes=[
             pltpu.VMEM((NODES, 8 * SLOTS), jnp.bfloat16),
             pltpu.VMEM((NODES, TB), jnp.float32),
-            pltpu.VMEM((NODES, D), jnp.float32),
-            pltpu.SemaphoreType.DMA((5,)),
-        ],
-        compiler_params=params(14),
+            pltpu.SemaphoreType.DMA,
+        ],
+        compiler_params=params(10),
         cost_estimate=cost(2 * NODES * NODES * D, 10 * MIB),
         name="tail_part",
-    )(near(arrive_node), near(arrived), far(sums), far(carry))
-
-
-def middle_part(placed, parts, carry):
+    )(near(arrive_node), near(arrived), far(sums))
+
+
+def middle_part(placed, parts, carry, tail):
     width = sum(part.shape[0] for part in parts)
 
-    def body(placed_ref, carry_ref, *refs):
+    def body(placed_ref, carry_ref, tail_ref, *refs):
         for step in range(4):
             lanes = slice(step * 256, (step + 1) * 256)
             hubs = jnp.concatenate([ref[:, lanes] for ref in refs[: len(parts)]], axis=0)
-            refs[-1][:, lanes] = product(placed_ref[:, 0:width], hubs) + carry_ref[:, lanes]
+            total = product(placed_ref[:, 0:width], hubs) + carry_ref[:, lanes]
+            refs[-1][:, lanes] = total + tail_ref[:, lanes]
 
     return pl.pallas_call(
         body,
-        in_specs=[ROWS] * (2 + len(parts)),
+        in_specs=[ROWS] * (3 + len(parts)),
         out_specs=ROWS,
         out_shape=pltpu.VMEM((NODES, D), jnp.float32),
         compiler_params=params(8),
         cost_estimate=cost(2 * NODES * width * D, 10 * MIB),
         name="middle_part",
-    )(near(placed), near(carry), *[near(part) for part in parts])
+    )(near(placed), near(carry), near(tail), *[near(part) for part in parts])
 
 
 def last_part(placed, parts, scale, carry, base, neigh_weight):
@@ -465,13 +453,13 @@
     )
 
     base = self_part(node_feats, self_weight, bias)
-    carry, scale = tail_part(sums, carry, arrive_node, arrived)
-
-    up_x, down_x, two_x, two_c, carry, base = lax.optimization_barrier(
-        (up_x, down_x, two_x, two_c, carry, base)
+    tail, scale = tail_part(sums, arrive_node, arrived)
+
+    up_x, down_x, two_x, two_c, carry, tail, base = lax.optimization_barrier(
+        (up_x, down_x, two_x, two_c, carry, tail, base)
     )
     late = [send(part, CORE) for part in (up_x, down_x, two_x)]
-    carry = middle_part(placed_later, [two, two_c, up_x, down_x, two_x], carry)
+    carry = middle_part(placed_later, [two, two_c, up_x, down_x, two_x], carry, tail)
     return last_part(placed_later, late, scale, carry, base, neigh_weight)
 
 

time: 63.8 us -> 62.5 us (0.980)
  Pallas kernels: 35.6 us -> 34.3 us
    pallas_call x2, Pallas kernels: 9.57 us -> 8.24 us  [the longest x1 4.7 us: middle_part(): pl.pallas_call(body, in_specs=[ROWS] * (3 + len(parts)), out_specs=ROWS,...]
    unnamed x20 -> x22, local copies, waits for them, and re-layouts: 2.89 us -> 2.89 us
  transfers between devices with their start and end apart: 16 -> 16, of which waited for: 0 -> 0; matrix products, arithmetic and copies ran while one was open for 0% -> 0% of each run, Pallas kernels for 48% -> 47%
where the time goes in v5:
time: 62.5 us; the launch traced here: 62.2 us
  Pallas kernels  34.3 us (55%)
  starting transfers between devices  24.5 us (39%)
  local copies, waits for them, and re-layouts  2.89 us (5%)
    ppermute x15, starting transfers between devices, send(): return lax.ppermute(value, MESH_AXES, pairs)  20.3 us
    pallas_call x1, Pallas kernels, hub_products(): pl.pallas_call(body, in_specs=[ROWS] * (1 + len(parts)), out_specs=FAR, o...  7.37 us
    pallas_call x1, Pallas kernels, messages(): pl.pallas_call(message_kernel, in_specs=[WORDS, FAR, FAR, FAR], out_specs...  5.47 us
    pallas_call x1, Pallas kernels, last_part(): pl.pallas_call(body, in_specs=[ROWS] * (5 + len(parts)), out_specs=FAR, o...  5.03 us
    pallas_call x1, Pallas kernels, middle_part(): pl.pallas_call(body, in_specs=[ROWS] * (3 + len(parts)), out_specs=ROWS,...  4.7 us
    pallas_call x1, Pallas kernels, placed_tiles(): pl.pallas_call(place_kernel, in_specs=[WORDS, ROWS], out_specs=[ROWS, FAR...  4.23 us
    all_to_all x1, starting transfers between devices, shards(): lax.all_to_all(message, 'row', split_axis=0, concat_axis=0, tiled=True)  4.18 us
    pallas_call x1, Pallas kernels, self_part(): pl.pallas_call(self_kernel, in_specs=[ROWS, ROWS, ROWS], out_specs=FAR, o...  3.88 us
  transfers between devices with their start and end apart: 16, of which 0 were waited for; matrix products, arithmetic and copies ran while one was open for 0% of the time, Pallas kernels for 47%

profile of v5, /device:TPU:1, one launch (start us, length us, event | category | flops | bytes accessed | tf_op | source)
XLA Modules:
  0.0 62.2 jit_solution(18125980075764807916)
XLA Ops:
  0.0 4.6 %collective-permute-start.1 = (bf16[256,1024]{1,0:T(8,128)(2,1)}, bf16[256,1024]{1,0:T(8,128)(2,1)S(1)}, u32[]{:S(2)}, u32[]{:S(2)}) collective-permute-start(bf16[256,1024]{1,0:T(8,128)(2,1)} %refs_0_.1), channel_id=1, source_target_pairs={{0,12},{1,13},{2,14},{3,15},{4,0},{5,1},{6,2},{7,3},{8,4},{9,5},{1... | collective-permute-start | bytes 1572872 | tf_op jit(solution)/shard_map/ppermute | solution.py:39
  4.6 2.5 %collective-permute-start.2 = (bf16[256,1024]{1,0:T(8,128)(2,1)}, bf16[256,1024]{1,0:T(8,128)(2,1)}, u32[]{:S(2)}, u32[]{:S(2)}) collective-permute-start(bf16[256,1024]{1,0:T(8,128)(2,1)} %refs_0_.1), channel_id=1, source_target_pairs={{0,18},{1,19},{2,16},{3,17},{4,22},{5,23},{6,20},{7,21},{8,26},{9,... | collective-permute-start | bytes 1572872 | tf_op jit(solution)/shard_map/ppermute | solution.py:39
  7.1 0.7 %copy-done.9 = s32[8,1]{0,1:T(1,128)S(1)} copy-done((s32[8,1]{0,1:T(1,128)S(1)}, s32[8,1]{0,1:T(1,128)}, u32[]{:S(2)}) %copy-start.9) | copy-done | bytes 56
  7.7 5.5 %messages.1 = bf16[8,136,1024]{2,1,0:T(8,128)(2,1)} custom-call(s32[8]{0:T(128)S(1)} %bitcast.5, s32[8,128]{1,0:T(8,128)} %rows_hbm.1, bf16[8,128]{1,0:T(8,128)(2,1)} %weight_hbm.1, bf16[1024,1024]{1,0:T(8,128)(2,1)} %feats_ref.1), custom_call_target="tpu_custom_call" | custom-call | flops 4294967296 | bytes 10485760 | tf_op jit(solution)/shard_map/messages/pallas_call | solution.py:135
  13.2 0.0 copy-start.5
  13.2 1.3 %collective-permute-start.3 = (bf16[256,1024]{1,0:T(8,128)(2,1)}, bf16[256,1024]{1,0:T(8,128)(2,1)}, u32[]{:S(2)}, u32[]{:S(2)}) collective-permute-start(bf16[256,1024]{1,0:T(8,128)(2,1)} %refs_0_.1), channel_id=1, source_target_pairs={{0,1},{1,0},{2,3},{3,2},{4,5},{5,4},{6,7},{7,6},{8,9},{9,8},{10,11... | collective-permute-start | bytes 1572872 | tf_op jit(solution)/shard_map/ppermute | solution.py:39
  14.5 4.2 %all-to-all-start = ((bf16[8,136,1024]{2,1,0:T(8,128)(2,1)}), bf16[8,136,1024]{2,1,0:T(8,128)(2,1)S(1)}, u32[]{:S(2)}, u32[]{:S(2)}) async-start(bf16[8,136,1024]{2,1,0:T(8,128)(2,1)} %messages.1), calls=%async_computation | async-start | bytes 4456448 | tf_op jit(solution)/shard_map/all_to_all | solution.py:434
  18.8 0.1 choose.1
  18.8 3.0 %collective-permute-start.4 = (bf16[256,1024]{1,0:T(8,128)(2,1)S(1)}, bf16[256,1024]{1,0:T(8,128)(2,1)}, u32[]{:S(2)}, u32[]{:S(2)}) collective-permute-start(bf16[256,1024]{1,0:T(8,128)(2,1)S(1)} %choose.1), channel_id=1, source_target_pairs={{0,4},{1,13},{2,6},{3,15},{4,8},{5,1},{6,10},{7,3},{8,12},{9,5},{1... | collective-permute-start | bytes 1572872 | tf_op jit(solution)/shard_map/ppermute | solution.py:39
  21.9 0.5 collective-permute-start.6
  22.4 2.2 %copy-done = bf16[128,128,128]{2,1,0:T(8,128)(2,1)S(1)} copy-done((bf16[128,128,128]{2,1,0:T(8,128)(2,1)S(1)}, bf16[128,128,128]{2,1,0:T(8,128)(2,1)}, u32[]{:S(2)}) %copy-start) | copy-done | bytes 4194328
  24.6 4.2 %placed_tiles.1 = (bf16[1024,2048]{1,0:T(8,128)(2,1)S(1)}, bf16[1024,2048]{1,0:T(8,128)(2,1)}, f32[1024,128]{1,0:T(8,128)}) custom-call(s32[128]{0:T(128)S(1)} %bitcast.4, bf16[128,128,128]{2,1,0:T(8,128)(2,1)S(1)} %copy-done), custom_call_target="tpu_custom_call" | custom-call | bytes 25165824 | tf_op jit(solution)/shard_map/placed_tiles/pallas_call | solution.py:187
  28.9 2.6 %collective-permute-start.9 = (bf16[256,1024]{1,0:T(8,128)(2,1)}, bf16[256,1024]{1,0:T(8,128)(2,1)}, u32[]{:S(2)}, u32[]{:S(2)}) collective-permute-start(bf16[256,1024]{1,0:T(8,128)(2,1)} %collective-permute-done.2.refs_1_), channel_id=1, source_target_pairs={{0,12},{1,13},{2,14},{3,15},{4,0},{5,1},{6,2},{7,3},{8,4},{9,5},{1... | collective-permute-start | bytes 1572872 | tf_op jit(solution)/shard_map/ppermute | solution.py:39
  31.5 1.7 %collective-permute-start.11 = (bf16[256,1024]{1,0:T(8,128)(2,1)}, bf16[256,1024]{1,0:T(8,128)(2,1)}, u32[]{:S(2)}, u32[]{:S(2)}) collective-permute-start(bf16[256,1024]{1,0:T(8,128)(2,1)} %collective-permute-done.4.refs_0_), channel_id=1, source_target_pairs={{0,1},{1,0},{2,3},{3,2},{4,5},{5,4},{6,7},{7,6},{8,9},{9,8},{10,11... | collective-permute-start | bytes 1572872 | tf_op jit(solution)/shard_map/ppermute | solution.py:39
  33.2 2.5 %collective-permute-start.10 = (bf16[256,1024]{1,0:T(8,128)(2,1)}, bf16[256,1024]{1,0:T(8,128)(2,1)}, u32[]{:S(2)}, u32[]{:S(2)}) collective-permute-start(bf16[256,1024]{1,0:T(8,128)(2,1)} %collective-permute-done.4.refs_0_), channel_id=1, source_target_pairs={{0,18},{1,19},{2,16},{3,17},{4,22},{5,23},{6,20},{7,21},{8,26},{9,... | collective-permute-start | bytes 1572872 | tf_op jit(solution)/shard_map/ppermute | solution.py:39
  35.7 7.4 %hub_products.1.carry_ref = f32[1024,1024]{1,0:T(8,128)} custom-call(bf16[1024,2048]{1,0:T(8,128)(2,1)S(1)} %get-tuple-element.45.placed_ref, bf16[256,1024]{1,0:T(8,128)(2,1)} %refs_0_.1, bf16[256,1024]{1,0:T(8,128)(2,1)} %collective-permute-done.2.refs_1_, bf16[256,1024]{1,0:T(8,128)(2,1)S(1)} %collective-permute-done.up_ref.refs_2_, ...), custom_call_target="tpu_custom_call" | custom-call | flops 12884901888 | bytes 31457280 | tf_op jit(solution)/shard_map/hub_products/pallas_call | solution.py:297
  43.1 0.0 copy-start.8
  43.1 3.9 %self_part.1.base_ref = f32[1024,1024]{1,0:T(8,128)} custom-call(bf16[1024,1024]{1,0:T(8,128)(2,1)S(1)} %copy-done.2, bf16[1024,1024]{1,0:T(8,128)(2,1)S(1)} %copy-done.3, f32[8,1024]{1,0:T(8,128)S(1)} %bias_rows.1.bias_ref), custom_call_target="tpu_custom_call" | custom-call | flops 2000 | bytes 2000 | tf_op jit(solution)/shard_map/self_part/pallas_call | solution.py:264
  47.0 3.5 %tail_part.1 = (f32[1024,1024]{1,0:T(8,128)S(1)}, f32[1024,128]{1,0:T(8,128)S(1)}) custom-call(s32[8,128]{1,0:T(8,128)S(1)} %copy-done.8, bf16[8,136,1024]{2,1,0:T(8,128)(2,1)S(1)} %all-to-all-done.got_ref, f32[1024,128]{1,0:T(8,128)} %get-tuple-element.33.sums_hbm), custom_call_target="tpu_custom_call" | custom-call | flops 4294967296 | bytes 20971520 | tf_op jit(solution)/shard_map/tail_part/pallas_call | solution.py:333
  50.6 1.1 %collective-permute-start.12 = (bf16[256,1024]{1,0:T(8,128)(2,1)}, bf16[256,1024]{1,0:T(8,128)(2,1)S(1)}, u32[]{:S(2)}, u32[]{:S(2)}) collective-permute-start(bf16[256,1024]{1,0:T(8,128)(2,1)} %collective-permute-done.8.refs_2_), channel_id=1, source_target_pairs={{0,1},{1,0},{2,3},{3,2},{4,5},{5,4},{6,7},{7,6},{8,9},{9,8},{10,11... | collective-permute-start | bytes 1572872 | tf_op jit(solution)/shard_map/ppermute | solution.py:39
  51.7 0.1 collective-permute-start.13
  51.8 0.4 collective-permute-start.14
  52.3 4.7 %middle_part.1.carry_ref = f32[1024,1024]{1,0:T(8,128)S(1)} custom-call(bf16[1024,2048]{1,0:T(8,128)(2,1)S(1)} %copy-done.6, f32[1024,1024]{1,0:T(8,128)S(1)} %copy-done.10, f32[1024,1024]{1,0:T(8,128)S(1)} %get-tuple-element.53.tail_ref, bf16[256,1024]{1,0:T(8,128)(2,1)} %collective-permute-done.4.refs_0_, ...), custom_call_target="tpu_custom_call" | custom-call | flops 5368709120 | bytes 20971520 | tf_op jit(solution)/shard_map/middle_part/pallas_call | solution.py:359
  57.0 5.0 %last_part.1 = bf16[1024,1024]{1,0:T(8,128)(2,1)} custom-call(f32[1024,128]{1,0:T(8,128)S(1)} %get-tuple-element.34.scale_ref, f32[1024,1024]{1,0:T(8,128)S(1)} %middle_part.1.carry_ref, f32[1024,1024]{1,0:T(8,128)S(1)} %copy-done.1, bf16[1024,1024]{1,0:T(8,128)(2,1)S(1)} %copy-done.7, bf16[1024,2048]{1,0:T(8,128)(2,1)S(1)} %copy-done.6, ...), custom_call_target="tpu_custom_call" | custom-call | flops 7516192768 | bytes 33554432 | tf_op jit(solution)/shard_map/last_part/pallas_call | solution.py:396
  (39 shorter events, 0.1 us)
Async XLA Ops:
  0.0 18.7 %collective-permute-start.1 = (bf16[256,1024]{1,0:T(8,128)(2,1)}, bf16[256,1024]{1,0:T(8,128)(2,1)S(1)}, u32[]{:S(2)}, u32[]{:S(2)}) collective-permute-start(bf16[256,1024]{1,0:T(8,128)(2,1)} %refs_0_.1), channel_id=1, source_target_pairs={{0,12},{1,13},{2,14},{3,15},{4,0},{5,1},{6,2},{7,3},{8,4},{9,5},{1... | collective-permute-start | bytes 1572872 | tf_op jit(solution)/shard_map/ppermute | solution.py:39
  4.6 14.2 %collective-permute-start = (bf16[256,1024]{1,0:T(8,128)(2,1)}, bf16[256,1024]{1,0:T(8,128)(2,1)S(1)}, u32[]{:S(2)}, u32[]{:S(2)}) collective-permute-start(bf16[256,1024]{1,0:T(8,128)(2,1)} %refs_0_.1), channel_id=1, source_target_pairs={{0,4},{1,5},{2,6},{3,7},{4,8},{5,9},{6,10},{7,11},{8,12},{9,13},{1... | collective-permute-start | bytes 1572872 | tf_op jit(solution)/shard_map/ppermute | solution.py:39
  4.6 14.2 %collective-permute-start.2 = (bf16[256,1024]{1,0:T(8,128)(2,1)}, bf16[256,1024]{1,0:T(8,128)(2,1)}, u32[]{:S(2)}, u32[]{:S(2)}) collective-permute-start(bf16[256,1024]{1,0:T(8,128)(2,1)} %refs_0_.1), channel_id=1, source_target_pairs={{0,18},{1,19},{2,16},{3,17},{4,22},{5,23},{6,20},{7,21},{8,26},{9,... | collective-permute-start | bytes 1572872 | tf_op jit(solution)/shard_map/ppermute | solution.py:39
  13.2 5.5 %copy-start.4 = (f32[1024]{0:T(1024)S(1)}, f32[1024]{0:T(1024)}, u32[]{:S(2)}) copy-start(f32[1024]{0:T(1024)} %param.15) | copy-start | bytes 12292
  13.2 9.2 %copy-start.5 = (s32[1,128]{1,0:T(1,128)S(1)}, s32[1,128]{1,0:T(1,128)}, u32[]{:S(2)}) copy-start(s32[1,128]{1,0:T(1,128)} %param.17) | copy-start | bytes 1540
  13.2 5.5 %collective-permute-start.3 = (bf16[256,1024]{1,0:T(8,128)(2,1)}, bf16[256,1024]{1,0:T(8,128)(2,1)}, u32[]{:S(2)}, u32[]{:S(2)}) collective-permute-start(bf16[256,1024]{1,0:T(8,128)(2,1)} %refs_0_.1), channel_id=1, source_target_pairs={{0,1},{1,0},{2,3},{3,2},{4,5},{5,4},{6,7},{7,6},{8,9},{9,8},{10,11... | collective-permute-start | bytes 1572872 | tf_op jit(solution)/shard_map/ppermute | solution.py:39
  14.5 32.4 %all-to-all-start = ((bf16[8,136,1024]{2,1,0:T(8,128)(2,1)}), bf16[8,136,1024]{2,1,0:T(8,128)(2,1)S(1)}, u32[]{:S(2)}, u32[]{:S(2)}) async-start(bf16[8,136,1024]{2,1,0:T(8,128)(2,1)} %messages.1), calls=%async_computation | async-start | bytes 4456448 | tf_op jit(solution)/shard_map/all_to_all | solution.py:434
  18.8 10.0 %collective-permute-start.4 = (bf16[256,1024]{1,0:T(8,128)(2,1)S(1)}, bf16[256,1024]{1,0:T(8,128)(2,1)}, u32[]{:S(2)}, u32[]{:S(2)}) collective-permute-start(bf16[256,1024]{1,0:T(8,128)(2,1)S(1)} %choose.1), channel_id=1, source_target_pairs={{0,4},{1,13},{2,6},{3,15},{4,8},{5,1},{6,10},{7,3},{8,12},{9,5},{1... | collective-permute-start | bytes 1572872 | tf_op jit(solution)/shard_map/ppermute | solution.py:39
  21.9 7.0 %collective-permute-start.5 = (bf16[256,1024]{1,0:T(8,128)(2,1)}, bf16[256,1024]{1,0:T(8,128)(2,1)S(1)}, u32[]{:S(2)}, u32[]{:S(2)}) collective-permute-start(bf16[256,1024]{1,0:T(8,128)(2,1)} %collective-permute-done.2.refs_1_), channel_id=1, source_target_pairs={{0,1},{1,0},{2,3},{3,2},{4,5},{5,4},{6,7},{7,6},{8,9},{9,8},{10,11... | collective-permute-start | bytes 1572872 | tf_op jit(solution)/shard_map/ppermute | solution.py:39
  21.9 7.0 %collective-permute-start.6 = (bf16[256,1024]{1,0:T(8,128)(2,1)S(1)}, bf16[256,1024]{1,0:T(8,128)(2,1)S(1)}, u32[]{:S(2)}, u32[]{:S(2)}) collective-permute-start(bf16[256,1024]{1,0:T(8,128)(2,1)S(1)} %collective-permute-done.up_ref.refs_2_), channel_id=1, source_target_pairs={{0,1},{1,0},{2,3},{3,2},{4,5},{5,4},{6,7},{7,6},{8,9},{9,8},{10,11... | collective-permute-start | bytes 1572872 | tf_op jit(solution)/shard_map/ppermute | solution.py:39
  22.4 6.5 %collective-permute-start.7 = (bf16[256,1024]{1,0:T(8,128)(2,1)S(1)}, bf16[256,1024]{1,0:T(8,128)(2,1)S(1)}, u32[]{:S(2)}, u32[]{:S(2)}) collective-permute-start(bf16[256,1024]{1,0:T(8,128)(2,1)S(1)} %collective-permute-done.1.down_ref.refs_3_), channel_id=1, source_target_pairs={{0,1},{1,0},{2,3},{3,2},{4,5},{5,4},{6,7},{7,6},{8,9},{9,8},{10,11... | collective-permute-start | bytes 1572872 | tf_op jit(solution)/shard_map/ppermute | solution.py:39
  28.9 14.2 %copy-start.2 = (bf16[1024,1024]{1,0:T(8,128)(2,1)S(1)}, bf16[1024,1024]{1,0:T(8,128)(2,1)}, u32[]{:S(2)}) copy-start(bf16[1024,1024]{1,0:T(8,128)(2,1)} %feats_ref.1) | copy-start | bytes 6291460
  28.9 14.2 %copy-start.3 = (bf16[1024,1024]{1,0:T(8,128)(2,1)S(1)}, bf16[1024,1024]{1,0:T(8,128)(2,1)}, u32[]{:S(2)}) copy-start(bf16[1024,1024]{1,0:T(8,128)(2,1)} %weight_ref.2) | copy-start | bytes 6291460
  28.9 21.7 %collective-permute-start.9 = (bf16[256,1024]{1,0:T(8,128)(2,1)}, bf16[256,1024]{1,0:T(8,128)(2,1)}, u32[]{:S(2)}, u32[]{:S(2)}) collective-permute-start(bf16[256,1024]{1,0:T(8,128)(2,1)} %collective-permute-done.2.refs_1_), channel_id=1, source_target_pairs={{0,12},{1,13},{2,14},{3,15},{4,0},{5,1},{6,2},{7,3},{8,4},{9,5},{1... | collective-permute-start | bytes 1572872 | tf_op jit(solution)/shard_map/ppermute | solution.py:39
  31.5 19.1 %collective-permute-start.8 = (bf16[256,1024]{1,0:T(8,128)(2,1)}, bf16[256,1024]{1,0:T(8,128)(2,1)}, u32[]{:S(2)}, u32[]{:S(2)}) collective-permute-start(bf16[256,1024]{1,0:T(8,128)(2,1)} %collective-permute-done.2.refs_1_), channel_id=1, source_target_pairs={{0,4},{1,5},{2,6},{3,7},{4,8},{5,9},{6,10},{7,11},{8,12},{9,13},{1... | collective-permute-start | bytes 1572872 | tf_op jit(solution)/shard_map/ppermute | solution.py:39
  31.5 19.1 %collective-permute-start.11 = (bf16[256,1024]{1,0:T(8,128)(2,1)}, bf16[256,1024]{1,0:T(8,128)(2,1)}, u32[]{:S(2)}, u32[]{:S(2)}) collective-permute-start(bf16[256,1024]{1,0:T(8,128)(2,1)} %collective-permute-done.4.refs_0_), channel_id=1, source_target_pairs={{0,1},{1,0},{2,3},{3,2},{4,5},{5,4},{6,7},{7,6},{8,9},{9,8},{10,11... | collective-permute-start | bytes 1572872 | tf_op jit(solution)/shard_map/ppermute | solution.py:39
  33.2 17.4 %collective-permute-start.10 = (bf16[256,1024]{1,0:T(8,128)(2,1)}, bf16[256,1024]{1,0:T(8,128)(2,1)}, u32[]{:S(2)}, u32[]{:S(2)}) collective-permute-start(bf16[256,1024]{1,0:T(8,128)(2,1)} %collective-permute-done.4.refs_0_), channel_id=1, source_target_pairs={{0,18},{1,19},{2,16},{3,17},{4,22},{5,23},{6,20},{7,21},{8,26},{9,... | collective-permute-start | bytes 1572872 | tf_op jit(solution)/shard_map/ppermute | solution.py:39
  47.0 5.2 %copy-start.6 = (bf16[1024,2048]{1,0:T(8,128)(2,1)S(1)}, bf16[1024,2048]{1,0:T(8,128)(2,1)}, u32[]{:S(2)}) copy-start(bf16[1024,2048]{1,0:T(8,128)(2,1)} %get-tuple-element.35.placed_ref) | copy-start | bytes 12582916
  47.0 5.2 %copy-start.10 = (f32[1024,1024]{1,0:T(8,128)S(1)}, f32[1024,1024]{1,0:T(8,128)}, u32[]{:S(2)}) copy-start(f32[1024,1024]{1,0:T(8,128)} %hub_products.1.carry_ref) | copy-start | bytes 12582916
  50.6 6.4 %collective-permute-start.12 = (bf16[256,1024]{1,0:T(8,128)(2,1)}, bf16[256,1024]{1,0:T(8,128)(2,1)S(1)}, u32[]{:S(2)}, u32[]{:S(2)}) collective-permute-start(bf16[256,1024]{1,0:T(8,128)(2,1)} %collective-permute-done.8.refs_2_), channel_id=1, source_target_pairs={{0,1},{1,0},{2,3},{3,2},{4,5},{5,4},{6,7},{7,6},{8,9},{9,8},{10,11... | collective-permute-start | bytes 1572872 | tf_op jit(solution)/shard_map/ppermute | solution.py:39
  51.7 5.2 %collective-permute-start.13 = (bf16[256,1024]{1,0:T(8,128)(2,1)}, bf16[256,1024]{1,0:T(8,128)(2,1)S(1)}, u32[]{:S(2)}, u32[]{:S(2)}) collective-permute-start(bf16[256,1024]{1,0:T(8,128)(2,1)} %collective-permute-done.9.refs_3_), channel_id=1, source_target_pairs={{0,1},{1,0},{2,3},{3,2},{4,5},{5,4},{6,7},{7,6},{8,9},{9,8},{10,11... | collective-permute-start | bytes 1572872 | tf_op jit(solution)/shard_map/ppermute | solution.py:39
  51.8 5.2 %collective-permute-start.14 = (bf16[256,1024]{1,0:T(8,128)(2,1)}, bf16[256,1024]{1,0:T(8,128)(2,1)S(1)}, u32[]{:S(2)}, u32[]{:S(2)}) collective-permute-start(bf16[256,1024]{1,0:T(8,128)(2,1)} %collective-permute-done.10.refs_4_), channel_id=1, source_target_pairs={{0,1},{1,0},{2,3},{3,2},{4,5},{5,4},{6,7},{7,6},{8,9},{9,8},{10,11... | collective-permute-start | bytes 1572872 | tf_op jit(solution)/shard_map/ppermute | solution.py:39
  52.2 4.7 %copy-start.1 = (f32[1024,1024]{1,0:T(8,128)S(1)}, f32[1024,1024]{1,0:T(8,128)}, u32[]{:S(2)}) copy-start(f32[1024,1024]{1,0:T(8,128)} %self_part.1.base_ref) | copy-start | bytes 12582916
  52.3 4.8 %copy-start.7 = (bf16[1024,1024]{1,0:T(8,128)(2,1)S(1)}, bf16[1024,1024]{1,0:T(8,128)(2,1)}, u32[]{:S(2)}) copy-start(bf16[1024,1024]{1,0:T(8,128)(2,1)} %weight_ref.3) | copy-start | bytes 6291460
  (3 other events, 6.8 us)

commit v6 on v5

--- a/solution.py
+++ b/solution.py
@@ -148,7 +148,7 @@
         compiler_params=params(12),
         cost_estimate=cost(2 * NODES * NODES * D, 5 * MIB),
         name="messages",
-    )(send_count.reshape(8), far(send_rows), far(send_weight), far(node_feats))
+    )(far(send_count.reshape(8)), far(send_rows), far(send_weight), far(node_feats))
 
 
 FIRST_HALVES = len(FIRST)
@@ -247,12 +247,10 @@
 def self_kernel(feats_ref, weight_ref, bias_ref, out_ref, stage_ref, sems):
     copies = []
     for step in range(4):
-        lanes = slice(step * 256, (step + 1) * 256)
-        stage_ref[:, lanes] = (
-            product(feats_ref[...], weight_ref[:, lanes]) + bias_ref[0:1, lanes]
-        )
+        rows = slice(step * 256, (step + 1) * 256)
+        stage_ref[rows, :] = product(feats_ref[rows, :], weight_ref[...]) + bias_ref[0:1, :]
         copy = pltpu.make_async_copy(
-            stage_ref.at[:, lanes], out_ref.at[:, lanes], sems.at[step]
+            stage_ref.at[rows], out_ref.at[rows], sems.at[step]
         )
         copy.start()
         copies.append(copy)
@@ -283,11 +281,11 @@
         out_ref, stage_ref, sems = refs[-3:]
         copies = []
         for step in range(4):
-            lanes = slice(step * 256, (step + 1) * 256)
-            hubs = jnp.concatenate([ref[:, lanes] for ref in refs[: len(parts)]], axis=0)
-            stage_ref[:, lanes] = product(placed_ref[:, :width], hubs)
+            rows = slice(step * 256, (step + 1) * 256)
+            hubs = jnp.concatenate([ref[...] for ref in refs[: len(parts)]], axis=0)
+            stage_ref[rows, :] = product(placed_ref[rows, :width], hubs)
             copy = pltpu.make_async_copy(
-                stage_ref.at[:, lanes], out_ref.at[:, lanes], sems.at[step]
+                stage_ref.at[rows], out_ref.at[rows], sems.at[step]
             )
             copy.start()
             copies.append(copy)
@@ -300,7 +298,7 @@
         out_specs=FAR,
         out_shape=pltpu.HBM((NODES, D), jnp.float32),
         scratch_shapes=[pltpu.VMEM((NODES, D), jnp.float32), pltpu.SemaphoreType.DMA((4,))],
-        compiler_params=params(10),
+        compiler_params=params(16),
         cost_estimate=cost(int(3 * NODES * width * D), 15 * MIB),
         name="hub_products",
     )(near(placed), *[near(part) for part in parts])

time: 62.5 us -> 62 us (level)
  Pallas kernels: 34.3 us -> 33.5 us
  waiting for transfers between devices: 0.04 us -> 0.72 us
  local copies, waits for them, and re-layouts: 2.89 us -> 2.23 us
    unnamed x22 -> x20, local copies, waits for them, and re-layouts: 2.89 us -> 2.23 us
  transfers between devices with their start and end apart: 16 -> 16, of which waited for: 0 -> 2; matrix products, arithmetic and copies ran while one was open for 0% -> 0% of each run, Pallas kernels for 47% -> 46%
where the time goes in v6:
time: 62 us; the launch traced here: 61.7 us
  Pallas kernels  33.5 us (54%)
  starting transfers between devices  24.8 us (40%)
  local copies, waits for them, and re-layouts  2.23 us (4%)
  waiting for transfers between devices  0.72 us (1%)
    ppermute x15, starting transfers between devices, send(): return lax.ppermute(value, MESH_AXES, pairs)  20.7 us
    pallas_call x1, Pallas kernels, hub_products(): pl.pallas_call(body, in_specs=[ROWS] * (1 + len(parts)), out_specs=FAR, o...  6.89 us
    pallas_call x1, Pallas kernels, messages(): pl.pallas_call(message_kernel, in_specs=[WORDS, FAR, FAR, FAR], out_specs...  5.57 us
    pallas_call x1, Pallas kernels, last_part(): pl.pallas_call(body, in_specs=[ROWS] * (5 + len(parts)), out_specs=FAR, o...  5.03 us
    pallas_call x1, Pallas kernels, middle_part(): pl.pallas_call(body, in_specs=[ROWS] * (3 + len(parts)), out_specs=ROWS,...  4.7 us
    pallas_call x1, Pallas kernels, placed_tiles(): pl.pallas_call(place_kernel, in_specs=[WORDS, ROWS], out_specs=[ROWS, FAR...  4.23 us
    all_to_all x1, starting transfers between devices, shards(): lax.all_to_all(message, 'row', split_axis=0, concat_axis=0, tiled=True)  4.19 us
    pallas_call x1, Pallas kernels, tail_part(): pl.pallas_call(body, in_specs=[ROWS] * 2 + [FAR], out_specs=[ROWS, ROWS],...  3.54 us
  transfers between devices with their start and end apart: 16, of which 2 were waited for; matrix products, arithmetic and copies ran while one was open for 0% of the time, Pallas kernels for 46%

profile of v6, /device:TPU:1, one launch (start us, length us, event | category | flops | bytes accessed | tf_op | source)
XLA Modules:
  0.0 61.7 jit_solution(6470743743124691779)
XLA Ops:
  0.0 4.6 %collective-permute-start.1 = (bf16[256,1024]{1,0:T(8,128)(2,1)}, bf16[256,1024]{1,0:T(8,128)(2,1)S(1)}, u32[]{:S(2)}, u32[]{:S(2)}) collective-permute-start(bf16[256,1024]{1,0:T(8,128)(2,1)} %refs_0_.1), channel_id=1, source_target_pairs={{0,12},{1,13},{2,14},{3,15},{4,0},{5,1},{6,2},{7,3},{8,4},{9,5},{1... | collective-permute-start | bytes 1572872 | tf_op jit(solution)/shard_map/ppermute | solution.py:39
  4.6 2.5 %collective-permute-start.2 = (bf16[256,1024]{1,0:T(8,128)(2,1)}, bf16[256,1024]{1,0:T(8,128)(2,1)}, u32[]{:S(2)}, u32[]{:S(2)}) collective-permute-start(bf16[256,1024]{1,0:T(8,128)(2,1)} %refs_0_.1), channel_id=1, source_target_pairs={{0,18},{1,19},{2,16},{3,17},{4,22},{5,23},{6,20},{7,21},{8,26},{9,... | collective-permute-start | bytes 1572872 | tf_op jit(solution)/shard_map/ppermute | solution.py:39
  7.1 5.6 %messages.1 = bf16[8,136,1024]{2,1,0:T(8,128)(2,1)} custom-call(s32[8]{0:T(128)} %bitcast.5, s32[8,128]{1,0:T(8,128)} %rows_hbm.1, bf16[8,128]{1,0:T(8,128)(2,1)} %weight_hbm.1, bf16[1024,1024]{1,0:T(8,128)(2,1)} %feats_ref.1), custom_call_target="tpu_custom_call" | custom-call | flops 4294967296 | bytes 10485760 | tf_op jit(solution)/shard_map/messages/pallas_call | solution.py:135
  12.7 1.3 %collective-permute-start.3 = (bf16[256,1024]{1,0:T(8,128)(2,1)}, bf16[256,1024]{1,0:T(8,128)(2,1)}, u32[]{:S(2)}, u32[]{:S(2)}) collective-permute-start(bf16[256,1024]{1,0:T(8,128)(2,1)} %refs_0_.1), channel_id=1, source_target_pairs={{0,1},{1,0},{2,3},{3,2},{4,5},{5,4},{6,7},{7,6},{8,9},{9,8},{10,11... | collective-permute-start | bytes 1572872 | tf_op jit(solution)/shard_map/ppermute | solution.py:39
  14.0 4.2 %all-to-all-start = ((bf16[8,136,1024]{2,1,0:T(8,128)(2,1)}), bf16[8,136,1024]{2,1,0:T(8,128)(2,1)S(1)}, u32[]{:S(2)}, u32[]{:S(2)}) async-start(bf16[8,136,1024]{2,1,0:T(8,128)(2,1)} %messages.1), calls=%async_computation | async-start | bytes 4456448 | tf_op jit(solution)/shard_map/all_to_all | solution.py:432
  18.2 0.4 collective-permute-done.up_ref.refs_2_
  18.6 2.7 %collective-permute-start.4 = (bf16[256,1024]{1,0:T(8,128)(2,1)S(1)}, bf16[256,1024]{1,0:T(8,128)(2,1)}, u32[]{:S(2)}, u32[]{:S(2)}) collective-permute-start(bf16[256,1024]{1,0:T(8,128)(2,1)S(1)} %choose.1), channel_id=1, source_target_pairs={{0,4},{1,13},{2,6},{3,15},{4,8},{5,1},{6,10},{7,3},{8,12},{9,5},{1... | collective-permute-start | bytes 1572872 | tf_op jit(solution)/shard_map/ppermute | solution.py:39
  21.3 0.5 collective-permute-start.6
  21.9 2.2 %copy-done = bf16[128,128,128]{2,1,0:T(8,128)(2,1)S(1)} copy-done((bf16[128,128,128]{2,1,0:T(8,128)(2,1)S(1)}, bf16[128,128,128]{2,1,0:T(8,128)(2,1)}, u32[]{:S(2)}) %copy-start) | copy-done | bytes 4194328
  24.0 4.2 %placed_tiles.1 = (bf16[1024,2048]{1,0:T(8,128)(2,1)S(1)}, bf16[1024,2048]{1,0:T(8,128)(2,1)}, f32[1024,128]{1,0:T(8,128)}) custom-call(s32[128]{0:T(128)S(1)} %bitcast.4, bf16[128,128,128]{2,1,0:T(8,128)(2,1)S(1)} %copy-done), custom_call_target="tpu_custom_call" | custom-call | bytes 25165824 | tf_op jit(solution)/shard_map/placed_tiles/pallas_call | solution.py:187
  28.3 0.0 copy-start.2
  28.3 0.0 copy-start.3
  28.4 2.6 %collective-permute-start.9 = (bf16[256,1024]{1,0:T(8,128)(2,1)}, bf16[256,1024]{1,0:T(8,128)(2,1)}, u32[]{:S(2)}, u32[]{:S(2)}) collective-permute-start(bf16[256,1024]{1,0:T(8,128)(2,1)} %collective-permute-done.2.refs_1_), channel_id=1, source_target_pairs={{0,12},{1,13},{2,14},{3,15},{4,0},{5,1},{6,2},{7,3},{8,4},{9,5},{1... | collective-permute-start | bytes 1572872 | tf_op jit(solution)/shard_map/ppermute | solution.py:39
  31.0 2.2 %collective-permute-start.11 = (bf16[256,1024]{1,0:T(8,128)(2,1)}, bf16[256,1024]{1,0:T(8,128)(2,1)}, u32[]{:S(2)}, u32[]{:S(2)}) collective-permute-start(bf16[256,1024]{1,0:T(8,128)(2,1)} %collective-permute-done.4.refs_0_), channel_id=1, source_target_pairs={{0,1},{1,0},{2,3},{3,2},{4,5},{5,4},{6,7},{7,6},{8,9},{9,8},{10,11... | collective-permute-start | bytes 1572872 | tf_op jit(solution)/shard_map/ppermute | solution.py:39
  33.2 2.5 %collective-permute-start.10 = (bf16[256,1024]{1,0:T(8,128)(2,1)}, bf16[256,1024]{1,0:T(8,128)(2,1)}, u32[]{:S(2)}, u32[]{:S(2)}) collective-permute-start(bf16[256,1024]{1,0:T(8,128)(2,1)} %collective-permute-done.4.refs_0_), channel_id=1, source_target_pairs={{0,18},{1,19},{2,16},{3,17},{4,22},{5,23},{6,20},{7,21},{8,26},{9,... | collective-permute-start | bytes 1572872 | tf_op jit(solution)/shard_map/ppermute | solution.py:39
  35.7 6.9 %hub_products.1.carry_ref = f32[1024,1024]{1,0:T(8,128)} custom-call(bf16[1024,2048]{1,0:T(8,128)(2,1)S(1)} %get-tuple-element.45.placed_ref, bf16[256,1024]{1,0:T(8,128)(2,1)} %refs_0_.1, bf16[256,1024]{1,0:T(8,128)(2,1)} %collective-permute-done.2.refs_1_, bf16[256,1024]{1,0:T(8,128)(2,1)S(1)} %collective-permute-done.up_ref.refs_2_, ...), custom_call_target="tpu_custom_call" | custom-call | flops 12884901888 | bytes 31457280 | tf_op jit(solution)/shard_map/hub_products/pallas_call | solution.py:295
  42.6 3.5 %self_part.1.base_ref = f32[1024,1024]{1,0:T(8,128)} custom-call(bf16[1024,1024]{1,0:T(8,128)(2,1)S(1)} %copy-done.2, bf16[1024,1024]{1,0:T(8,128)(2,1)S(1)} %copy-done.3, f32[8,1024]{1,0:T(8,128)S(1)} %bias_rows.1.bias_ref), custom_call_target="tpu_custom_call" | custom-call | flops 2000 | bytes 2000 | tf_op jit(solution)/shard_map/self_part/pallas_call | solution.py:262
  46.1 0.3 all-to-all-done.got_ref
  46.4 3.5 %tail_part.1 = (f32[1024,1024]{1,0:T(8,128)S(1)}, f32[1024,128]{1,0:T(8,128)S(1)}) custom-call(s32[8,128]{1,0:T(8,128)S(1)} %copy-done.8, bf16[8,136,1024]{2,1,0:T(8,128)(2,1)S(1)} %all-to-all-done.got_ref, f32[1024,128]{1,0:T(8,128)} %get-tuple-element.33.sums_hbm), custom_call_target="tpu_custom_call" | custom-call | flops 4294967296 | bytes 20971520 | tf_op jit(solution)/shard_map/tail_part/pallas_call | solution.py:331
  50.0 1.2 %collective-permute-start.12 = (bf16[256,1024]{1,0:T(8,128)(2,1)}, bf16[256,1024]{1,0:T(8,128)(2,1)S(1)}, u32[]{:S(2)}, u32[]{:S(2)}) collective-permute-start(bf16[256,1024]{1,0:T(8,128)(2,1)} %collective-permute-done.8.refs_2_), channel_id=1, source_target_pairs={{0,1},{1,0},{2,3},{3,2},{4,5},{5,4},{6,7},{7,6},{8,9},{9,8},{10,11... | collective-permute-start | bytes 1572872 | tf_op jit(solution)/shard_map/ppermute | solution.py:39
  51.2 0.1 collective-permute-start.13
  51.3 0.4 collective-permute-start.14
  51.7 4.7 %middle_part.1.carry_ref = f32[1024,1024]{1,0:T(8,128)S(1)} custom-call(bf16[1024,2048]{1,0:T(8,128)(2,1)S(1)} %copy-done.6, f32[1024,1024]{1,0:T(8,128)S(1)} %copy-done.9, f32[1024,1024]{1,0:T(8,128)S(1)} %get-tuple-element.53.tail_ref, bf16[256,1024]{1,0:T(8,128)(2,1)} %collective-permute-done.4.refs_0_, ...), custom_call_target="tpu_custom_call" | custom-call | flops 5368709120 | bytes 20971520 | tf_op jit(solution)/shard_map/middle_part/pallas_call | solution.py:357
  56.5 5.0 %last_part.1 = bf16[1024,1024]{1,0:T(8,128)(2,1)} custom-call(f32[1024,128]{1,0:T(8,128)S(1)} %get-tuple-element.34.scale_ref, f32[1024,1024]{1,0:T(8,128)S(1)} %middle_part.1.carry_ref, f32[1024,1024]{1,0:T(8,128)S(1)} %copy-done.1, bf16[1024,1024]{1,0:T(8,128)(2,1)S(1)} %copy-done.7, bf16[1024,2048]{1,0:T(8,128)(2,1)S(1)} %copy-done.6, ...), custom_call_target="tpu_custom_call" | custom-call | flops 7516192768 | bytes 33554432 | tf_op jit(solution)/shard_map/last_part/pallas_call | solution.py:394
  (37 shorter events, 0.1 us)
Async XLA Ops:
  0.0 18.2 %collective-permute-start.1 = (bf16[256,1024]{1,0:T(8,128)(2,1)}, bf16[256,1024]{1,0:T(8,128)(2,1)S(1)}, u32[]{:S(2)}, u32[]{:S(2)}) collective-permute-start(bf16[256,1024]{1,0:T(8,128)(2,1)} %refs_0_.1), channel_id=1, source_target_pairs={{0,12},{1,13},{2,14},{3,15},{4,0},{5,1},{6,2},{7,3},{8,4},{9,5},{1... | collective-permute-start | bytes 1572872 | tf_op jit(solution)/shard_map/ppermute | solution.py:39
  4.6 14.0 %collective-permute-start = (bf16[256,1024]{1,0:T(8,128)(2,1)}, bf16[256,1024]{1,0:T(8,128)(2,1)S(1)}, u32[]{:S(2)}, u32[]{:S(2)}) collective-permute-start(bf16[256,1024]{1,0:T(8,128)(2,1)} %refs_0_.1), channel_id=1, source_target_pairs={{0,4},{1,5},{2,6},{3,7},{4,8},{5,9},{6,10},{7,11},{8,12},{9,13},{1... | collective-permute-start | bytes 1572872 | tf_op jit(solution)/shard_map/ppermute | solution.py:39
  4.6 14.0 %collective-permute-start.2 = (bf16[256,1024]{1,0:T(8,128)(2,1)}, bf16[256,1024]{1,0:T(8,128)(2,1)}, u32[]{:S(2)}, u32[]{:S(2)}) collective-permute-start(bf16[256,1024]{1,0:T(8,128)(2,1)} %refs_0_.1), channel_id=1, source_target_pairs={{0,18},{1,19},{2,16},{3,17},{4,22},{5,23},{6,20},{7,21},{8,26},{9,... | collective-permute-start | bytes 1572872 | tf_op jit(solution)/shard_map/ppermute | solution.py:39
  12.6 5.5 %copy-start.4 = (f32[1024]{0:T(1024)S(1)}, f32[1024]{0:T(1024)}, u32[]{:S(2)}) copy-start(f32[1024]{0:T(1024)} %param.15) | copy-start | bytes 12292
  12.7 9.2 %copy-start.5 = (s32[1,128]{1,0:T(1,128)S(1)}, s32[1,128]{1,0:T(1,128)}, u32[]{:S(2)}) copy-start(s32[1,128]{1,0:T(1,128)} %param.17) | copy-start | bytes 1540
  12.7 5.9 %collective-permute-start.3 = (bf16[256,1024]{1,0:T(8,128)(2,1)}, bf16[256,1024]{1,0:T(8,128)(2,1)}, u32[]{:S(2)}, u32[]{:S(2)}) collective-permute-start(bf16[256,1024]{1,0:T(8,128)(2,1)} %refs_0_.1), channel_id=1, source_target_pairs={{0,1},{1,0},{2,3},{3,2},{4,5},{5,4},{6,7},{7,6},{8,9},{9,8},{10,11... | collective-permute-start | bytes 1572872 | tf_op jit(solution)/shard_map/ppermute | solution.py:39
  14.0 32.4 %all-to-all-start = ((bf16[8,136,1024]{2,1,0:T(8,128)(2,1)}), bf16[8,136,1024]{2,1,0:T(8,128)(2,1)S(1)}, u32[]{:S(2)}, u32[]{:S(2)}) async-start(bf16[8,136,1024]{2,1,0:T(8,128)(2,1)} %messages.1), calls=%async_computation | async-start | bytes 4456448 | tf_op jit(solution)/shard_map/all_to_all | solution.py:432
  18.6 9.7 %collective-permute-start.4 = (bf16[256,1024]{1,0:T(8,128)(2,1)S(1)}, bf16[256,1024]{1,0:T(8,128)(2,1)}, u32[]{:S(2)}, u32[]{:S(2)}) collective-permute-start(bf16[256,1024]{1,0:T(8,128)(2,1)S(1)} %choose.1), channel_id=1, source_target_pairs={{0,4},{1,13},{2,6},{3,15},{4,8},{5,1},{6,10},{7,3},{8,12},{9,5},{1... | collective-permute-start | bytes 1572872 | tf_op jit(solution)/shard_map/ppermute | solution.py:39
  21.3 7.0 %collective-permute-start.5 = (bf16[256,1024]{1,0:T(8,128)(2,1)}, bf16[256,1024]{1,0:T(8,128)(2,1)S(1)}, u32[]{:S(2)}, u32[]{:S(2)}) collective-permute-start(bf16[256,1024]{1,0:T(8,128)(2,1)} %collective-permute-done.2.refs_1_), channel_id=1, source_target_pairs={{0,1},{1,0},{2,3},{3,2},{4,5},{5,4},{6,7},{7,6},{8,9},{9,8},{10,11... | collective-permute-start | bytes 1572872 | tf_op jit(solution)/shard_map/ppermute | solution.py:39
  21.3 7.0 %collective-permute-start.6 = (bf16[256,1024]{1,0:T(8,128)(2,1)S(1)}, bf16[256,1024]{1,0:T(8,128)(2,1)S(1)}, u32[]{:S(2)}, u32[]{:S(2)}) collective-permute-start(bf16[256,1024]{1,0:T(8,128)(2,1)S(1)} %collective-permute-done.up_ref.refs_2_), channel_id=1, source_target_pairs={{0,1},{1,0},{2,3},{3,2},{4,5},{5,4},{6,7},{7,6},{8,9},{9,8},{10,11... | collective-permute-start | bytes 1572872 | tf_op jit(solution)/shard_map/ppermute | solution.py:39
  21.9 6.5 %collective-permute-start.7 = (bf16[256,1024]{1,0:T(8,128)(2,1)S(1)}, bf16[256,1024]{1,0:T(8,128)(2,1)S(1)}, u32[]{:S(2)}, u32[]{:S(2)}) collective-permute-start(bf16[256,1024]{1,0:T(8,128)(2,1)S(1)} %collective-permute-done.1.down_ref.refs_3_), channel_id=1, source_target_pairs={{0,1},{1,0},{2,3},{3,2},{4,5},{5,4},{6,7},{7,6},{8,9},{9,8},{10,11... | collective-permute-start | bytes 1572872 | tf_op jit(solution)/shard_map/ppermute | solution.py:39
  28.3 14.3 %copy-start.2 = (bf16[1024,1024]{1,0:T(8,128)(2,1)S(1)}, bf16[1024,1024]{1,0:T(8,128)(2,1)}, u32[]{:S(2)}) copy-start(bf16[1024,1024]{1,0:T(8,128)(2,1)} %feats_ref.1) | copy-start | bytes 6291460
  28.3 14.2 %copy-start.3 = (bf16[1024,1024]{1,0:T(8,128)(2,1)S(1)}, bf16[1024,1024]{1,0:T(8,128)(2,1)}, u32[]{:S(2)}) copy-start(bf16[1024,1024]{1,0:T(8,128)(2,1)} %weight_ref.2) | copy-start | bytes 6291460
  28.4 21.6 %collective-permute-start.9 = (bf16[256,1024]{1,0:T(8,128)(2,1)}, bf16[256,1024]{1,0:T(8,128)(2,1)}, u32[]{:S(2)}, u32[]{:S(2)}) collective-permute-start(bf16[256,1024]{1,0:T(8,128)(2,1)} %collective-permute-done.2.refs_1_), channel_id=1, source_target_pairs={{0,12},{1,13},{2,14},{3,15},{4,0},{5,1},{6,2},{7,3},{8,4},{9,5},{1... | collective-permute-start | bytes 1572872 | tf_op jit(solution)/shard_map/ppermute | solution.py:39
  31.0 19.0 %collective-permute-start.8 = (bf16[256,1024]{1,0:T(8,128)(2,1)}, bf16[256,1024]{1,0:T(8,128)(2,1)}, u32[]{:S(2)}, u32[]{:S(2)}) collective-permute-start(bf16[256,1024]{1,0:T(8,128)(2,1)} %collective-permute-done.2.refs_1_), channel_id=1, source_target_pairs={{0,4},{1,5},{2,6},{3,7},{4,8},{5,9},{6,10},{7,11},{8,12},{9,13},{1... | collective-permute-start | bytes 1572872 | tf_op jit(solution)/shard_map/ppermute | solution.py:39
  31.0 19.0 %collective-permute-start.11 = (bf16[256,1024]{1,0:T(8,128)(2,1)}, bf16[256,1024]{1,0:T(8,128)(2,1)}, u32[]{:S(2)}, u32[]{:S(2)}) collective-permute-start(bf16[256,1024]{1,0:T(8,128)(2,1)} %collective-permute-done.4.refs_0_), channel_id=1, source_target_pairs={{0,1},{1,0},{2,3},{3,2},{4,5},{5,4},{6,7},{7,6},{8,9},{9,8},{10,11... | collective-permute-start | bytes 1572872 | tf_op jit(solution)/shard_map/ppermute | solution.py:39
  33.2 16.8 %collective-permute-start.10 = (bf16[256,1024]{1,0:T(8,128)(2,1)}, bf16[256,1024]{1,0:T(8,128)(2,1)}, u32[]{:S(2)}, u32[]{:S(2)}) collective-permute-start(bf16[256,1024]{1,0:T(8,128)(2,1)} %collective-permute-done.4.refs_0_), channel_id=1, source_target_pairs={{0,18},{1,19},{2,16},{3,17},{4,22},{5,23},{6,20},{7,21},{8,26},{9,... | collective-permute-start | bytes 1572872 | tf_op jit(solution)/shard_map/ppermute | solution.py:39
  46.4 5.3 %copy-start.6 = (bf16[1024,2048]{1,0:T(8,128)(2,1)S(1)}, bf16[1024,2048]{1,0:T(8,128)(2,1)}, u32[]{:S(2)}) copy-start(bf16[1024,2048]{1,0:T(8,128)(2,1)} %get-tuple-element.35.placed_ref) | copy-start | bytes 12582916
  46.4 5.3 %copy-start.9 = (f32[1024,1024]{1,0:T(8,128)S(1)}, f32[1024,1024]{1,0:T(8,128)}, u32[]{:S(2)}) copy-start(f32[1024,1024]{1,0:T(8,128)} %hub_products.1.carry_ref) | copy-start | bytes 12582916
  50.0 6.4 %collective-permute-start.12 = (bf16[256,1024]{1,0:T(8,128)(2,1)}, bf16[256,1024]{1,0:T(8,128)(2,1)S(1)}, u32[]{:S(2)}, u32[]{:S(2)}) collective-permute-start(bf16[256,1024]{1,0:T(8,128)(2,1)} %collective-permute-done.8.refs_2_), channel_id=1, source_target_pairs={{0,1},{1,0},{2,3},{3,2},{4,5},{5,4},{6,7},{7,6},{8,9},{9,8},{10,11... | collective-permute-start | bytes 1572872 | tf_op jit(solution)/shard_map/ppermute | solution.py:39
  51.2 5.2 %collective-permute-start.13 = (bf16[256,1024]{1,0:T(8,128)(2,1)}, bf16[256,1024]{1,0:T(8,128)(2,1)S(1)}, u32[]{:S(2)}, u32[]{:S(2)}) collective-permute-start(bf16[256,1024]{1,0:T(8,128)(2,1)} %collective-permute-done.9.refs_3_), channel_id=1, source_target_pairs={{0,1},{1,0},{2,3},{3,2},{4,5},{5,4},{6,7},{7,6},{8,9},{9,8},{10,11... | collective-permute-start | bytes 1572872 | tf_op jit(solution)/shard_map/ppermute | solution.py:39
  51.3 5.2 %collective-permute-start.14 = (bf16[256,1024]{1,0:T(8,128)(2,1)}, bf16[256,1024]{1,0:T(8,128)(2,1)S(1)}, u32[]{:S(2)}, u32[]{:S(2)}) collective-permute-start(bf16[256,1024]{1,0:T(8,128)(2,1)} %collective-permute-done.10.refs_4_), channel_id=1, source_target_pairs={{0,1},{1,0},{2,3},{3,2},{4,5},{5,4},{6,7},{7,6},{8,9},{9,8},{10,11... | collective-permute-start | bytes 1572872 | tf_op jit(solution)/shard_map/ppermute | solution.py:39
  51.7 4.7 %copy-start.1 = (f32[1024,1024]{1,0:T(8,128)S(1)}, f32[1024,1024]{1,0:T(8,128)}, u32[]{:S(2)}) copy-start(f32[1024,1024]{1,0:T(8,128)} %self_part.1.base_ref) | copy-start | bytes 12582916
  51.7 4.8 %copy-start.7 = (bf16[1024,1024]{1,0:T(8,128)(2,1)S(1)}, bf16[1024,1024]{1,0:T(8,128)(2,1)}, u32[]{:S(2)}) copy-start(bf16[1024,1024]{1,0:T(8,128)(2,1)} %weight_ref.3) | copy-start | bytes 6291460
  (2 other events, 6.0 us)

commit v7 on v6

--- a/solution.py
+++ b/solution.py
@@ -451,12 +451,14 @@
     )
 
     base = self_part(node_feats, self_weight, bias)
+    two_x, base, carry = lax.optimization_barrier((two_x, base, carry))
+    two_xc = send(two_x, CORE)
     tail, scale = tail_part(sums, arrive_node, arrived)
 
-    up_x, down_x, two_x, two_c, carry, tail, base = lax.optimization_barrier(
-        (up_x, down_x, two_x, two_c, carry, tail, base)
-    )
-    late = [send(part, CORE) for part in (up_x, down_x, two_x)]
+    up_x, down_x, two_x, two_xc, two_c, carry, tail = lax.optimization_barrier(
+        (up_x, down_x, two_x, two_xc, two_c, carry, tail)
+    )
+    late = [send(up_x, CORE), send(down_x, CORE), two_xc]
     carry = middle_part(placed_later, [two, two_c, up_x, down_x, two_x], carry, tail)
     return last_part(placed_later, late, scale, carry, base, neigh_weight)
 

time: 62 us -> 63.5 us (1.024)
  waiting for transfers between devices: 0.72 us -> 2.62 us
    ppermute x15, waiting for transfers between devices: 0.41 us -> 2.61 us  [send(): return lax.ppermute(value, MESH_AXES, pairs)]
  transfers between devices with their start and end apart: 16 -> 16, of which waited for: 2 -> 2; matrix products, arithmetic and copies ran while one was open for 0% -> 0% of each run, Pallas kernels for 46% -> 45%
where the time goes in v7:
time: 63.5 us; the launch traced here: 63.2 us
  Pallas kernels  33.4 us (53%)
  starting transfers between devices  24.5 us (39%)
  waiting for transfers between devices  2.62 us (4%)
  local copies, waits for them, and re-layouts  2.23 us (4%)
    ppermute x15, starting transfers between devices, send(): return lax.ppermute(value, MESH_AXES, pairs)  20.3 us
    pallas_call x1, Pallas kernels, hub_products(): pl.pallas_call(body, in_specs=[ROWS] * (1 + len(parts)), out_specs=FAR, o...  6.89 us
    pallas_call x1, Pallas kernels, messages(): pl.pallas_call(message_kernel, in_specs=[WORDS, FAR, FAR, FAR], out_specs...  5.57 us
    pallas_call x1, Pallas kernels, last_part(): pl.pallas_call(body, in_specs=[ROWS] * (5 + len(parts)), out_specs=FAR, o...  5.03 us
    pallas_call x1, Pallas kernels, middle_part(): pl.pallas_call(body, in_specs=[ROWS] * (3 + len(parts)), out_specs=ROWS,...  4.7 us
    pallas_call x1, Pallas kernels, placed_tiles(): pl.pallas_call(place_kernel, in_specs=[WORDS, ROWS], out_specs=[ROWS, FAR...  4.23 us
    all_to_all x1, starting transfers between devices, shards(): lax.all_to_all(message, 'row', split_axis=0, concat_axis=0, tiled=True)  4.19 us
    pallas_call x1, Pallas kernels, tail_part(): pl.pallas_call(body, in_specs=[ROWS] * 2 + [FAR], out_specs=[ROWS, ROWS],...  3.53 us
  transfers between devices with their start and end apart: 16, of which 2 were waited for; matrix products, arithmetic and copies ran while one was open for 0% of the time, Pallas kernels for 45%

profile of v7, /device:TPU:1, one launch (start us, length us, event | category | flops | bytes accessed | tf_op | source)
XLA Modules:
  0.0 63.2 jit_solution(12846397954149829521)
XLA Ops:
  0.0 4.6 %collective-permute-start.1 = (bf16[256,1024]{1,0:T(8,128)(2,1)}, bf16[256,1024]{1,0:T(8,128)(2,1)S(1)}, u32[]{:S(2)}, u32[]{:S(2)}) collective-permute-start(bf16[256,1024]{1,0:T(8,128)(2,1)} %refs_0_.1), channel_id=1, source_target_pairs={{0,12},{1,13},{2,14},{3,15},{4,0},{5,1},{6,2},{7,3},{8,4},{9,5},{1... | collective-permute-start | bytes 1572872 | tf_op jit(solution)/shard_map/ppermute | solution.py:39
  4.6 2.5 %collective-permute-start.2 = (bf16[256,1024]{1,0:T(8,128)(2,1)}, bf16[256,1024]{1,0:T(8,128)(2,1)}, u32[]{:S(2)}, u32[]{:S(2)}) collective-permute-start(bf16[256,1024]{1,0:T(8,128)(2,1)} %refs_0_.1), channel_id=1, source_target_pairs={{0,18},{1,19},{2,16},{3,17},{4,22},{5,23},{6,20},{7,21},{8,26},{9,... | collective-permute-start | bytes 1572872 | tf_op jit(solution)/shard_map/ppermute | solution.py:39
  7.1 5.6 %messages.1 = bf16[8,136,1024]{2,1,0:T(8,128)(2,1)} custom-call(s32[8]{0:T(128)} %bitcast.5, s32[8,128]{1,0:T(8,128)} %rows_hbm.1, bf16[8,128]{1,0:T(8,128)(2,1)} %weight_hbm.1, bf16[1024,1024]{1,0:T(8,128)(2,1)} %feats_ref.1), custom_call_target="tpu_custom_call" | custom-call | flops 4294967296 | bytes 10485760 | tf_op jit(solution)/shard_map/messages/pallas_call | solution.py:135
  12.6 0.0 copy-start.4
  12.7 0.0 copy-start.5
  12.7 1.3 %collective-permute-start.3 = (bf16[256,1024]{1,0:T(8,128)(2,1)}, bf16[256,1024]{1,0:T(8,128)(2,1)}, u32[]{:S(2)}, u32[]{:S(2)}) collective-permute-start(bf16[256,1024]{1,0:T(8,128)(2,1)} %refs_0_.1), channel_id=1, source_target_pairs={{0,1},{1,0},{2,3},{3,2},{4,5},{5,4},{6,7},{7,6},{8,9},{9,8},{10,11... | collective-permute-start | bytes 1572872 | tf_op jit(solution)/shard_map/ppermute | solution.py:39
  14.0 4.2 %all-to-all-start = ((bf16[8,136,1024]{2,1,0:T(8,128)(2,1)}), bf16[8,136,1024]{2,1,0:T(8,128)(2,1)S(1)}, u32[]{:S(2)}, u32[]{:S(2)}) async-start(bf16[8,136,1024]{2,1,0:T(8,128)(2,1)} %messages.1), calls=%async_computation | async-start | bytes 4456448 | tf_op jit(solution)/shard_map/all_to_all | solution.py:432
  18.2 0.4 collective-permute-done.up_ref.refs_2_
  18.6 2.7 %collective-permute-start.4 = (bf16[256,1024]{1,0:T(8,128)(2,1)S(1)}, bf16[256,1024]{1,0:T(8,128)(2,1)}, u32[]{:S(2)}, u32[]{:S(2)}) collective-permute-start(bf16[256,1024]{1,0:T(8,128)(2,1)S(1)} %choose.1), channel_id=1, source_target_pairs={{0,4},{1,13},{2,6},{3,15},{4,8},{5,1},{6,10},{7,3},{8,12},{9,5},{1... | collective-permute-start | bytes 1572872 | tf_op jit(solution)/shard_map/ppermute | solution.py:39
  21.3 0.5 collective-permute-start.6
  21.9 2.2 %copy-done = bf16[128,128,128]{2,1,0:T(8,128)(2,1)S(1)} copy-done((bf16[128,128,128]{2,1,0:T(8,128)(2,1)S(1)}, bf16[128,128,128]{2,1,0:T(8,128)(2,1)}, u32[]{:S(2)}) %copy-start) | copy-done | bytes 4194328
  24.0 4.2 %placed_tiles.1 = (bf16[1024,2048]{1,0:T(8,128)(2,1)S(1)}, bf16[1024,2048]{1,0:T(8,128)(2,1)}, f32[1024,128]{1,0:T(8,128)}) custom-call(s32[128]{0:T(128)S(1)} %bitcast.4, bf16[128,128,128]{2,1,0:T(8,128)(2,1)S(1)} %copy-done), custom_call_target="tpu_custom_call" | custom-call | bytes 25165824 | tf_op jit(solution)/shard_map/placed_tiles/pallas_call | solution.py:187
  28.4 2.6 %collective-permute-start.9 = (bf16[256,1024]{1,0:T(8,128)(2,1)}, bf16[256,1024]{1,0:T(8,128)(2,1)}, u32[]{:S(2)}, u32[]{:S(2)}) collective-permute-start(bf16[256,1024]{1,0:T(8,128)(2,1)} %collective-permute-done.2.refs_1_), channel_id=1, source_target_pairs={{0,12},{1,13},{2,14},{3,15},{4,0},{5,1},{6,2},{7,3},{8,4},{9,5},{1... | collective-permute-start | bytes 1572872 | tf_op jit(solution)/shard_map/ppermute | solution.py:39
  31.0 2.2 %collective-permute-start.12 = (bf16[256,1024]{1,0:T(8,128)(2,1)}, bf16[256,1024]{1,0:T(8,128)(2,1)}, u32[]{:S(2)}, u32[]{:S(2)}) collective-permute-start(bf16[256,1024]{1,0:T(8,128)(2,1)} %collective-permute-done.4.refs_0_), channel_id=1, source_target_pairs={{0,1},{1,0},{2,3},{3,2},{4,5},{5,4},{6,7},{7,6},{8,9},{9,8},{10,11... | collective-permute-start | bytes 1572872 | tf_op jit(solution)/shard_map/ppermute | solution.py:39
  33.2 2.5 %collective-permute-start.10 = (bf16[256,1024]{1,0:T(8,128)(2,1)}, bf16[256,1024]{1,0:T(8,128)(2,1)}, u32[]{:S(2)}, u32[]{:S(2)}) collective-permute-start(bf16[256,1024]{1,0:T(8,128)(2,1)} %collective-permute-done.4.refs_0_), channel_id=1, source_target_pairs={{0,18},{1,19},{2,16},{3,17},{4,22},{5,23},{6,20},{7,21},{8,26},{9,... | collective-permute-start | bytes 1572872 | tf_op jit(solution)/shard_map/ppermute | solution.py:39
  35.7 6.9 %hub_products.1.carry_ref = f32[1024,1024]{1,0:T(8,128)} custom-call(bf16[1024,2048]{1,0:T(8,128)(2,1)S(1)} %get-tuple-element.49.placed_ref, bf16[256,1024]{1,0:T(8,128)(2,1)} %refs_0_.1, bf16[256,1024]{1,0:T(8,128)(2,1)} %collective-permute-done.2.refs_1_, bf16[256,1024]{1,0:T(8,128)(2,1)S(1)} %collective-permute-done.up_ref.refs_2_, ...), custom_call_target="tpu_custom_call" | custom-call | flops 12884901888 | bytes 31457280 | tf_op jit(solution)/shard_map/hub_products/pallas_call | solution.py:295
  42.6 3.5 %self_part.1.base_ref = f32[1024,1024]{1,0:T(8,128)} custom-call(bf16[1024,1024]{1,0:T(8,128)(2,1)S(1)} %copy-done.2, bf16[1024,1024]{1,0:T(8,128)(2,1)S(1)} %copy-done.3, f32[8,1024]{1,0:T(8,128)S(1)} %bias_rows.1.bias_ref), custom_call_target="tpu_custom_call" | custom-call | flops 2000 | bytes 2000 | tf_op jit(solution)/shard_map/self_part/pallas_call | solution.py:262
  46.1 2.2 %collective-permute-done.10.refs_4_ = bf16[256,1024]{1,0:T(8,128)(2,1)} collective-permute-done((bf16[256,1024]{1,0:T(8,128)(2,1)}, bf16[256,1024]{1,0:T(8,128)(2,1)}, u32[]{:S(2)}, u32[]{:S(2)}) %collective-permute-start.10) | collective-permute-done | bytes 524320 | tf_op jit(solution)/shard_map/ppermute | solution.py:39
  48.3 0.8 %collective-permute-start.11 = (bf16[256,1024]{1,0:T(8,128)(2,1)}, bf16[256,1024]{1,0:T(8,128)(2,1)S(1)}, u32[]{:S(2)}, u32[]{:S(2)}) collective-permute-start(bf16[256,1024]{1,0:T(8,128)(2,1)} %collective-permute-done.10.refs_4_), channel_id=1, source_target_pairs={{0,1},{1,0},{2,3},{3,2},{4,5},{5,4},{6,7},{7,6},{8,9},{9,8},{10,11... | collective-permute-start | bytes 1572872 | tf_op jit(solution)/shard_map/ppermute | solution.py:39
  49.1 3.5 %tail_part.1 = (f32[1024,1024]{1,0:T(8,128)S(1)}, f32[1024,128]{1,0:T(8,128)S(1)}) custom-call(s32[8,128]{1,0:T(8,128)S(1)} %copy-done.8, bf16[8,136,1024]{2,1,0:T(8,128)(2,1)S(1)} %all-to-all-done.got_ref, f32[1024,128]{1,0:T(8,128)} %get-tuple-element.36.sums_hbm), custom_call_target="tpu_custom_call" | custom-call | flops 4294967296 | bytes 20971520 | tf_op jit(solution)/shard_map/tail_part/pallas_call | solution.py:331
  52.7 0.1 collective-permute-start.13
  52.8 0.5 collective-permute-start.14
  53.3 4.7 %middle_part.1.carry_ref = f32[1024,1024]{1,0:T(8,128)S(1)} custom-call(bf16[1024,2048]{1,0:T(8,128)(2,1)S(1)} %copy-done.6, f32[1024,1024]{1,0:T(8,128)S(1)} %copy-done.9, f32[1024,1024]{1,0:T(8,128)S(1)} %get-tuple-element.58.tail_ref, bf16[256,1024]{1,0:T(8,128)(2,1)} %collective-permute-done.4.refs_0_, ...), custom_call_target="tpu_custom_call" | custom-call | flops 5368709120 | bytes 20971520 | tf_op jit(solution)/shard_map/middle_part/pallas_call | solution.py:357
  58.0 5.0 %last_part.1 = bf16[1024,1024]{1,0:T(8,128)(2,1)} custom-call(f32[1024,128]{1,0:T(8,128)S(1)} %get-tuple-element.37.scale_ref, f32[1024,1024]{1,0:T(8,128)S(1)} %middle_part.1.carry_ref, f32[1024,1024]{1,0:T(8,128)S(1)} %copy-done.1, bf16[1024,1024]{1,0:T(8,128)(2,1)S(1)} %copy-done.7, bf16[1024,2048]{1,0:T(8,128)(2,1)S(1)} %copy-done.6, ...), custom_call_target="tpu_custom_call" | custom-call | flops 7516192768 | bytes 33554432 | tf_op jit(solution)/shard_map/last_part/pallas_call | solution.py:394
  (37 shorter events, 0.1 us)
Async XLA Ops:
  0.0 18.2 %collective-permute-start.1 = (bf16[256,1024]{1,0:T(8,128)(2,1)}, bf16[256,1024]{1,0:T(8,128)(2,1)S(1)}, u32[]{:S(2)}, u32[]{:S(2)}) collective-permute-start(bf16[256,1024]{1,0:T(8,128)(2,1)} %refs_0_.1), channel_id=1, source_target_pairs={{0,12},{1,13},{2,14},{3,15},{4,0},{5,1},{6,2},{7,3},{8,4},{9,5},{1... | collective-permute-start | bytes 1572872 | tf_op jit(solution)/shard_map/ppermute | solution.py:39
  4.6 14.0 %collective-permute-start = (bf16[256,1024]{1,0:T(8,128)(2,1)}, bf16[256,1024]{1,0:T(8,128)(2,1)S(1)}, u32[]{:S(2)}, u32[]{:S(2)}) collective-permute-start(bf16[256,1024]{1,0:T(8,128)(2,1)} %refs_0_.1), channel_id=1, source_target_pairs={{0,4},{1,5},{2,6},{3,7},{4,8},{5,9},{6,10},{7,11},{8,12},{9,13},{1... | collective-permute-start | bytes 1572872 | tf_op jit(solution)/shard_map/ppermute | solution.py:39
  4.6 14.0 %collective-permute-start.2 = (bf16[256,1024]{1,0:T(8,128)(2,1)}, bf16[256,1024]{1,0:T(8,128)(2,1)}, u32[]{:S(2)}, u32[]{:S(2)}) collective-permute-start(bf16[256,1024]{1,0:T(8,128)(2,1)} %refs_0_.1), channel_id=1, source_target_pairs={{0,18},{1,19},{2,16},{3,17},{4,22},{5,23},{6,20},{7,21},{8,26},{9,... | collective-permute-start | bytes 1572872 | tf_op jit(solution)/shard_map/ppermute | solution.py:39
  12.6 5.5 %copy-start.4 = (f32[1024]{0:T(1024)S(1)}, f32[1024]{0:T(1024)}, u32[]{:S(2)}) copy-start(f32[1024]{0:T(1024)} %param.15) | copy-start | bytes 12292
  12.7 9.2 %copy-start.5 = (s32[1,128]{1,0:T(1,128)S(1)}, s32[1,128]{1,0:T(1,128)}, u32[]{:S(2)}) copy-start(s32[1,128]{1,0:T(1,128)} %param.17) | copy-start | bytes 1540
  12.7 5.9 %collective-permute-start.3 = (bf16[256,1024]{1,0:T(8,128)(2,1)}, bf16[256,1024]{1,0:T(8,128)(2,1)}, u32[]{:S(2)}, u32[]{:S(2)}) collective-permute-start(bf16[256,1024]{1,0:T(8,128)(2,1)} %refs_0_.1), channel_id=1, source_target_pairs={{0,1},{1,0},{2,3},{3,2},{4,5},{5,4},{6,7},{7,6},{8,9},{9,8},{10,11... | collective-permute-start | bytes 1572872 | tf_op jit(solution)/shard_map/ppermute | solution.py:39
  14.0 35.1 %all-to-all-start = ((bf16[8,136,1024]{2,1,0:T(8,128)(2,1)}), bf16[8,136,1024]{2,1,0:T(8,128)(2,1)S(1)}, u32[]{:S(2)}, u32[]{:S(2)}) async-start(bf16[8,136,1024]{2,1,0:T(8,128)(2,1)} %messages.1), calls=%async_computation | async-start | bytes 4456448 | tf_op jit(solution)/shard_map/all_to_all | solution.py:432
  18.6 9.7 %collective-permute-start.4 = (bf16[256,1024]{1,0:T(8,128)(2,1)S(1)}, bf16[256,1024]{1,0:T(8,128)(2,1)}, u32[]{:S(2)}, u32[]{:S(2)}) collective-permute-start(bf16[256,1024]{1,0:T(8,128)(2,1)S(1)} %choose.1), channel_id=1, source_target_pairs={{0,4},{1,13},{2,6},{3,15},{4,8},{5,1},{6,10},{7,3},{8,12},{9,5},{1... | collective-permute-start | bytes 1572872 | tf_op jit(solution)/shard_map/ppermute | solution.py:39
  21.3 7.0 %collective-permute-start.5 = (bf16[256,1024]{1,0:T(8,128)(2,1)}, bf16[256,1024]{1,0:T(8,128)(2,1)S(1)}, u32[]{:S(2)}, u32[]{:S(2)}) collective-permute-start(bf16[256,1024]{1,0:T(8,128)(2,1)} %collective-permute-done.2.refs_1_), channel_id=1, source_target_pairs={{0,1},{1,0},{2,3},{3,2},{4,5},{5,4},{6,7},{7,6},{8,9},{9,8},{10,11... | collective-permute-start | bytes 1572872 | tf_op jit(solution)/shard_map/ppermute | solution.py:39
  21.3 7.0 %collective-permute-start.6 = (bf16[256,1024]{1,0:T(8,128)(2,1)S(1)}, bf16[256,1024]{1,0:T(8,128)(2,1)S(1)}, u32[]{:S(2)}, u32[]{:S(2)}) collective-permute-start(bf16[256,1024]{1,0:T(8,128)(2,1)S(1)} %collective-permute-done.up_ref.refs_2_), channel_id=1, source_target_pairs={{0,1},{1,0},{2,3},{3,2},{4,5},{5,4},{6,7},{7,6},{8,9},{9,8},{10,11... | collective-permute-start | bytes 1572872 | tf_op jit(solution)/shard_map/ppermute | solution.py:39
  21.9 6.5 %collective-permute-start.7 = (bf16[256,1024]{1,0:T(8,128)(2,1)S(1)}, bf16[256,1024]{1,0:T(8,128)(2,1)S(1)}, u32[]{:S(2)}, u32[]{:S(2)}) collective-permute-start(bf16[256,1024]{1,0:T(8,128)(2,1)S(1)} %collective-permute-done.1.down_ref.refs_3_), channel_id=1, source_target_pairs={{0,1},{1,0},{2,3},{3,2},{4,5},{5,4},{6,7},{7,6},{8,9},{9,8},{10,11... | collective-permute-start | bytes 1572872 | tf_op jit(solution)/shard_map/ppermute | solution.py:39
  28.3 14.3 %copy-start.2 = (bf16[1024,1024]{1,0:T(8,128)(2,1)S(1)}, bf16[1024,1024]{1,0:T(8,128)(2,1)}, u32[]{:S(2)}) copy-start(bf16[1024,1024]{1,0:T(8,128)(2,1)} %feats_ref.1) | copy-start | bytes 6291460
  28.3 14.2 %copy-start.3 = (bf16[1024,1024]{1,0:T(8,128)(2,1)S(1)}, bf16[1024,1024]{1,0:T(8,128)(2,1)}, u32[]{:S(2)}) copy-start(bf16[1024,1024]{1,0:T(8,128)(2,1)} %weight_ref.2) | copy-start | bytes 6291460
  28.4 24.3 %collective-permute-start.9 = (bf16[256,1024]{1,0:T(8,128)(2,1)}, bf16[256,1024]{1,0:T(8,128)(2,1)}, u32[]{:S(2)}, u32[]{:S(2)}) collective-permute-start(bf16[256,1024]{1,0:T(8,128)(2,1)} %collective-permute-done.2.refs_1_), channel_id=1, source_target_pairs={{0,12},{1,13},{2,14},{3,15},{4,0},{5,1},{6,2},{7,3},{8,4},{9,5},{1... | collective-permute-start | bytes 1572872 | tf_op jit(solution)/shard_map/ppermute | solution.py:39
  31.0 21.7 %collective-permute-start.8 = (bf16[256,1024]{1,0:T(8,128)(2,1)}, bf16[256,1024]{1,0:T(8,128)(2,1)}, u32[]{:S(2)}, u32[]{:S(2)}) collective-permute-start(bf16[256,1024]{1,0:T(8,128)(2,1)} %collective-permute-done.2.refs_1_), channel_id=1, source_target_pairs={{0,4},{1,5},{2,6},{3,7},{4,8},{5,9},{6,10},{7,11},{8,12},{9,13},{1... | collective-permute-start | bytes 1572872 | tf_op jit(solution)/shard_map/ppermute | solution.py:39
  31.0 21.7 %collective-permute-start.12 = (bf16[256,1024]{1,0:T(8,128)(2,1)}, bf16[256,1024]{1,0:T(8,128)(2,1)}, u32[]{:S(2)}, u32[]{:S(2)}) collective-permute-start(bf16[256,1024]{1,0:T(8,128)(2,1)} %collective-permute-done.4.refs_0_), channel_id=1, source_target_pairs={{0,1},{1,0},{2,3},{3,2},{4,5},{5,4},{6,7},{7,6},{8,9},{9,8},{10,11... | collective-permute-start | bytes 1572872 | tf_op jit(solution)/shard_map/ppermute | solution.py:39
  33.2 15.1 %collective-permute-start.10 = (bf16[256,1024]{1,0:T(8,128)(2,1)}, bf16[256,1024]{1,0:T(8,128)(2,1)}, u32[]{:S(2)}, u32[]{:S(2)}) collective-permute-start(bf16[256,1024]{1,0:T(8,128)(2,1)} %collective-permute-done.4.refs_0_), channel_id=1, source_target_pairs={{0,18},{1,19},{2,16},{3,17},{4,22},{5,23},{6,20},{7,21},{8,26},{9,... | collective-permute-start | bytes 1572872 | tf_op jit(solution)/shard_map/ppermute | solution.py:39
  42.6 6.5 %copy-start.8 = (s32[8,128]{1,0:T(8,128)S(1)}, s32[8,128]{1,0:T(8,128)}, u32[]{:S(2)}) copy-start(s32[8,128]{1,0:T(8,128)} %at_ref.1) | copy-start | bytes 12292
  48.3 4.4 %collective-permute-start.11 = (bf16[256,1024]{1,0:T(8,128)(2,1)}, bf16[256,1024]{1,0:T(8,128)(2,1)S(1)}, u32[]{:S(2)}, u32[]{:S(2)}) collective-permute-start(bf16[256,1024]{1,0:T(8,128)(2,1)} %collective-permute-done.10.refs_4_), channel_id=1, source_target_pairs={{0,1},{1,0},{2,3},{3,2},{4,5},{5,4},{6,7},{7,6},{8,9},{9,8},{10,11... | collective-permute-start | bytes 1572872 | tf_op jit(solution)/shard_map/ppermute | solution.py:39
  49.1 4.2 %copy-start.9 = (f32[1024,1024]{1,0:T(8,128)S(1)}, f32[1024,1024]{1,0:T(8,128)}, u32[]{:S(2)}) copy-start(f32[1024,1024]{1,0:T(8,128)} %hub_products.1.carry_ref) | copy-start | bytes 12582916
  52.7 5.3 %collective-permute-start.13 = (bf16[256,1024]{1,0:T(8,128)(2,1)}, bf16[256,1024]{1,0:T(8,128)(2,1)S(1)}, u32[]{:S(2)}, u32[]{:S(2)}) collective-permute-start(bf16[256,1024]{1,0:T(8,128)(2,1)} %collective-permute-done.8.refs_2_), channel_id=1, source_target_pairs={{0,1},{1,0},{2,3},{3,2},{4,5},{5,4},{6,7},{7,6},{8,9},{9,8},{10,11... | collective-permute-start | bytes 1572872 | tf_op jit(solution)/shard_map/ppermute | solution.py:39
  52.8 5.2 %collective-permute-start.14 = (bf16[256,1024]{1,0:T(8,128)(2,1)}, bf16[256,1024]{1,0:T(8,128)(2,1)S(1)}, u32[]{:S(2)}, u32[]{:S(2)}) collective-permute-start(bf16[256,1024]{1,0:T(8,128)(2,1)} %collective-permute-done.9.refs_3_), channel_id=1, source_target_pairs={{0,1},{1,0},{2,3},{3,2},{4,5},{5,4},{6,7},{7,6},{8,9},{9,8},{10,11... | collective-permute-start | bytes 1572872 | tf_op jit(solution)/shard_map/ppermute | solution.py:39
  53.3 4.7 %copy-start.1 = (f32[1024,1024]{1,0:T(8,128)S(1)}, f32[1024,1024]{1,0:T(8,128)}, u32[]{:S(2)}) copy-start(f32[1024,1024]{1,0:T(8,128)} %self_part.1.base_ref) | copy-start | bytes 12582916
  53.3 4.7 %copy-start.7 = (bf16[1024,1024]{1,0:T(8,128)(2,1)S(1)}, bf16[1024,1024]{1,0:T(8,128)(2,1)}, u32[]{:S(2)}) copy-start(bf16[1024,1024]{1,0:T(8,128)(2,1)} %weight_ref.3) | copy-start | bytes 6291460
  (2 other events, 6.4 us)
